TPU v7x, 128 devices: a whole 4x4x4 slice. The times are simulated.
128 devices in a mesh: row: 8 (over x_lo, y), col: 16 (over x_hi, z, core).
Axes of the slice: x: 4 (x_hi: 2, x_lo: 2; x = x_hi * 2 + x_lo), y: 4, z: 4, core: 2. Of those that a mesh axis runs over, the one named last changes fastest.
Arguments:
- sensitivity: bfloat16 [128, 8, 2, 256, 128], P(('row', 'col')), may hold values from -0.3984375 to 0.3984375
- tile_ids: int32 [128, 8, 2], P(('row', 'col')), may hold values from 0 to 15, as said below
- counts: int32 [128, 8], P(('row', 'col')), may hold values from 0 to 2, as said below
- weight_class: int32 [128, 256], P(('row', 'col')), may hold values from 0 to 3
Outputs:
- normal_matrix: float32 [16384, 16384], P('row', 'col')
Inputs may be any that keep to these rules, and one draw needn't show every extreme that they name: `tile_ids`: within one station block and one row owner the 2 slots name distinct tiles. `counts`: slots at or beyond the count are padding; in every draw some station block uses all 2 slots of every row owner.
All inputs are finite; a program needn't handle non-finite values.
Results may differ from a plain program's by a relative error of at most 0.0003.
Values may be sent and summed in bfloat16 or wider, within the bound.
A program may use at most 128 MiB of HBM per device.

v0:
```python
import jax
import jax.numpy as jnp
from jax import lax
from jax.sharding import PartitionSpec as P

TILES = 128


def station_scale(weight_class):
    levels = jnp.array([1.0, 0.5, 0.25, 0.125], jnp.float32)
    hits = weight_class[..., None] == jnp.arange(4, dtype=jnp.int32)
    return jnp.sum(jnp.where(hits, levels, jnp.float32(0.0)), axis=-1)


def local(sensitivity, tile_ids, counts, weight_class):
    row_devices = lax.axis_size("row")
    col_devices = lax.axis_size("col")
    blocks, _, slots, rows, width = sensitivity.shape
    per_row = TILES // row_devices
    per_col = TILES // col_devices
    ratio = col_devices // row_devices
    live = jnp.arange(slots, dtype=jnp.int32)[None, None, :] < counts[:, :, None]
    factor = station_scale(weight_class)[:, None, None, :, None] * live[:, :, :, None, None].astype(
        jnp.float32
    )
    weighted = (sensitivity.astype(jnp.float32) * factor).astype(jnp.bfloat16)
    left_ids = jnp.where(live, tile_ids, -1)
    owned_data, owned_ids = (
        lax.all_to_all(weighted, "row", split_axis=1, concat_axis=0, tiled=True),
        lax.all_to_all(left_ids, "row", split_axis=1, concat_axis=0, tiled=True),
    )
    left_data, left_tiles = (
        lax.all_gather(owned_data, "col", axis=1, tiled=True),
        lax.all_gather(owned_ids, "col", axis=1, tiled=True),
    )
    stations = row_devices * col_devices * blocks
    left_data = left_data.reshape(stations, slots, rows, width)
    left_tiles = left_tiles.reshape(stations, slots)
    picked = jnp.repeat(weighted, ratio, axis=1)
    picked_ids = jnp.repeat(left_ids, ratio, axis=1)
    offsets = (jnp.arange(col_devices, dtype=jnp.int32) % ratio * per_col)[None, :, None]
    inside = (picked_ids >= offsets) & (picked_ids < offsets + per_col)
    chosen_ids = jnp.where(inside, picked_ids - offsets, -1)
    sorted_data, sorted_ids = (
        lax.all_to_all(picked, "col", split_axis=1, concat_axis=0, tiled=True),
        lax.all_to_all(chosen_ids, "col", split_axis=1, concat_axis=0, tiled=True),
    )
    right_data, right_tiles = (
        lax.all_gather(sorted_data, "row", axis=0, tiled=True),
        lax.all_gather(sorted_ids, "row", axis=0, tiled=True),
    )
    right_data = right_data.reshape(stations, slots, rows, width)
    right_tiles = right_tiles.reshape(stations, slots)
    group = min(stations, 32)

    def accumulate(index, normal):
        start = index * group
        left_part = lax.dynamic_slice_in_dim(left_data, start, group, 0)
        left_part_ids = lax.dynamic_slice_in_dim(left_tiles, start, group, 0)
        right_part = lax.dynamic_slice_in_dim(right_data, start, group, 0)
        right_part_ids = lax.dynamic_slice_in_dim(right_tiles, start, group, 0)
        gram = jnp.einsum(
            "girk,gjrn->gijkn", left_part, right_part, preferred_element_type=jnp.float32
        )
        left_place = jnp.where(left_part_ids >= 0, left_part_ids, per_row)
        right_place = jnp.where(right_part_ids >= 0, right_part_ids, per_col)
        return normal.at[left_place[:, :, None], :, right_place[:, None, :], :].add(
            gram, mode="drop"
        )

    normal = jnp.zeros((per_row, width, per_col, width), jnp.float32)
    normal = lax.fori_loop(0, stations // group, accumulate, normal)
    return normal.reshape(per_row * width, per_col * width)


def solution(mesh):
    in_specs = (
        P(("row", "col"), None, None, None, None),
        P(("row", "col"), None, None),
        P(("row", "col"), None),
        P(("row", "col"), None),
    )
    out_specs = P("row", "col")
    return jax.shard_map(local, mesh=mesh, in_specs=in_specs, out_specs=out_specs, check_vma=False)
```

profile of v0, /device:TPU:1, one launch (start us, length us, event | category | flops | bytes accessed | tf_op | source)
XLA Modules:
  0.0 544.6 jit_solution(8788862461360481018)
XLA Ops:
  6.5 0.0 all-gather.7.cloned.1.call-start
  6.5 0.7 fusion.11
  7.3 0.8 select_reduce_fusion
  8.0 0.1 broadcast_multiply_fusion
  8.1 1.7 fusion.13
  9.9 0.0 copy-start
  9.9 0.5 copy.33
  10.4 0.2 broadcast_in_dim.90
  10.7 0.0 copy-start.2
  10.7 0.0 copy-start.1
  10.7 37.2 %all_to_all.48 = bf16[1,16,2,256,128]{3,4,2,0,1:T(8,128)(2,1)S(1)} all-to-all(bf16[1,16,2,256,128]{3,4,2,0,1:T(8,128)(2,1)S(1)} %bitcast.52), channel_id=1, replica_groups=mesh['row'=8,'col'=16] {'col'}, dimensions={1} | all-to-all | bytes 4194304 | tf_op jit(solution)/shard_map/all_to_all | solution.py:45
  47.9 2.4 copy.34
  50.3 0.0 all-gather.7.cloned.1.call-update
  50.3 0.0 all-gather.9.cloned.1.call-start
  50.3 0.0 copy-done
  50.4 0.7 multiply_convert_fusion
  51.1 27.1 %all_to_all.49 = bf16[1,8,2,256,128]{4,3,2,0,1:T(8,128)(2,1)} all-to-all(bf16[1,8,2,256,128]{4,3,2,0,1:T(8,128)(2,1)S(1)} %multiply_convert_fusion), channel_id=1, replica_groups=mesh['row'=8,'col'=16] {'row'}, dimensions={1} | all-to-all | bytes 2097152 | tf_op jit(solution)/shard_map/all_to_all | solution.py:29
  78.2 0.0 all-gather.9.cloned.1.call-update
  78.2 0.0 copy-done.2
  78.2 0.1 copy.27
  78.3 0.0 copy-done.1
  78.3 0.7 compare_select_fusion.4
  79.0 3.4 all-to-all-start
  82.4 0.8 copy.30
  83.2 0.1 broadcast_in_dim.85
  83.2 0.1 broadcast_in_dim.86
  83.3 0.7 copy.31
  84.0 3.3 all-to-all-done
  87.3 8.4 %all-to-all-start.1 = ((s32[1,16,2]{2,0,1:T(1,128)}), s32[1,16,2]{2,0,1:T(1,128)S(1)}, u32[]{:S(2)}, u32[]{:S(2)}) async-start(s32[1,16,2]{2,0,1:T(1,128)} %copy.31), calls=%async_computation.1 | async-start | bytes 16384 | tf_op jit(solution)/shard_map/all_to_all | solution.py:46
  95.8 0.1 copy.28
  95.8 24.5 %all-gather = s32[1,8,32]{1,0,2:T(1,128)S(1)} all-gather(s32[1,8,2]{1,0,2:T(1,128)S(1)} %copy.28), channel_id=2, replica_groups=mesh['row'=8,'col'=16] {'col'}, dimensions={2}, use_global_device_ids=true | all-gather | bytes 1088 | tf_op jit(solution)/shard_map/all_gather | solution.py:34
  120.3 0.1 copy.29
  120.4 0.1 reshape.312
  120.5 0.0 all-to-all-done.1
  120.5 24.5 %all-gather.1 = s32[1,128,2]{2,0,1:T(1,128)S(1)} all-gather(s32[1,16,2]{2,0,1:T(1,128)S(1)} %all-to-all-done.1), channel_id=3, replica_groups=mesh['row'=8,'col'=16] {'row'}, dimensions={1}, use_global_device_ids=true | all-gather | bytes 1152 | tf_op jit(solution)/shard_map/all_gather | solution.py:50
  145.0 85.1 %all-gather.7.cloned.1.call-done = bf16[1,128,2,256,128]{4,3,2,0,1:T(8,128)(2,1)} async-done(((bf16[1,16,2,256,128]{4,3,2,0,1:T(8,128)(2,1)}), bf16[1,128,2,256,128]{4,3,2,0,1:T(8,128)(2,1)}) %all-gather.7.cloned.1.call-update) | async-done | bytes 16777232 | tf_op jit(solution)/shard_map/all_gather | solution.py:49
  230.1 108.0 %all-gather.9.cloned.1.call-done = bf16[1,8,32,256,128]{4,3,2,0,1:T(8,128)(2,1)} async-done(((bf16[1,8,2,256,128]{4,3,2,0,1:T(8,128)(2,1)}), bf16[1,8,32,256,128]{4,3,2,0,1:T(8,128)(2,1)}) %all-gather.9.cloned.1.call-update) | async-done | bytes 16777232 | tf_op jit(solution)/shard_map/all_gather | solution.py:33
  338.1 4.5 broadcast_in_dim.83
  342.6 179.8 %while.13 = (s32[]{:T(128)}, f32[16,128,8,128]{3,1,2,0:T(8,128)}, s32[128,2]{1,0:T(8,128)S(1)}, s32[128,2]{1,0:T(8,128)S(1)}, bf16[128,2,256,128]{3,2,1,0:T(8,12...) while((s32[]{:T(128)}, f32[16,128,8,128]{3,1,2,0:T(8,128)}, ...), condition=%wide.region_3.4_spmd, body=%wide.region_1.3_spmd.sunk | while | flops 1075841152 | bytes 58726296 | solution.py:72
  342.6 0.1 or_select_fusion.2
  342.8 0.1 reshape.338
  342.9 8.0 %fusion.19 = f32[32,2,2,128,128]{3,4,1,2,0:T(8,128)} fusion(bf16[128,2,256,128]{3,2,1,0:T(8,128)(2,1)} %get-tuple-element.227, s32[]{:T(128)S(6)} %select_n.135, bf16[128,2,256,128]{3,2,1,0:T(8,128)(2,1)} %get-tuple-element.226), kind=kOutput, calls=%fused_computation.6.clone.1 | convolution fusion | flops 1073741824 | bytes 16778240 | tf_op jit(solution)/shard_map/while/body/eval_jaxpr/girk,gjrn->gijkn/dot_general | solution.py:62
  350.9 8.9 %copy.44 = f32[32,2,2,128,128]{4,3,2,1,0:T(8,128)} copy(f32[32,2,2,128,128]{3,4,1,2,0:T(8,128)} %fusion.19) | data formatting | bytes 16777216 | tf_op jit(solution)/shard_map/while/body/eval_jaxpr/girk,gjrn->gijkn/transpose | solution.py:62
  359.8 27.2 %scatter_fusion = f32[16,128,8,128]{3,1,2,0:T(8,128)} fusion(f32[16,128,8,128]{3,1,2,0:T(8,128)} %get-tuple-element.213, s32[128]{0:T(128)S(1)} %reshape.338, f32[128,128,128]{2,1,0:T(8,128)} %bitcast.48), kind=kCustom, calls=%fused_computation.clone.1 | custom fusion | flops 2097152 | bytes 25166848 | tf_op jit(solution)/shard_map/while/body/eval_jaxpr/scatter-add | solution.py:67
  387.1 0.1 or_select_fusion.2
  387.2 0.1 reshape.338
  387.4 8.0 %fusion.19 = f32[32,2,2,128,128]{3,4,1,2,0:T(8,128)} fusion(bf16[128,2,256,128]{3,2,1,0:T(8,128)(2,1)} %get-tuple-element.227, s32[]{:T(128)S(6)} %select_n.135, bf16[128,2,256,128]{3,2,1,0:T(8,128)(2,1)} %get-tuple-element.226), kind=kOutput, calls=%fused_computation.6.clone.1 | convolution fusion | flops 1073741824 | bytes 16778240 | tf_op jit(solution)/shard_map/while/body/eval_jaxpr/girk,gjrn->gijkn/dot_general | solution.py:62
  395.3 8.9 %copy.44 = f32[32,2,2,128,128]{4,3,2,1,0:T(8,128)} copy(f32[32,2,2,128,128]{3,4,1,2,0:T(8,128)} %fusion.19) | data formatting | bytes 16777216 | tf_op jit(solution)/shard_map/while/body/eval_jaxpr/girk,gjrn->gijkn/transpose | solution.py:62
  404.3 28.0 %scatter_fusion = f32[16,128,8,128]{3,1,2,0:T(8,128)} fusion(f32[16,128,8,128]{3,1,2,0:T(8,128)} %get-tuple-element.213, s32[128]{0:T(128)S(1)} %reshape.338, f32[128,128,128]{2,1,0:T(8,128)} %bitcast.48), kind=kCustom, calls=%fused_computation.clone.1 | custom fusion | flops 2097152 | bytes 25166848 | tf_op jit(solution)/shard_map/while/body/eval_jaxpr/scatter-add | solution.py:67
  432.3 0.1 or_select_fusion.2
  432.5 0.1 reshape.338
  432.6 8.0 %fusion.19 = f32[32,2,2,128,128]{3,4,1,2,0:T(8,128)} fusion(bf16[128,2,256,128]{3,2,1,0:T(8,128)(2,1)} %get-tuple-element.227, s32[]{:T(128)S(6)} %select_n.135, bf16[128,2,256,128]{3,2,1,0:T(8,128)(2,1)} %get-tuple-element.226), kind=kOutput, calls=%fused_computation.6.clone.1 | convolution fusion | flops 1073741824 | bytes 16778240 | tf_op jit(solution)/shard_map/while/body/eval_jaxpr/girk,gjrn->gijkn/dot_general | solution.py:62
  440.6 8.9 %copy.44 = f32[32,2,2,128,128]{4,3,2,1,0:T(8,128)} copy(f32[32,2,2,128,128]{3,4,1,2,0:T(8,128)} %fusion.19) | data formatting | bytes 16777216 | tf_op jit(solution)/shard_map/while/body/eval_jaxpr/girk,gjrn->gijkn/transpose | solution.py:62
  449.6 27.3 %scatter_fusion = f32[16,128,8,128]{3,1,2,0:T(8,128)} fusion(f32[16,128,8,128]{3,1,2,0:T(8,128)} %get-tuple-element.213, s32[128]{0:T(128)S(1)} %reshape.338, f32[128,128,128]{2,1,0:T(8,128)} %bitcast.48), kind=kCustom, calls=%fused_computation.clone.1 | custom fusion | flops 2097152 | bytes 25166848 | tf_op jit(solution)/shard_map/while/body/eval_jaxpr/scatter-add | solution.py:67
  476.9 0.1 or_select_fusion.2
  477.1 0.1 reshape.338
  477.2 8.0 %fusion.19 = f32[32,2,2,128,128]{3,4,1,2,0:T(8,128)} fusion(bf16[128,2,256,128]{3,2,1,0:T(8,128)(2,1)} %get-tuple-element.227, s32[]{:T(128)S(6)} %select_n.135, bf16[128,2,256,128]{3,2,1,0:T(8,128)(2,1)} %get-tuple-element.226), kind=kOutput, calls=%fused_computation.6.clone.1 | convolution fusion | flops 1073741824 | bytes 16778240 | tf_op jit(solution)/shard_map/while/body/eval_jaxpr/girk,gjrn->gijkn/dot_general | solution.py:62
  485.2 8.9 %copy.44 = f32[32,2,2,128,128]{4,3,2,1,0:T(8,128)} copy(f32[32,2,2,128,128]{3,4,1,2,0:T(8,128)} %fusion.19) | data formatting | bytes 16777216 | tf_op jit(solution)/shard_map/while/body/eval_jaxpr/girk,gjrn->gijkn/transpose | solution.py:62
  494.1 28.2 %scatter_fusion = f32[16,128,8,128]{3,1,2,0:T(8,128)} fusion(f32[16,128,8,128]{3,1,2,0:T(8,128)} %get-tuple-element.213, s32[128]{0:T(128)S(1)} %reshape.338, f32[128,128,128]{2,1,0:T(8,128)} %bitcast.48), kind=kCustom, calls=%fused_computation.clone.1 | custom fusion | flops 2097152 | bytes 25166848 | tf_op jit(solution)/shard_map/while/body/eval_jaxpr/scatter-add | solution.py:67
  522.3 9.9 %copy.36 = f32[16,128,8,128]{3,2,1,0:T(8,128)S(1)} copy(f32[16,128,8,128]{3,1,2,0:T(8,128)} %get-tuple-element.114) | data formatting | bytes 16777216 | tf_op jit(solution)/shard_map/while | solution.py:72
  532.2 5.5 %copy.42 = f32[256,8,8,128]{3,1,2,0:T(8,128)} copy(f32[256,8,8,128]{3,2,1,0:T(8,128)S(1)} %bitcast.49) | data formatting | bytes 16777216
  (10 shorter events, 0.2 us)
Async XLA Ops:
  6.5 223.6 %all-gather.7.cloned.1.call-start = ((), (), s32[]{:S(2)}) async-start(), calls=%async_computation.4 | async-start | bytes 18874368 | tf_op jit(solution)/shard_map/all_gather | solution.py:49
  9.9 40.5 %copy-start = (bf16[1,8,2,256,128]{4,3,2,1,0:T(8,128)(2,1)S(1)}, bf16[1,8,2,256,128]{4,3,2,1,0:T(8,128)(2,1)}, u32[]{:S(2)}) copy-start(bf16[1,8,2,256,128]{4,3,2,1,0:T(8,128)(2,1)} %param.7) | copy-start | bytes 3145732
  10.7 67.5 %copy-start.2 = (s32[1,8,2]{1,2,0:T(2,128)S(1)}, s32[1,8,2]{1,2,0:T(2,128)}, u32[]{:S(2)}) copy-start(s32[1,8,2]{1,2,0:T(2,128)} %param.8) | copy-start | bytes 196
  10.7 67.6 %copy-start.1 = (s32[1,8]{1,0:T(1,128)S(1)}, s32[1,8]{1,0:T(1,128)}, u32[]{:S(2)}) copy-start(s32[1,8]{1,0:T(1,128)} %param.9) | copy-start | bytes 100
  50.3 287.8 %all-gather.9.cloned.1.call-start = ((), (), s32[]{:S(2)}) async-start(), calls=%async_computation.5 | async-start | bytes 17825792 | tf_op jit(solution)/shard_map/all_gather | solution.py:33
  79.0 8.4 %all-to-all-start = ((s32[1,8,2]{2,0,1:T(1,128)}), s32[1,8,2]{2,0,1:T(1,128)S(1)}, u32[]{:S(2)}, u32[]{:S(2)}) async-start(s32[1,8,2]{2,0,1:T(1,128)} %compare_select_fusion.4), calls=%async_computation | async-start | bytes 8192 | tf_op jit(solution)/shard_map/all_to_all | solution.py:30
  87.3 33.1 %all-to-all-start.1 = ((s32[1,16,2]{2,0,1:T(1,128)}), s32[1,16,2]{2,0,1:T(1,128)S(1)}, u32[]{:S(2)}, u32[]{:S(2)}) async-start(s32[1,16,2]{2,0,1:T(1,128)} %copy.31), calls=%async_computation.1 | async-start | bytes 16384 | tf_op jit(solution)/shard_map/all_to_all | solution.py:46
Sparse Core Ops, SparseCore 0:
  50.4 179.6 all-gather.6
  232.6 105.4 all-gather.8
where the time goes:
time: 547 us; the launch traced here: 545 us
  waiting for transfers between devices  196 us (36%)
  other arithmetic  116 us (21%)
  blocking collectives  113 us (21%)
  local copies, waits for them, and re-layouts  61.3 us (11%)
  matrix products  32 us (6%)
  between operations  13.5 us (2%)
  starting transfers between devices  11.9 us (2%)
    scatter-add x4, other arithmetic, accumulate(): normal.at[left_place[:, :, None], :, right_place[:, None, :], :]  111 us
    all_gather x1, waiting for transfers between devices, local(): lax.all_gather(owned_data, 'col', axis=1, tiled=True)  108 us
    all_gather x1, waiting for transfers between devices, local(): lax.all_gather(sorted_data, 'row', axis=0, tiled=True)  85.1 us
    all_to_all x1, blocking collectives, local(): lax.all_to_all(picked, 'col', split_axis=1, concat_axis=0, tiled=True)  37.2 us
    transpose x4, local copies, waits for them, and re-layouts, accumulate(): jnp.einsum('girk,gjrn->gijkn', left_part, right_part, preferred_element_t...  35.8 us
    dot_general x4, matrix products, accumulate(): jnp.einsum('girk,gjrn->gijkn', left_part, right_part, preferred_element_t...  32 us
    all_to_all x1, blocking collectives, local(): lax.all_to_all(weighted, 'row', split_axis=1, concat_axis=0, tiled=True)  27.1 us
    all_gather x1, blocking collectives, local(): lax.all_gather(sorted_ids, 'row', axis=0, tiled=True)  24.5 us
  transfers between devices with their start and end apart: 4, of which 3 were waited for; matrix products, arithmetic and copies ran while one was open for 1% of the time, Pallas kernels for 0%

commit v1 on v0

--- a/solution.py
+++ b/solution.py
@@ -1,15 +1,79 @@
+import functools
+
 import jax
 import jax.numpy as jnp
 from jax import lax
+from jax.experimental import pallas as pl
+from jax.experimental.pallas import tpu as pltpu
 from jax.sharding import PartitionSpec as P
 
 TILES = 128
+GROUP = 8
 
 
 def station_scale(weight_class):
     levels = jnp.array([1.0, 0.5, 0.25, 0.125], jnp.float32)
     hits = weight_class[..., None] == jnp.arange(4, dtype=jnp.int32)
     return jnp.sum(jnp.where(hits, levels, jnp.float32(0.0)), axis=-1)
+
+
+def gram_kernel(slots, width, lids_ref, rids_ref, left_ref, right_ref, out_ref):
+    g = pl.program_id(0)
+
+    @pl.when(g == 0)
+    def _():
+        out_ref[...] = jnp.zeros_like(out_ref)
+
+    def body(k, carry):
+        b = g * GROUP + k
+        for i in range(slots):
+            li = lids_ref[b * slots + i]
+            for j in range(slots):
+                rj = rids_ref[b * slots + j]
+
+                @pl.when((li >= 0) & (rj >= 0))
+                def _():
+                    prod = lax.dot_general(
+                        left_ref[k, i],
+                        right_ref[k, j],
+                        (((0,), (0,)), ((), ())),
+                        preferred_element_type=jnp.float32,
+                    )
+                    rows = pl.ds(pl.multiple_of(li * width, width), width)
+                    cols = pl.ds(pl.multiple_of(rj * width, width), width)
+                    out_ref[rows, cols] += prod
+
+        return carry
+
+    lax.fori_loop(0, GROUP, body, 0)
+
+
+def accumulate(left_data, left_ids, right_data, right_ids, per_row, per_col):
+    stations, slots, rows, width = left_data.shape
+    block = (GROUP, slots, rows, width)
+    grid_spec = pltpu.PrefetchScalarGridSpec(
+        num_scalar_prefetch=2,
+        grid=(stations // GROUP,),
+        in_specs=[
+            pl.BlockSpec(block, lambda g, lids, rids: (g, 0, 0, 0)),
+            pl.BlockSpec(block, lambda g, lids, rids: (g, 0, 0, 0)),
+        ],
+        out_specs=pl.BlockSpec((per_row * width, per_col * width), lambda g, lids, rids: (0, 0)),
+    )
+    flops = 2 * stations * slots * slots * rows * width * width
+    return pl.pallas_call(
+        functools.partial(gram_kernel, slots, width),
+        grid_spec=grid_spec,
+        out_shape=jax.ShapeDtypeStruct((per_row * width, per_col * width), jnp.float32),
+        compiler_params=pltpu.CompilerParams(
+            dimension_semantics=("arbitrary",), vmem_limit_bytes=48 * 1024 * 1024
+        ),
+        cost_estimate=pl.CostEstimate(
+            flops=flops,
+            bytes_accessed=2 * left_data.size * 2 + per_row * per_col * width * width * 4,
+            transcendentals=0,
+        ),
+    )(left_ids.reshape(-1), right_ids.reshape(-1), left_data, right_data)
 
 
 def local(sensitivity, tile_ids, counts, weight_class):
@@ -51,26 +115,7 @@
     )
     right_data = right_data.reshape(stations, slots, rows, width)
     right_tiles = right_tiles.reshape(stations, slots)
-    group = min(stations, 32)
-
-    def accumulate(index, normal):
-        start = index * group
-        left_part = lax.dynamic_slice_in_dim(left_data, start, group, 0)
-        left_part_ids = lax.dynamic_slice_in_dim(left_tiles, start, group, 0)
-        right_part = lax.dynamic_slice_in_dim(right_data, start, group, 0)
-        right_part_ids = lax.dynamic_slice_in_dim(right_tiles, start, group, 0)
-        gram = jnp.einsum(
-            "girk,gjrn->gijkn", left_part, right_part, preferred_element_type=jnp.float32
-        )
-        left_place = jnp.where(left_part_ids >= 0, left_part_ids, per_row)
-        right_place = jnp.where(right_part_ids >= 0, right_part_ids, per_col)
-        return normal.at[left_place[:, :, None], :, right_place[:, None, :], :].add(
-            gram, mode="drop"
-        )
-
-    normal = jnp.zeros((per_row, width, per_col, width), jnp.float32)
-    normal = lax.fori_loop(0, stations // group, accumulate, normal)
-    return normal.reshape(per_row * width, per_col * width)
+    return accumulate(left_data, left_tiles, right_data, right_tiles, per_row, per_col)
 
 
 def solution(mesh):

time: 547 us -> 380 us (0.69)
  other arithmetic: 116 us -> 5.5 us
  local copies, waits for them, and re-layouts: 61.3 us -> 4.35 us
  Pallas kernels: 0 us -> 32.3 us
  matrix products: 32 us -> 0 us
    scatter-add x4 -> x0, other arithmetic: 111 us -> none  [accumulate(): normal.at[left_place[:, :, None], :, right_place[:, None, :], :]]
    transpose x4 -> x0, local copies, waits for them, and re-layouts: 35.8 us -> none  [accumulate(): jnp.einsum('girk,gjrn->gijkn', left_part, right_part, preferred_element_t...]
    pallas_call x0 -> x1, Pallas kernels: none -> 32.3 us  [accumulate(): pl.pallas_call(functools.partial(gram_kernel, slots, width), grid_spec=gr...]
    dot_general x4 -> x0, matrix products: 32 us -> none  [accumulate(): jnp.einsum('girk,gjrn->gijkn', left_part, right_part, preferred_element_t...]
    while x1 -> x0, local copies, waits for them, and re-layouts: 9.92 us -> none  [local(): normal = lax.fori_loop(0, stations // group, accumulate, normal)]
where the time goes in v1:
time: 380 us; the launch traced here: 376 us
  waiting for transfers between devices  194 us (51%)
  blocking collectives  116 us (31%)
  Pallas kernels  32.3 us (8%)
  between operations  13.5 us (4%)
  starting transfers between devices  10.4 us (3%)
  other arithmetic  5.5 us (1%)
  local copies, waits for them, and re-layouts  4.35 us (1%)
    all_gather x1, waiting for transfers between devices, local(): lax.all_gather(owned_data, 'col', axis=1, tiled=True)  108 us
    all_gather x1, waiting for transfers between devices, local(): lax.all_gather(sorted_data, 'row', axis=0, tiled=True)  82.5 us
    all_to_all x1, blocking collectives, local(): lax.all_to_all(picked, 'col', split_axis=1, concat_axis=0, tiled=True)  37.3 us
    pallas_call x1, Pallas kernels, accumulate(): pl.pallas_call(functools.partial(gram_kernel, slots, width), grid_spec=gr...  32.3 us
    all_to_all x1, blocking collectives, local(): lax.all_to_all(weighted, 'row', split_axis=1, concat_axis=0, tiled=True)  29.4 us
    all_gather x1, blocking collectives, local(): lax.all_gather(sorted_ids, 'row', axis=0, tiled=True)  24.5 us
    all_gather x1, blocking collectives, local(): lax.all_gather(owned_ids, 'col', axis=1, tiled=True)  24.5 us
  transfers between devices with their start and end apart: 4, of which 3 were waited for; matrix products, arithmetic and copies ran while one was open for 1% of the time, Pallas kernels for 0%

profile of v1, /device:TPU:1, one launch (start us, length us, event | category | flops | bytes accessed | tf_op | source)
XLA Modules:
  0.0 376.1 jit_solution(11550586290590239082)
XLA Ops:
  6.5 0.0 all-gather.9.cloned.1.call-start
  6.5 0.7 fusion
  7.3 0.8 select_reduce_fusion
  8.0 0.1 broadcast_multiply_fusion
  8.1 1.7 fusion.2
  9.9 0.6 broadcast_in_dim.39
  10.5 37.3 %all_to_all.48 = bf16[1,16,2,256,128]{4,3,2,0,1:T(8,128)(2,1)} all-to-all(bf16[1,16,2,256,128]{4,3,2,0,1:T(8,128)(2,1)S(1)} %bitcast.17), channel_id=1, replica_groups=mesh['row'=8,'col'=16] {'col'}, dimensions={1} | all-to-all | bytes 4194304 | tf_op jit(solution)/shard_map/all_to_all | solution.py:109
  47.8 0.0 copy-start
  47.8 0.0 all-gather.9.cloned.1.call-update
  47.8 0.0 all-gather.7.cloned.1.call-start
  47.9 1.1 copy-done
  49.0 0.7 multiply_convert_fusion
  49.7 0.0 copy-start.2
  49.7 0.0 copy-start.1
  49.8 29.4 %all_to_all.49 = bf16[1,8,2,256,128]{4,3,2,0,1:T(8,128)(2,1)} all-to-all(bf16[1,8,2,256,128]{4,3,2,0,1:T(8,128)(2,1)S(1)} %multiply_convert_fusion), channel_id=1, replica_groups=mesh['row'=8,'col'=16] {'row'}, dimensions={1} | all-to-all | bytes 2097152 | tf_op jit(solution)/shard_map/all_to_all | solution.py:93
  79.2 0.0 all-gather.7.cloned.1.call-update
  79.2 0.0 copy-done.2
  79.2 0.1 copy.14
  79.3 0.0 copy-done.1
  79.3 0.7 compare_select_fusion
  80.0 3.5 all-to-all-start
  83.5 0.8 copy.17
  84.3 0.1 broadcast_in_dim.34
  84.4 0.1 broadcast_in_dim.35
  84.5 0.7 copy.18
  85.1 3.3 all-to-all-done
  88.5 6.9 %all-to-all-start.1 = ((s32[1,16,2]{2,0,1:T(1,128)}), s32[1,16,2]{2,0,1:T(1,128)S(1)}, u32[]{:S(2)}, u32[]{:S(2)}) async-start(s32[1,16,2]{2,0,1:T(1,128)} %copy.18), calls=%async_computation.1 | async-start | bytes 16384 | tf_op jit(solution)/shard_map/all_to_all | solution.py:110
  95.3 0.1 copy.15
  95.4 24.5 %all-gather = s32[1,8,32]{1,0,2:T(1,128)S(1)} all-gather(s32[1,8,2]{1,0,2:T(1,128)S(1)} %copy.15), channel_id=2, replica_groups=mesh['row'=8,'col'=16] {'col'}, dimensions={2}, use_global_device_ids=true | all-gather | bytes 1088 | tf_op jit(solution)/shard_map/all_gather | solution.py:98
  119.9 0.1 copy.16
  119.9 0.1 reshape_reshape.6.lids_ref
  120.0 0.0 all-to-all-done.1
  120.0 24.5 %all-gather.1 = s32[1,128,2]{2,0,1:T(1,128)S(1)} all-gather(s32[1,16,2]{2,0,1:T(1,128)S(1)} %all-to-all-done.1), channel_id=3, replica_groups=mesh['row'=8,'col'=16] {'row'}, dimensions={1}, use_global_device_ids=true | all-gather | bytes 1152 | tf_op jit(solution)/shard_map/all_gather | solution.py:114
  144.5 0.5 broadcast.233
  145.1 0.8 reduce.4
  145.9 0.1 reshape_reshape.7.rids_ref
  146.0 82.5 %all-gather.9.cloned.1.call-done = bf16[1,128,2,256,128]{4,3,2,0,1:T(8,128)(2,1)} async-done(((bf16[1,16,2,256,128]{4,3,2,0,1:T(8,128)(2,1)}), bf16[1,128,2,256,128]{4,3,2,0,1:T(8,128)(2,1)}) %all-gather.9.cloned.1.call-update) | async-done | bytes 16777232 | tf_op jit(solution)/shard_map/all_gather | solution.py:113
  228.5 108.4 %all-gather.7.cloned.1.call-done = bf16[1,8,32,256,128]{4,3,2,0,1:T(8,128)(2,1)} async-done(((bf16[1,8,2,256,128]{4,3,2,0,1:T(8,128)(2,1)}), bf16[1,8,32,256,128]{4,3,2,0,1:T(8,128)(2,1)}) %all-gather.7.cloned.1.call-update) | async-done | bytes 16777232 | tf_op jit(solution)/shard_map/all_gather | solution.py:97
  337.0 32.3 %shard_map.61 = f32[2048,1024]{1,0:T(8,128)} custom-call(s32[256]{0:T(256)S(1)} %reshape_reshape.6.lids_ref, s32[256]{0:T(256)S(1)} %reshape_reshape.7.rids_ref, bf16[128,2,256,128]{3,2,1,0:T(8,128)(2,1)} %bitcast.16, bf16[128,2,256,128]{3,2,1,0:T(8,128)(2,1)} %bitcast.15), custom_call_target="tpu_custom_call" | custom-call | flops 4294967296 | bytes 41943040 | tf_op jit(solution)/shard_map/pallas_call | solution.py:64
  (2 shorter events, 0.0 us)
Async XLA Ops:
  6.5 222.0 %all-gather.9.cloned.1.call-start = ((), (), s32[]{:S(2)}) async-start(), calls=%async_computation.5 | async-start | bytes 18874368 | tf_op jit(solution)/shard_map/all_gather | solution.py:113
  47.8 1.2 copy-start
  47.8 289.2 %all-gather.7.cloned.1.call-start = ((), (), s32[]{:S(2)}) async-start(), calls=%async_computation.4 | async-start | bytes 17825792 | tf_op jit(solution)/shard_map/all_gather | solution.py:97
  49.7 29.5 %copy-start.2 = (s32[1,8,2]{1,2,0:T(2,128)S(1)}, s32[1,8,2]{1,2,0:T(2,128)}, u32[]{:S(2)}) copy-start(s32[1,8,2]{1,2,0:T(2,128)} %param.6) | copy-start | bytes 196
  49.7 29.5 %copy-start.1 = (s32[1,8]{1,0:T(1,128)S(1)}, s32[1,8]{1,0:T(1,128)}, u32[]{:S(2)}) copy-start(s32[1,8]{1,0:T(1,128)} %param.7) | copy-start | bytes 100
  80.0 8.5 %all-to-all-start = ((s32[1,8,2]{2,0,1:T(1,128)}), s32[1,8,2]{2,0,1:T(1,128)S(1)}, u32[]{:S(2)}, u32[]{:S(2)}) async-start(s32[1,8,2]{2,0,1:T(1,128)} %compare_select_fusion), calls=%async_computation | async-start | bytes 8192 | tf_op jit(solution)/shard_map/all_to_all | solution.py:94
  88.5 31.6 %all-to-all-start.1 = ((s32[1,16,2]{2,0,1:T(1,128)}), s32[1,16,2]{2,0,1:T(1,128)S(1)}, u32[]{:S(2)}, u32[]{:S(2)}) async-start(s32[1,16,2]{2,0,1:T(1,128)} %copy.18), calls=%async_computation.1 | async-start | bytes 16384 | tf_op jit(solution)/shard_map/all_to_all | solution.py:110
Sparse Core Ops, SparseCore 0:
  48.0 180.5 all-gather.8
  231.1 105.8 all-gather.6

commit v2 on v1

--- a/solution.py
+++ b/solution.py
@@ -78,52 +78,56 @@
 
 def local(sensitivity, tile_ids, counts, weight_class):
     row_devices = lax.axis_size("row")
-    col_devices = lax.axis_size("col")
+    chips = lax.axis_size("chip")
+    cores = lax.axis_size("core")
+    me_row = lax.axis_index("row")
+    me_chip = lax.axis_index("chip")
+    me_core = lax.axis_index("core")
     blocks, _, slots, rows, width = sensitivity.shape
     per_row = TILES // row_devices
-    per_col = TILES // col_devices
-    ratio = col_devices // row_devices
+    per_col = per_row // cores
     live = jnp.arange(slots, dtype=jnp.int32)[None, None, :] < counts[:, :, None]
     factor = station_scale(weight_class)[:, None, None, :, None] * live[:, :, :, None, None].astype(
         jnp.float32
     )
     weighted = (sensitivity.astype(jnp.float32) * factor).astype(jnp.bfloat16)
-    left_ids = jnp.where(live, tile_ids, -1)
-    owned_data, owned_ids = (
-        lax.all_to_all(weighted, "row", split_axis=1, concat_axis=0, tiled=True),
-        lax.all_to_all(left_ids, "row", split_axis=1, concat_axis=0, tiled=True),
-    )
-    left_data, left_tiles = (
-        lax.all_gather(owned_data, "col", axis=1, tiled=True),
-        lax.all_gather(owned_ids, "col", axis=1, tiled=True),
-    )
-    stations = row_devices * col_devices * blocks
-    left_data = left_data.reshape(stations, slots, rows, width)
-    left_tiles = left_tiles.reshape(stations, slots)
-    picked = jnp.repeat(weighted, ratio, axis=1)
-    picked_ids = jnp.repeat(left_ids, ratio, axis=1)
-    offsets = (jnp.arange(col_devices, dtype=jnp.int32) % ratio * per_col)[None, :, None]
-    inside = (picked_ids >= offsets) & (picked_ids < offsets + per_col)
-    chosen_ids = jnp.where(inside, picked_ids - offsets, -1)
-    sorted_data, sorted_ids = (
-        lax.all_to_all(picked, "col", split_axis=1, concat_axis=0, tiled=True),
-        lax.all_to_all(chosen_ids, "col", split_axis=1, concat_axis=0, tiled=True),
-    )
-    right_data, right_tiles = (
-        lax.all_gather(sorted_data, "row", axis=0, tiled=True),
-        lax.all_gather(sorted_ids, "row", axis=0, tiled=True),
-    )
-    right_data = right_data.reshape(stations, slots, rows, width)
-    right_tiles = right_tiles.reshape(stations, slots)
-    return accumulate(left_data, left_tiles, right_data, right_tiles, per_row, per_col)
+    live_ids = jnp.where(live, tile_ids, -1)
+    all_ids = lax.all_gather(live_ids, ("row", "chip", "core"), axis=0, tiled=True)
+
+    left = lax.all_to_all(weighted, "row", split_axis=1, concat_axis=0, tiled=True)
+    left = lax.all_gather(left, "chip", axis=1, tiled=True)
+    left = lax.all_gather(left, "core", axis=0, tiled=False)
+    right = lax.all_to_all(weighted, "chip", split_axis=1, concat_axis=1, tiled=True)
+    right = lax.all_gather(right, "row", axis=0, tiled=True)
+    right = lax.all_gather(right, "core", axis=0, tiled=False)
+
+    stations = row_devices * chips * cores * blocks
+    left = left.reshape(stations, slots, rows, width)
+    right = right.reshape(stations, slots, rows, width)
+    order = (
+        jnp.arange(row_devices, dtype=jnp.int32)[None, :, None] * (chips * cores)
+        + jnp.arange(chips, dtype=jnp.int32)[None, None, :] * cores
+        + jnp.arange(cores, dtype=jnp.int32)[:, None, None]
+    ).reshape(-1)
+    picked = all_ids[order]
+    left_ids = picked[:, me_row, :]
+    right_ids = picked[:, me_chip, :] - me_core * per_col
+    right_ids = jnp.where((right_ids >= 0) & (right_ids < per_col), right_ids, -1)
+    return accumulate(left, left_ids, right, right_ids, per_row, per_col)
 
 
 def solution(mesh):
+    row_devices, col_devices = mesh.devices.shape
+    cores = 2
+    mesh3 = jax.sharding.Mesh(
+        mesh.devices.reshape(row_devices, col_devices // cores, cores), ("row", "chip", "core")
+    )
+    blocks = ("row", "chip", "core")
     in_specs = (
-        P(("row", "col"), None, None, None, None),
-        P(("row", "col"), None, None),
-        P(("row", "col"), None),
-        P(("row", "col"), None),
+        P(blocks, None, None, None, None),
+        P(blocks, None, None),
+        P(blocks, None),
+        P(blocks, None),
     )
-    out_specs = P("row", "col")
-    return jax.shard_map(local, mesh=mesh, in_specs=in_specs, out_specs=out_specs, check_vma=False)
+    out_specs = P("row", ("chip", "core"))
+    return jax.shard_map(local, mesh=mesh3, in_specs=in_specs, out_specs=out_specs, check_vma=False)

time: 380 us -> 459 us (1.21)
  blocking collectives: 116 us -> 219 us
  starting transfers between devices: 10.4 us -> 0.12 us
  waiting for transfers between devices: 194 us -> 184 us
    all_gather x2 -> x1, blocking collectives: 49 us -> 175 us  [local(): lax.all_gather(live_ids, ('row', 'chip', 'core'), axis=0, tiled=True)]
    all_to_all x1, blocking collectives: 37.3 us -> 23.8 us  [local(): lax.all_to_all(weighted, 'chip', split_axis=1, concat_axis=1, tiled=True)]
    all_to_all x2 -> x0, starting transfers between devices: 10.4 us -> none  [the longest x1 6.86 us: local(): lax.all_to_all(chosen_ids, 'col', split_axis=1, concat_axis=0, tiled=True)]
    all_to_all x1, blocking collectives: 29.4 us -> 20.7 us  [local(): lax.all_to_all(weighted, 'row', split_axis=1, concat_axis=0, tiled=True)]
    all_gather x2 -> x4, waiting for transfers between devices: 191 us -> 184 us  [the longest x1 105 us: local(): left = lax.all_gather(left, 'chip', axis=1, tiled=True)]
    sub x0 -> x1, other arithmetic: none -> 4.68 us  [local(): right_ids = picked[:, me_chip, :] - me_core * per_col]
  transfers between devices with their start and end apart: 4 -> 4, of which waited for: 3 -> 2; matrix products, arithmetic and copies ran while one was open for 1% -> 1% of each run, Pallas kernels for 0% -> 0%
where the time goes in v2:
time: 459 us; the launch traced here: 458 us
  blocking collectives  219 us (48%)
  waiting for transfers between devices  184 us (40%)
  Pallas kernels  32.7 us (7%)
  between operations  13.2 us (3%)
  other arithmetic  8.11 us (2%)
    all_gather x1, blocking collectives, local(): lax.all_gather(live_ids, ('row', 'chip', 'core'), axis=0, tiled=True)  175 us
    all_gather x1, waiting for transfers between devices, local(): left = lax.all_gather(left, 'chip', axis=1, tiled=True)  105 us
    all_gather x1, waiting for transfers between devices, local(): right = lax.all_gather(right, 'row', axis=0, tiled=True)  78.8 us
    pallas_call x1, Pallas kernels, accumulate(): pl.pallas_call(functools.partial(gram_kernel, slots, width), grid_spec=gr...  32.7 us
    all_to_all x1, blocking collectives, local(): lax.all_to_all(weighted, 'chip', split_axis=1, concat_axis=1, tiled=True)  23.8 us
    all_to_all x1, blocking collectives, local(): lax.all_to_all(weighted, 'row', split_axis=1, concat_axis=0, tiled=True)  20.7 us
  transfers between devices with their start and end apart: 4, of which 2 were waited for; matrix products, arithmetic and copies ran while one was open for 1% of the time, Pallas kernels for 0%

profile of v2, /device:TPU:1, one launch (start us, length us, event | category | flops | bytes accessed | tf_op | source)
XLA Modules:
  0.0 458.3 jit_solution(4131471339473138737)
XLA Ops:
  6.5 0.0 all-gather.8.cloned.1.call-start
  6.5 0.7 fusion
  7.3 0.8 select_reduce_fusion
  8.0 0.1 broadcast_multiply_fusion
  8.1 1.7 multiply_convert_fusion
  9.9 23.8 %all_to_all.17 = bf16[1,8,2,256,128]{4,3,2,0,1:T(8,128)(2,1)} all-to-all(bf16[1,8,2,256,128]{4,3,2,0,1:T(8,128)(2,1)S(1)} %multiply_convert_fusion), channel_id=1, replica_groups=mesh['row'=8,'chip'=8,'core'=2] {'chip'}, dimensions={1} | all-to-all | bytes 2097152 | tf_op jit(solution)/shard_map/all_to_all | solution.py:100
  33.7 0.0 all-gather.8.cloned.1.call-update
  33.7 0.0 all-gather.10.cloned.1.call-start
  33.8 20.7 %all_to_all.18 = bf16[1,8,2,256,128]{4,3,2,0,1:T(8,128)(2,1)} all-to-all(bf16[1,8,2,256,128]{4,3,2,0,1:T(8,128)(2,1)S(1)} %multiply_convert_fusion), channel_id=1, replica_groups=mesh['row'=8,'chip'=8,'core'=2] {'row'}, dimensions={1} | all-to-all | bytes 2097152 | tf_op jit(solution)/shard_map/all_to_all | solution.py:97
  54.5 0.0 all-gather.10.cloned.1.call-update
  54.5 0.0 all-gather.14.cloned.1.call-start
  54.5 78.8 %all-gather.8.cloned.1.call-done = bf16[8,8,2,256,128]{4,3,2,1,0:T(8,128)(2,1)} async-done(((bf16[1,8,2,256,128]{4,3,2,1,0:T(8,128)(2,1)}), bf16[8,8,2,256,128]{4,3,2,1,0:T(8,128)(2,1)}) %all-gather.8.cloned.1.call-update) | async-done | bytes 8388624 | tf_op jit(solution)/shard_map/all_gather | solution.py:101
  133.3 0.0 copy-start
  133.3 0.0 copy-start.1
  133.3 0.0 all-gather.14.cloned.1.call-update
  133.4 0.0 all-gather.12.cloned.1.call-start
  133.4 104.9 %all-gather.10.cloned.1.call-done = bf16[1,8,16,256,128]{4,3,2,0,1:T(8,128)(2,1)} async-done(((bf16[1,8,2,256,128]{4,3,2,0,1:T(8,128)(2,1)}), bf16[1,8,16,256,128]{4,3,2,0,1:T(8,128)(2,1)}) %all-gather.10.cloned.1.call-update) | async-done | bytes 8388624 | tf_op jit(solution)/shard_map/all_gather | solution.py:98
  238.3 0.0 all-gather.12.cloned.1.call-update
  238.4 0.1 broadcast_add_fusion
  238.5 0.1 add.67
  238.6 0.0 copy-done
  238.6 0.0 copy-done.1
  238.6 174.7 %all_gather.21 = s32[128,8,2]{1,2,0:T(2,128)S(1)} all-gather(s32[1,8,2]{1,2,0:T(2,128)S(1)} %compare_select_fusion.1), channel_id=1, replica_groups=mesh['row'=8,'chip'=8,'core'=2] {'row','chip','core'}, dimensions={0}, use_global_device_ids=true | all-gather | bytes 8256 | tf_op jit(solution)/shard_map/all_gather | solution.py:95
  413.3 0.7 gather_fusion
  414.1 4.7 %subtract_reduce_fusion = (s32[128,2]{1,0:T(8,128)S(1)}, s32[128,2]{1,0:T(8,128)S(1)}) fusion(s32[128,8,2]{1,2,0:T(2,128)S(1)} %gather_fusion, s32[]{:T(128)S(6)} %select_n.40, s32[]{:T(128)S(6)} %mul.47, s32[]{:T(128)S(6)} %select_n.39), kind=kLoop, calls=%fused_computation.2 | loop fusion | flops 256 | bytes 4108 | tf_op jit(solution)/shard_map/sub | solution.py:114
  418.8 0.1 sub.12
  418.9 0.1 reshape_squeeze.3.lids_ref
  419.0 0.0 all-gather.14.cloned.1.call-done
  419.1 0.0 all-gather.12.cloned.1.call-done
  419.1 32.7 %shard_map.61 = f32[2048,1024]{1,0:T(8,128)} custom-call(s32[256]{0:T(256)S(1)} %reshape_squeeze.3.lids_ref, s32[256]{0:T(256)S(1)} %and_select_fusion.rids_ref, bf16[128,2,256,128]{3,2,1,0:T(8,128)(2,1)} %bitcast.11, bf16[128,2,256,128]{3,2,1,0:T(8,128)(2,1)} %bitcast.10), custom_call_target="tpu_custom_call" | custom-call | flops 4294967296 | bytes 41943040 | tf_op jit(solution)/shard_map/pallas_call | solution.py:64
  (6 shorter events, 0.0 us)
Async XLA Ops:
  6.5 126.8 %all-gather.8.cloned.1.call-start = ((), (), s32[]{:S(2)}) async-start(), calls=%async_computation.2 | async-start | bytes 9437184 | tf_op jit(solution)/shard_map/all_gather | solution.py:101
  33.7 204.6 %all-gather.10.cloned.1.call-start = ((), (), s32[]{:S(2)}) async-start(), calls=%async_computation.3 | async-start | bytes 9437184 | tf_op jit(solution)/shard_map/all_gather | solution.py:98
  54.5 364.6 %all-gather.14.cloned.1.call-start = ((), (), s32[]{:S(2)}) async-start(), calls=%async_computation.5 | async-start | bytes 25165824 | tf_op jit(solution)/shard_map/all_gather | solution.py:102
  133.3 105.2 %copy-start = (s32[1,8]{1,0:T(1,128)S(1)}, s32[1,8]{1,0:T(1,128)}, u32[]{:S(2)}) copy-start(s32[1,8]{1,0:T(1,128)} %param.7) | copy-start | bytes 100
  133.3 105.2 %copy-start.1 = (s32[1,8,2]{1,2,0:T(2,128)S(1)}, s32[1,8,2]{1,2,0:T(2,128)}, u32[]{:S(2)}) copy-start(s32[1,8,2]{1,2,0:T(2,128)} %param.6) | copy-start | bytes 196
  133.4 285.7 %all-gather.12.cloned.1.call-start = ((), (), s32[]{:S(2)}) async-start(), calls=%async_computation.4 | async-start | bytes 25165824 | tf_op jit(solution)/shard_map/all_gather | solution.py:99
Sparse Core Ops, SparseCore 0:
  33.8 99.4 all-gather.7
  135.6 102.6 all-gather.9
  240.0 31.3 all-gather.13
  272.9 34.1 all-gather.11

commit v3 on v2

v3 whole, which is shorter than its diff:
```python
import functools

import jax
import jax.numpy as jnp
from jax import lax
from jax.experimental import pallas as pl
from jax.experimental.pallas import tpu as pltpu
from jax.sharding import PartitionSpec as P

TILES = 128
BAND = 16


def station_scale(weight_class):
    levels = jnp.array([1.0, 0.5, 0.25, 0.125], jnp.float32)
    hits = weight_class[..., None] == jnp.arange(4, dtype=jnp.int32)
    return jnp.sum(jnp.where(hits, levels, jnp.float32(0.0)), axis=-1)


def gram_kernel(slots, rows, width, group, lids_ref, rids_ref, left_ref, right_ref, out_ref):
    co = pl.program_id(0)
    r = pl.program_id(1)

    @pl.when((co == 0) & (r == 0))
    def _():
        out_ref[...] = jnp.zeros_like(out_ref)

    base = (co * pl.num_programs(1) + r) * group

    def body(k, carry):
        b = base + k
        for i in range(slots):
            li = lids_ref[b * slots + i]
            for j in range(slots):
                rj = rids_ref[b * slots + j]

                @pl.when((li >= 0) & (rj >= 0))
                def _():
                    prod = lax.dot_general(
                        left_ref[k, i, :rows, :],
                        right_ref[k, j, :rows, :],
                        (((0,), (0,)), ((), ())),
                        preferred_element_type=jnp.float32,
                    )
                    out_rows = pl.ds(pl.multiple_of(li * width, width), width)
                    out_cols = pl.ds(pl.multiple_of(rj * width, width), width)
                    out_ref[out_rows, out_cols] += prod

        return carry

    lax.fori_loop(0, group, body, 0)


def accumulate(left, left_ids, right, right_ids, rows, per_row, per_col):
    n_row, n_chip, n_core, slots, band_rows, width = left.shape
    block = (None, n_chip, None, slots, band_rows, width)
    grid_spec = pltpu.PrefetchScalarGridSpec(
        num_scalar_prefetch=2,
        grid=(n_core, n_row),
        in_specs=[
            pl.BlockSpec(block, lambda co, r, lids, rids: (r, 0, co, 0, 0, 0)),
            pl.BlockSpec((None, None, n_chip, slots, band_rows, width), lambda co, r, lids, rids: (co, r, 0, 0, 0, 0)),
        ],
        out_specs=pl.BlockSpec((per_row * width, per_col * width), lambda co, r, lids, rids: (0, 0)),
    )
    stations = n_row * n_chip * n_core
    flops = 2 * stations * slots * slots * rows * width * width
    return pl.pallas_call(
        functools.partial(gram_kernel, slots, rows, width, n_chip),
        grid_spec=grid_spec,
        out_shape=jax.ShapeDtypeStruct((per_row * width, per_col * width), jnp.float32),
        compiler_params=pltpu.CompilerParams(
            dimension_semantics=("arbitrary", "arbitrary"), vmem_limit_bytes=48 * 1024 * 1024
        ),
        cost_estimate=pl.CostEstimate(
            flops=flops,
            bytes_accessed=2 * left.size * 2 + per_row * per_col * width * width * 4,
            transcendentals=0,
        ),
    )(left_ids.reshape(-1), right_ids.reshape(-1), left, right)


def local(sensitivity, tile_ids, counts, weight_class):
    row_devices = lax.axis_size("row")
    chips = lax.axis_size("chip")
    cores = lax.axis_size("core")
    me_core = lax.axis_index("core")
    blocks, owners, slots, rows, width = sensitivity.shape
    per_row = TILES // row_devices
    per_col = per_row // cores
    live = jnp.arange(slots, dtype=jnp.int32)[None, None, :] < counts[:, :, None]
    factor = station_scale(weight_class)[:, None, None, :, None] * live[:, :, :, None, None].astype(
        jnp.float32
    )
    weighted = (sensitivity.astype(jnp.float32) * factor).astype(jnp.bfloat16)
    live_ids = jnp.where(live, tile_ids, -1).astype(jnp.bfloat16)
    band = jnp.zeros((blocks, owners, slots, BAND, width), jnp.bfloat16)
    band = band.at[:, :, :, 0, :].set(live_ids[..., None])
    tagged = jnp.concatenate([weighted, band], axis=3)
    band_rows = rows + BAND

    left = lax.all_to_all(tagged, "row", split_axis=1, concat_axis=0, tiled=True)
    left = lax.all_gather(left, ("chip", "core"), axis=1, tiled=True)
    left = left.reshape(row_devices, chips, cores, slots, band_rows, width)
    right = lax.all_to_all(tagged, "chip", split_axis=1, concat_axis=1, tiled=True)
    right = lax.all_gather(right, "row", axis=0, tiled=True)
    right = lax.all_gather(right, "core", axis=0, tiled=False)
    right = right.reshape(cores, row_devices, chips, slots, band_rows, width)

    left_ids = jnp.transpose(left[:, :, :, :, rows, 0], (2, 0, 1, 3)).astype(jnp.int32)
    right_ids = right[:, :, :, :, rows, 0].astype(jnp.int32) - me_core * per_col
    right_ids = jnp.where((right_ids >= 0) & (right_ids < per_col), right_ids, -1)
    return accumulate(left, left_ids, right, right_ids, rows, per_row, per_col)


def solution(mesh):
    row_devices, col_devices = mesh.devices.shape
    cores = 2
    mesh3 = jax.sharding.Mesh(
        mesh.devices.reshape(row_devices, col_devices // cores, cores), ("row", "chip", "core")
    )
    blocks = ("row", "chip", "core")
    in_specs = (
        P(blocks, None, None, None, None),
        P(blocks, None, None),
        P(blocks, None),
        P(blocks, None),
    )
    out_specs = P("row", ("chip", "core"))
    return jax.shard_map(local, mesh=mesh3, in_specs=in_specs, out_specs=out_specs, check_vma=False)
```

time: 459 us -> 340 us (0.74)
  blocking collectives: 219 us -> 49.3 us
  waiting for transfers between devices: 184 us -> 227 us
    all_gather x1 -> x0, blocking collectives: 175 us -> none  [local(): lax.all_gather(live_ids, ('row', 'chip', 'core'), axis=0, tiled=True)]
    all_gather x1, waiting for transfers between devices: 0.02 us -> 32.7 us  [local(): right = lax.all_gather(right, 'core', axis=0, tiled=False)]
    all_gather x2 -> x1, waiting for transfers between devices: 105 us -> 113 us  [local(): left = lax.all_gather(left, ('chip', 'core'), axis=1, tiled=True)]
    all_to_all x2, blocking collectives: 44.5 us -> 49.3 us  [the longest x1 24.9 us: local(): lax.all_to_all(tagged, 'chip', split_axis=1, concat_axis=1, tiled=True)]
  transfers between devices with their start and end apart: 4 -> 3, of which waited for: 2 -> 3; matrix products, arithmetic and copies ran while one was open for 1% -> 1% of each run, Pallas kernels for 0% -> 0%
where the time goes in v3:
time: 340 us; the launch traced here: 337 us
  waiting for transfers between devices  227 us (67%)
  blocking collectives  49.3 us (14%)
  Pallas kernels  35.4 us (10%)
  between operations  13.2 us (4%)
  other arithmetic  10.9 us (3%)
    all_gather x1, waiting for transfers between devices, local(): left = lax.all_gather(left, ('chip', 'core'), axis=1, tiled=True)  113 us
    all_gather x1, waiting for transfers between devices, local(): right = lax.all_gather(right, 'row', axis=0, tiled=True)  81 us
    pallas_call x1, Pallas kernels, accumulate(): pl.pallas_call(functools.partial(gram_kernel, slots, rows, width, n_chip)...  35.4 us
    all_gather x1, waiting for transfers between devices, local(): right = lax.all_gather(right, 'core', axis=0, tiled=False)  32.7 us
    all_to_all x1, blocking collectives, local(): lax.all_to_all(tagged, 'chip', split_axis=1, concat_axis=1, tiled=True)  24.9 us
    all_to_all x1, blocking collectives, local(): lax.all_to_all(tagged, 'row', split_axis=1, concat_axis=0, tiled=True)  24.4 us
  transfers between devices with their start and end apart: 3, of which 3 were waited for; matrix products, arithmetic and copies ran while one was open for 1% of the time, Pallas kernels for 0%

profile of v3, /device:TPU:1, one launch (start us, length us, event | category | flops | bytes accessed | tf_op | source)
XLA Modules:
  0.0 336.7 jit_solution(17729125983739768120)
XLA Ops:
  6.5 0.0 all-gather.6.cloned.1.call-start
  6.5 0.7 fusion.4
  7.3 0.7 fusion.6
  7.9 0.1 copy.21
  8.0 0.8 select_reduce_fusion
  8.8 0.1 broadcast_multiply_fusion
  8.9 1.7 multiply_convert_fusion
  10.7 0.1 broadcast.165
  10.7 0.1 fusion.1
  10.8 24.9 %all_to_all.17 = bf16[1,8,2,272,128]{4,3,2,0,1:T(8,128)(2,1)} all-to-all(bf16[1,8,2,272,128]{4,3,2,0,1:T(8,128)(2,1)S(1)} %fusion.1), channel_id=1, replica_groups=mesh['row'=8,'chip'=8,'core'=2] {'chip'}, dimensions={1} | all-to-all | bytes 2228224 | tf_op jit(solution)/shard_map/all_to_all | solution.py:105
  35.7 0.0 all-gather.6.cloned.1.call-update
  35.7 0.0 all-gather.8.cloned.1.call-start
  35.8 24.4 %all_to_all.18 = bf16[1,8,2,272,128]{4,3,2,0,1:T(8,128)(2,1)} all-to-all(bf16[1,8,2,272,128]{4,3,2,0,1:T(8,128)(2,1)S(1)} %fusion.1), channel_id=1, replica_groups=mesh['row'=8,'chip'=8,'core'=2] {'row'}, dimensions={1} | all-to-all | bytes 2228224 | tf_op jit(solution)/shard_map/all_to_all | solution.py:102
  60.2 0.0 all-gather.8.cloned.1.call-update
  60.2 0.0 all-gather.10.cloned.1.call-start
  60.2 81.0 %all-gather.6.cloned.1.call-done = bf16[8,8,2,272,128]{4,3,2,1,0:T(8,128)(2,1)} async-done(((bf16[1,8,2,272,128]{4,3,2,1,0:T(8,128)(2,1)}), bf16[8,8,2,272,128]{4,3,2,1,0:T(8,128)(2,1)}) %all-gather.6.cloned.1.call-update) | async-done | bytes 8912912 | tf_op jit(solution)/shard_map/all_gather | solution.py:106
  141.2 0.0 all-gather.10.cloned.1.call-update
  141.2 112.8 %all-gather.8.cloned.1.call-done = bf16[1,8,32,272,128]{4,3,2,0,1:T(8,128)(2,1)} async-done(((bf16[1,8,2,272,128]{4,3,2,0,1:T(8,128)(2,1)}), bf16[1,8,32,272,128]{4,3,2,0,1:T(8,128)(2,1)}) %all-gather.8.cloned.1.call-update) | async-done | bytes 17825808 | tf_op jit(solution)/shard_map/all_gather | solution.py:103
  254.1 1.1 slice_convert_fusion.1
  255.2 0.9 copy.25
  256.1 0.1 reshape.201.lids_ref
  256.2 32.7 %all-gather.10.cloned.1.call-done = bf16[16,8,2,272,128]{4,3,2,1,0:T(8,128)(2,1)} async-done(((bf16[8,8,2,272,128]{4,3,2,1,0:T(8,128)(2,1)}), bf16[16,8,2,272,128]{4,3,2,1,0:T(8,128)(2,1)}) %all-gather.10.cloned.1.call-update) | async-done | bytes 17825808 | tf_op jit(solution)/shard_map/all_gather | solution.py:107
  288.9 5.7 %fusion.3 = s32[2,8,8,2]{3,2,1,0:T(8,128)S(1)} fusion(bf16[2,8,8,2,272,128]{5,4,3,2,1,0:T(8,128)(2,1)} %bitcast.18, s32[]{:T(128)S(6)} %mul.34), kind=kLoop, calls=%fused_computation.7 | loop fusion | flops 512 | bytes 1540 | tf_op jit(solution)/shard_map/sub | solution.py:111
  294.6 0.1 sub.12
  294.7 35.4 %shard_map.58 = f32[2048,1024]{1,0:T(8,128)} custom-call(s32[256]{0:T(256)S(1)} %reshape.201.lids_ref, s32[256]{0:T(256)S(1)} %and_select_fusion.rids_ref, bf16[8,8,2,2,272,128]{5,4,3,2,1,0:T(8,128)(2,1)} %bitcast.17, bf16[2,8,8,2,272,128]{5,4,3,2,1,0:T(8,128)(2,1)} %bitcast.19), custom_call_target="tpu_custom_call" | custom-call | flops 4294967296 | bytes 44040192 | tf_op jit(solution)/shard_map/pallas_call | solution.py:68
  (1 shorter events, 0.0 us)
Async XLA Ops:
  6.5 134.7 %all-gather.6.cloned.1.call-start = ((), (), s32[]{:S(2)}) async-start(), calls=%async_computation.2 | async-start | bytes 10027008 | tf_op jit(solution)/shard_map/all_gather | solution.py:106
  35.7 218.3 %all-gather.8.cloned.1.call-start = ((), (), s32[]{:S(2)}) async-start(), calls=%async_computation.3 | async-start | bytes 18939904 | tf_op jit(solution)/shard_map/all_gather | solution.py:103
  60.2 228.7 %all-gather.10.cloned.1.call-start = ((), (), s32[]{:S(2)}) async-start(), calls=%async_computation.4 | async-start | bytes 26738688 | tf_op jit(solution)/shard_map/all_gather | solution.py:107
Sparse Core Ops, SparseCore 0:
  35.8 105.2 all-gather.5
  143.7 110.2 all-gather.7
  255.7 33.0 all-gather.9

commit v4 on v3

v4 whole, which is shorter than its diff:
```python
import functools

import jax
import jax.numpy as jnp
from jax import lax
from jax.experimental import pallas as pl
from jax.experimental.pallas import tpu as pltpu
from jax.sharding import PartitionSpec as P

TILES = 128
BAND = 16


def station_scale(weight_class):
    levels = jnp.array([1.0, 0.5, 0.25, 0.125], jnp.float32)
    hits = weight_class[..., None] == jnp.arange(4, dtype=jnp.int32)
    return jnp.sum(jnp.where(hits, levels, jnp.float32(0.0)), axis=-1)


def gram_kernel(slots, rows, width, group, carry_in, lids_ref, rids_ref, rot_ref, *refs):
    if carry_in:
        prev_ref, left_ref, right_ref, out_ref = refs
    else:
        left_ref, right_ref, out_ref = refs
    r = pl.program_id(0)

    @pl.when(r == 0)
    def _():
        if carry_in:
            out_ref[...] = prev_ref[...]
        else:
            out_ref[...] = jnp.zeros_like(out_ref)

    def body(k, carry):
        b = r * group + k
        for i in range(slots):
            li = lids_ref[b * slots + i]
            for j in range(slots):
                rj = rids_ref[b * slots + j]

                @pl.when((li >= 0) & (rj >= 0))
                def _():
                    prod = lax.dot_general(
                        left_ref[k, i, :rows, :],
                        right_ref[k, j, :rows, :],
                        (((0,), (0,)), ((), ())),
                        preferred_element_type=jnp.float32,
                    )
                    out_rows = pl.ds(pl.multiple_of(li * width, width), width)
                    out_cols = pl.ds(pl.multiple_of(rj * width, width), width)
                    out_ref[out_rows, out_cols] += prod

        return carry

    lax.fori_loop(0, group, body, 0)


def accumulate(prev, left, left_ids, right, right_ids, rot, rows, per_row, per_col):
    n_row, n_chip, n_core, slots, band_rows, width = left.shape
    n_y = right.shape[0]
    out_shape = (per_row * width, per_col * width)

    def right_map(r, lids, rids, rot):
        return (lax.rem(lax.rem(r, n_y) - rot[0] + n_y, n_y), r // n_y, 0, 0, 0, 0)

    in_specs = [
        pl.BlockSpec((None, n_chip, None, slots, band_rows, width), lambda r, lids, rids, rot: (r, 0, rot[1], 0, 0, 0)),
        pl.BlockSpec((None, None, n_chip, slots, band_rows, width), right_map),
    ]
    operands = [left, right]
    carry_in = prev is not None
    if carry_in:
        in_specs = [pl.BlockSpec(out_shape, lambda r, lids, rids, rot: (0, 0))] + in_specs
        operands = [prev] + operands
    grid_spec = pltpu.PrefetchScalarGridSpec(
        num_scalar_prefetch=3,
        grid=(n_row,),
        in_specs=in_specs,
        out_specs=pl.BlockSpec(out_shape, lambda r, lids, rids, rot: (0, 0)),
    )
    stations = n_row * n_chip
    flops = 2 * stations * slots * slots * rows * width * width
    return pl.pallas_call(
        functools.partial(gram_kernel, slots, rows, width, n_chip, carry_in),
        grid_spec=grid_spec,
        out_shape=jax.ShapeDtypeStruct(out_shape, jnp.float32),
        input_output_aliases={3: 0} if carry_in else {},
        compiler_params=pltpu.CompilerParams(
            dimension_semantics=("arbitrary",), vmem_limit_bytes=56 * 1024 * 1024
        ),
        cost_estimate=pl.CostEstimate(
            flops=flops,
            bytes_accessed=2 * right.size * 2 + per_row * per_col * width * width * 4,
            transcendentals=0,
        ),
    )(left_ids.reshape(-1), right_ids.reshape(-1), rot, *operands)

def shift(x, axis, step):
    n = lax.axis_size(axis)
    return lax.ppermute(x, axis, [(i, (i + step) % n) for i in range(n)])


def ring_gather(piece):
    other = shift(piece, "xlo", 1)
    first = lax.axis_index("xlo") == 0
    bundle = jnp.where(first, jnp.stack([piece, other]), jnp.stack([other, piece]))
    from_below = shift(bundle, "y", 1)
    from_above = shift(bundle, "y", -1)
    far_low = shift(from_below[:1], "y", 1)
    far_high = shift(from_above[1:], "y", -1)
    far = jnp.concatenate([far_low, far_high], axis=0)
    return jnp.stack([bundle, from_above, far, from_below])


def local(sensitivity, tile_ids, counts, weight_class):
    row_devices = lax.axis_size("xlo") * lax.axis_size("y")
    chips = lax.axis_size("chip")
    cores = lax.axis_size("core")
    me_core = lax.axis_index("core")
    blocks, owners, slots, rows, width = sensitivity.shape
    per_row = TILES // row_devices
    per_col = per_row // cores
    live = jnp.arange(slots, dtype=jnp.int32)[None, None, :] < counts[:, :, None]
    factor = station_scale(weight_class)[:, None, None, :, None] * live[:, :, :, None, None].astype(
        jnp.float32
    )
    weighted = (sensitivity.astype(jnp.float32) * factor).astype(jnp.bfloat16)
    live_ids = jnp.where(live, tile_ids, -1).astype(jnp.bfloat16)
    band = jnp.zeros((blocks, owners, slots, BAND, width), jnp.bfloat16)
    band = band.at[:, :, :, 0, :].set(live_ids[..., None])
    tagged = jnp.concatenate([weighted, band], axis=3)
    band_rows = rows + BAND

    left = lax.all_to_all(tagged, ("xlo", "y"), split_axis=1, concat_axis=0, tiled=True)
    left, tagged = lax.optimization_barrier((left, tagged))
    left = lax.all_gather(left, ("chip", "core"), axis=1, tiled=True)
    left = left.reshape(row_devices, chips, cores, slots, band_rows, width)
    right = lax.all_to_all(tagged, "chip", split_axis=1, concat_axis=1, tiled=True)
    right_own = ring_gather(right[0])
    right_other = shift(right_own, "core", 1)

    n_y = lax.axis_size("y")
    me_y = lax.axis_index("y")
    absolute_y = (jnp.arange(n_y, dtype=jnp.int32) - me_y) % n_y
    band_ids = left[:, :, :, :, rows, 0].astype(jnp.int32)

    def part(prev, right_half, core):
        left_ids = band_ids[:, :, core]
        right_ids = right_half[:, :, :, :, rows, 0].astype(jnp.int32) - me_core * per_col
        right_ids = jnp.transpose(right_ids[absolute_y], (1, 0, 2, 3))
        right_ids = jnp.where((right_ids >= 0) & (right_ids < per_col), right_ids, -1)
        rot = jnp.stack([me_y, core]).astype(jnp.int32)
        return accumulate(prev, left, left_ids, right_half, right_ids, rot, rows, per_row, per_col)

    normal = part(None, right_own, me_core)
    return part(normal, right_other, 1 - me_core)

def solution(mesh):
    row_devices, col_devices = mesh.devices.shape
    cores = 2
    x_lo = 2
    mesh3 = jax.sharding.Mesh(
        mesh.devices.reshape(x_lo, row_devices // x_lo, col_devices // cores, cores),
        ("xlo", "y", "chip", "core"),
    )
    blocks = ("xlo", "y", "chip", "core")
    in_specs = (
        P(blocks, None, None, None, None),
        P(blocks, None, None),
        P(blocks, None),
        P(blocks, None),
    )
    out_specs = P(("xlo", "y"), ("chip", "core"))
    return jax.shard_map(local, mesh=mesh3, in_specs=in_specs, out_specs=out_specs, check_vma=False)
```

time: 340 us -> 263 us (0.77)
  the two profiles are of different devices: /device:TPU:1 before, /device:TPU:7 now
where the time goes in v4:
time: 263 us
  waiting for transfers between devices  109 us (41%)
  Pallas kernels  51.5 us (20%)
  blocking collectives  41.2 us (16%)
  local copies, waits for them, and re-layouts  23.7 us (9%)
  between operations  13.5 us (5%)
  starting transfers between devices  12 us (5%)
  other arithmetic  11.9 us (5%)
    ppermute x6, waiting for transfers between devices, shift(): return lax.ppermute(x, axis, [(i, (i + step) % n) for i in range(n)])  109 us
    pallas_call x2, Pallas kernels, accumulate(): pl.pallas_call(functools.partial(gram_kernel, slots, rows, width, n_chip,...  51.5 us
    all_to_all x1, blocking collectives, local(): lax.all_to_all(tagged, 'chip', split_axis=1, concat_axis=1, tiled=True)  21.6 us
    all_to_all x1, blocking collectives, local(): lax.all_to_all(tagged, ('xlo', 'y'), split_axis=1, concat_axis=0, tiled=T...  19.5 us
    ppermute x6, starting transfers between devices, shift(): return lax.ppermute(x, axis, [(i, (i + step) % n) for i in range(n)])  12 us
    all_gather x1, local copies, waits for them, and re-layouts, local(): left = lax.all_gather(left, ('chip', 'core'), axis=1, tiled=True)  8.23 us
    unnamed x2, local copies, waits for them, and re-layouts  6.1 us
  transfers between devices with their start and end apart: 7, of which 5 were waited for; matrix products, arithmetic and copies ran while one was open for 4% of the time, Pallas kernels for 0%

profile of v4, /device:TPU:7, one launch (start us, length us, event | category | flops | bytes accessed | tf_op | source)
XLA Modules:
  0.0 262.6 jit_solution(13080147485299962600)
XLA Ops:
  6.5 0.0 all-gather.2.cloned.1.call-start
  6.5 0.7 fusion.4
  7.3 0.7 fusion.6
  7.9 0.1 copy.48
  8.0 0.8 select_reduce_fusion
  8.8 0.1 broadcast_multiply_fusion
  8.9 1.7 multiply_convert_fusion
  10.7 0.1 broadcast.238
  10.7 0.1 fusion.1
  10.8 19.5 %all_to_all.17 = bf16[1,8,2,272,128]{4,3,2,0,1:T(8,128)(2,1)} all-to-all(bf16[1,8,2,272,128]{4,3,2,0,1:T(8,128)(2,1)S(1)} %fusion.1), channel_id=1, replica_groups=mesh['xlo'=2,'y'=4,'chip'=8,'core'=2] {'xlo','y'}, dimensions={1} | all-to-all | bytes 2228224 | tf_op jit(solution)/shard_map/all_to_all | solution.py:134
  30.4 0.0 all-gather.2.cloned.1.call-update
  30.4 21.6 %all_to_all.18 = bf16[1,8,2,272,128]{4,3,2,0,1:T(8,128)(2,1)S(1)} all-to-all(bf16[1,8,2,272,128]{4,3,2,0,1:T(8,128)(2,1)S(1)} %fusion.1), channel_id=1, replica_groups=mesh['xlo'=2,'y'=4,'chip'=8,'core'=2] {'chip'}, dimensions={1} | all-to-all | bytes 2228224 | tf_op jit(solution)/shard_map/all_to_all | solution.py:138
  52.0 1.9 collective-permute-start
  54.0 30.8 %collective-permute-done = bf16[8,2,272,128]{3,2,1,0:T(8,128)(2,1)S(1)} collective-permute-done((bf16[8,2,272,128]{3,2,1,0:T(8,128)(2,1)S(1)}, bf16[8,2,272,128]{3,2,1,0:T(8,128)(2,1)S(1)}, u32[]{:S(2)}, u32[]{:S(2)}) %collective-permute-start) | collective-permute-done | bytes 1114144 | tf_op jit(solution)/shard_map/ppermute | solution.py:100
  84.8 0.4 maximum_select_fusion.1
  85.2 1.5 collective-permute-start.1
  86.6 0.1 collective-permute-start.2
  86.7 44.9 %collective-permute-done.1 = bf16[2,8,2,272,128]{4,3,2,1,0:T(8,128)(2,1)S(1)} collective-permute-done((bf16[2,8,2,272,128]{4,3,2,1,0:T(8,128)(2,1)S(1)}, bf16[2,8,2,272,128]{4,3,2,1,0:T(8,128)(2,1)S(1)}, u32[]{:S(2)}, u32[]{:S(2)}) %collective-permute-start.1) | collective-permute-done | bytes 2228256 | tf_op jit(solution)/shard_map/ppermute | solution.py:100
  131.5 0.1 slice.55
  131.6 3.2 %collective-permute-start.4 = (bf16[1,8,2,272,128]{4,3,2,1,0:T(8,128)(2,1)S(1)}, bf16[1,8,2,272,128]{4,3,2,1,0:T(8,128)(2,1)S(1)}, u32[]{:S(2)}, u32[]{:S(2)}) collective-permute-start(bf16[1,8,2,272,128]{4,3,2,1,0:T(8,128)(2,1)S(1)} %slice.55), channel_id=1, source_target_pairs={{0,48},{16,0},{32,16},{48,32},{1,49},{17,1},{33,17},{49,33},{2,50}... | collective-permute-start | bytes 3342344 | tf_op jit(solution)/shard_map/ppermute | solution.py:100
  134.8 0.0 collective-permute-done.2
  134.8 0.1 slice.54
  134.9 0.1 collective-permute-start.3
  134.9 0.4 maximum_select_fusion
  135.3 19.3 %collective-permute-done.4 = bf16[1,8,2,272,128]{4,3,2,1,0:T(8,128)(2,1)S(1)} collective-permute-done((bf16[1,8,2,272,128]{4,3,2,1,0:T(8,128)(2,1)S(1)}, bf16[1,8,2,272,128]{4,3,2,1,0:T(8,128)(2,1)S(1)}, u32[]{:S(2)}, u32[]{:S(2)}) %collective-permute-start.4) | collective-permute-done | bytes 1114144 | tf_op jit(solution)/shard_map/ppermute | solution.py:100
  154.6 3.3 %collective-permute-done.3 = bf16[1,8,2,272,128]{4,3,2,1,0:T(8,128)(2,1)S(1)} collective-permute-done((bf16[1,8,2,272,128]{4,3,2,1,0:T(8,128)(2,1)S(1)}, bf16[1,8,2,272,128]{4,3,2,1,0:T(8,128)(2,1)S(1)}, u32[]{:S(2)}, u32[]{:S(2)}) %collective-permute-start.3) | collective-permute-done | bytes 1114144 | tf_op jit(solution)/shard_map/ppermute | solution.py:100
  157.9 0.2 maximum_bitcast_fusion
  158.1 4.0 %pad_maximum_fusion.refs_1_ = bf16[4,2,8,2,272,128]{5,4,3,2,1,0:T(8,128)(2,1)} fusion(bf16[1,2,8,2,272,128]{5,4,3,2,1,0:T(8,128)(2,1)S(1)} %bitcast.39, bf16[1,2,8,2,272,128]{5,4,3,2,1,0:T(8,128)(2,1)S(1)} %maximum_bitcast_fusion, bf16[1,2,8,2,272,128]{5,4,3,2,1,0:T(8,128)(2,1)S(1)} %bitcast.38, bf16[1,2,8,2,272,128]{5,4,3,2,1,0:T(8,128)(2,1)S(1)} %maximum_select_fusion), kind=kLoop, calls=%fused_computation.2 | loop fusion | flops 13369344 | bytes 17825792 | tf_op jit(solution)/shard_map/stack | solution.py:112
  162.1 5.2 %collective-permute-start.5 = (bf16[4,2,8,2,272,128]{5,4,3,2,1,0:T(8,128)(2,1)}, bf16[4,2,8,2,272,128]{5,4,3,2,1,0:T(8,128)(2,1)}, u32[]{:S(2)}, u32[]{:S(2)}) collective-permute-start(bf16[4,2,8,2,272,128]{5,4,3,2,1,0:T(8,128)(2,1)} %pad_maximum_fusion.refs_1_), channel_id=1, source_target_pairs={{0,1},{1,0},{2,3},{3,2},{4,5},{5,4},{6,7},{7,6},{8,9},{9,8},{10,11... | collective-permute-start | bytes 26738696 | tf_op jit(solution)/shard_map/ppermute | solution.py:100
  167.4 0.7 pad_add_fusion
  168.1 1.0 fusion.2
  169.1 0.2 copy.55
  169.3 0.6 gather_fusion.1
  169.8 0.1 copy.57
  170.0 0.6 reshape.310.rids_ref
  170.6 10.6 %collective-permute-done.5.refs_2_ = bf16[4,2,8,2,272,128]{5,4,3,2,1,0:T(8,128)(2,1)} collective-permute-done((bf16[4,2,8,2,272,128]{5,4,3,2,1,0:T(8,128)(2,1)}, bf16[4,2,8,2,272,128]{5,4,3,2,1,0:T(8,128)(2,1)}, u32[]{:S(2)}, u32[]{:S(2)}) %collective-permute-start.5) | collective-permute-done | bytes 8912928 | tf_op jit(solution)/shard_map/ppermute | solution.py:100
  181.3 1.0 fusion.3
  182.3 0.2 copy.52
  182.5 0.6 gather_fusion
  183.0 0.1 copy.54
  183.2 0.6 reshape.309.rids_ref
  183.8 0.0 all-gather.2.cloned.1.call-done
  183.8 8.2 %copy.49 = bf16[8,16,2,272,128]{4,3,2,1,0:T(8,128)(2,1)S(1)} copy(bf16[8,16,2,272,128]{4,3,2,0,1:T(8,128)(2,1)} %all-gather.2.cloned.1.call-done) | data formatting | bytes 35651584 | tf_op jit(solution)/shard_map/all_gather | solution.py:136
  192.1 0.0 copy-start
  192.1 6.1 %copy-done = bf16[8,16,2,272,128]{4,3,2,1,0:T(8,128)(2,1)} copy-done((bf16[8,16,2,272,128]{4,3,2,1,0:T(8,128)(2,1)}, bf16[8,16,2,272,128]{4,3,2,1,0:T(8,128)(2,1)S(1)}, u32[]{:S(2)}) %copy-start) | copy-done | bytes 17825816
  198.2 0.1 slice_convert_fusion
  198.3 4.6 %dynamic-slice_reduce_fusion = (s32[8,8,2]{2,1,0:T(8,128)S(1)}, s32[8,8,2]{2,1,0:T(8,128)S(1)}) fusion(s32[8,8,2,2,1,1]{5,4,3,2,1,0:T(1,128)S(1)} %slice_convert_fusion, s32[]{:T(128)S(6)} %select_n.83, s32[]{:T(128)S(6)} %select_n.75), kind=kLoop, calls=%fused_computation.15 | loop fusion | bytes 2056 | tf_op jit(solution)/shard_map/dynamic_slice | solution.py:148
  202.9 0.7 reshape_squeeze.6.lids_ref
  203.6 0.7 reshape_squeeze.7.lids_ref
  204.3 25.2 %shard_map.58.refs_0_ = f32[2048,1024]{1,0:T(8,128)} custom-call(s32[128]{0:T(128)} %reshape_squeeze.7.lids_ref, s32[128]{0:T(128)} %reshape.310.rids_ref, s32[2]{0:T(128)} %get-tuple-element.24.rot_ref, bf16[8,8,2,2,272,128]{5,4,3,2,1,0:T(8,128)(2,1)} %bitcast.33, bf16[4,2,8,2,272,128]{5,4,3,2,1,0:T(8,128)(2,1)} %pad_maximum_fusion.refs_1_), custom_call_target="tpu_custom_call" | custom-call | flops 2147483648 | bytes 26214400 | tf_op jit(solution)/shard_map/pallas_call | solution.py:83
  229.5 26.3 %shard_map.59 = f32[2048,1024]{1,0:T(8,128)} custom-call(s32[128]{0:T(128)} %reshape_squeeze.6.lids_ref, s32[128]{0:T(128)} %reshape.309.rids_ref, s32[2]{0:T(128)} %get-tuple-element.23.rot_ref, f32[2048,1024]{1,0:T(8,128)} %shard_map.58.refs_0_, bf16[8,8,2,2,272,128]{5,4,3,2,1,0:T(8,128)(2,1)} %bitcast.34, ...), custom_call_target="tpu_custom_call", output_to_operand_aliasing={{}: (3, {})} | custom-call | flops 2147483648 | bytes 26214400 | tf_op jit(solution)/shard_map/pallas_call | solution.py:83
  (6 shorter events, 0.1 us)
Async XLA Ops:
  6.5 177.3 %all-gather.2.cloned.1.call-start = ((), (), s32[]{:S(2)}) async-start(), calls=%async_computation.2 | async-start | bytes 18939904 | tf_op jit(solution)/shard_map/all_gather | solution.py:136
  52.0 32.8 %collective-permute-start = (bf16[8,2,272,128]{3,2,1,0:T(8,128)(2,1)S(1)}, bf16[8,2,272,128]{3,2,1,0:T(8,128)(2,1)S(1)}, u32[]{:S(2)}, u32[]{:S(2)}) collective-permute-start(bf16[8,2,272,128]{3,2,1,0:T(8,128)(2,1)S(1)} %bitcast.35), channel_id=1, source_target_pairs={{0,64},{64,0},{1,65},{65,1},{2,66},{66,2},{3,67},{67,3},{4,68},{68... | collective-permute-start | bytes 3342344 | tf_op jit(solution)/shard_map/ppermute | solution.py:100
  85.2 46.4 %collective-permute-start.1 = (bf16[2,8,2,272,128]{4,3,2,1,0:T(8,128)(2,1)S(1)}, bf16[2,8,2,272,128]{4,3,2,1,0:T(8,128)(2,1)S(1)}, u32[]{:S(2)}, u32[]{:S(2)}) collective-permute-start(bf16[2,8,2,272,128]{4,3,2,1,0:T(8,128)(2,1)S(1)} %maximum_select_fusion.1), channel_id=1, source_target_pairs={{0,48},{16,0},{32,16},{48,32},{1,49},{17,1},{33,17},{49,33},{2,50}... | collective-permute-start | bytes 6684680 | tf_op jit(solution)/shard_map/ppermute | solution.py:100
  86.6 48.2 %collective-permute-start.2 = (bf16[2,8,2,272,128]{4,3,2,1,0:T(8,128)(2,1)S(1)}, bf16[2,8,2,272,128]{4,3,2,1,0:T(8,128)(2,1)S(1)}, u32[]{:S(2)}, u32[]{:S(2)}) collective-permute-start(bf16[2,8,2,272,128]{4,3,2,1,0:T(8,128)(2,1)S(1)} %maximum_select_fusion.1), channel_id=1, source_target_pairs={{0,16},{16,32},{32,48},{48,0},{1,17},{17,33},{33,49},{49,1},{2,18}... | collective-permute-start | bytes 6684680 | tf_op jit(solution)/shard_map/ppermute | solution.py:100
  131.6 23.0 %collective-permute-start.4 = (bf16[1,8,2,272,128]{4,3,2,1,0:T(8,128)(2,1)S(1)}, bf16[1,8,2,272,128]{4,3,2,1,0:T(8,128)(2,1)S(1)}, u32[]{:S(2)}, u32[]{:S(2)}) collective-permute-start(bf16[1,8,2,272,128]{4,3,2,1,0:T(8,128)(2,1)S(1)} %slice.55), channel_id=1, source_target_pairs={{0,48},{16,0},{32,16},{48,32},{1,49},{17,1},{33,17},{49,33},{2,50}... | collective-permute-start | bytes 3342344 | tf_op jit(solution)/shard_map/ppermute | solution.py:100
  134.9 23.0 %collective-permute-start.3 = (bf16[1,8,2,272,128]{4,3,2,1,0:T(8,128)(2,1)S(1)}, bf16[1,8,2,272,128]{4,3,2,1,0:T(8,128)(2,1)S(1)}, u32[]{:S(2)}, u32[]{:S(2)}) collective-permute-start(bf16[1,8,2,272,128]{4,3,2,1,0:T(8,128)(2,1)S(1)} %slice.54), channel_id=1, source_target_pairs={{0,16},{16,32},{32,48},{48,0},{1,17},{17,33},{33,49},{49,1},{2,18}... | collective-permute-start | bytes 3342344 | tf_op jit(solution)/shard_map/ppermute | solution.py:100
  162.1 19.1 %collective-permute-start.5 = (bf16[4,2,8,2,272,128]{5,4,3,2,1,0:T(8,128)(2,1)}, bf16[4,2,8,2,272,128]{5,4,3,2,1,0:T(8,128)(2,1)}, u32[]{:S(2)}, u32[]{:S(2)}) collective-permute-start(bf16[4,2,8,2,272,128]{5,4,3,2,1,0:T(8,128)(2,1)} %pad_maximum_fusion.refs_1_), channel_id=1, source_target_pairs={{0,1},{1,0},{2,3},{3,2},{4,5},{5,4},{6,7},{7,6},{8,9},{9,8},{10,11... | collective-permute-start | bytes 26738696 | tf_op jit(solution)/shard_map/ppermute | solution.py:100
  192.1 6.1 %copy-start = (bf16[8,16,2,272,128]{4,3,2,1,0:T(8,128)(2,1)}, bf16[8,16,2,272,128]{4,3,2,1,0:T(8,128)(2,1)S(1)}, u32[]{:S(2)}) copy-start(bf16[8,16,2,272,128]{4,3,2,1,0:T(8,128)(2,1)S(1)} %copy.49) | copy-start | bytes 53477380
Sparse Core Ops, SparseCore 0:
  30.5 126.0 all-gather.1

commit v5 on v4

--- a/solution.py
+++ b/solution.py
@@ -31,8 +31,13 @@
         else:
             out_ref[...] = jnp.zeros_like(out_ref)
 
+    n_z = left_ref.shape[1]
+
     def body(k, carry):
         b = r * group + k
+        x_rel = k // n_z
+        z_rel = lax.rem(k, n_z)
+        chip = lax.rem(rot_ref[1] + x_rel, 2) * n_z + lax.rem(rot_ref[2] + z_rel, n_z)
         for i in range(slots):
             li = lids_ref[b * slots + i]
             for j in range(slots):
@@ -41,8 +46,8 @@
                 @pl.when((li >= 0) & (rj >= 0))
                 def _():
                     prod = lax.dot_general(
-                        left_ref[k, i, :rows, :],
-                        right_ref[k, j, :rows, :],
+                        left_ref[x_rel, z_rel, i, :rows, :],
+                        right_ref[chip, j, :rows, :],
                         (((0,), (0,)), ((), ())),
                         preferred_element_type=jnp.float32,
                     )
@@ -56,7 +61,8 @@
 
 
 def accumulate(prev, left, left_ids, right, right_ids, rot, rows, per_row, per_col):
-    n_row, n_chip, n_core, slots, band_rows, width = left.shape
+    n_xhi, n_z, n_row, slots, band_rows, width = left.shape
+    n_chip = n_xhi * n_z
     n_y = right.shape[0]
     out_shape = (per_row * width, per_col * width)
 
@@ -64,7 +70,7 @@
         return (lax.rem(lax.rem(r, n_y) - rot[0] + n_y, n_y), r // n_y, 0, 0, 0, 0)
 
     in_specs = [
-        pl.BlockSpec((None, n_chip, None, slots, band_rows, width), lambda r, lids, rids, rot: (r, 0, rot[1], 0, 0, 0)),
+        pl.BlockSpec((n_xhi, n_z, None, slots, band_rows, width), lambda r, lids, rids, rot: (0, 0, r, 0, 0, 0)),
         pl.BlockSpec((None, None, n_chip, slots, band_rows, width), right_map),
     ]
     operands = [left, right]
@@ -100,6 +106,16 @@
     return lax.ppermute(x, axis, [(i, (i + step) % n) for i in range(n)])
 
 
+def z_ring(piece):
+    from_above = shift(piece, "z", -1)
+    from_below = shift(piece, "z", 1)
+    half = piece.shape[0] // 2
+    far_low = shift(from_below[:half], "z", 1)
+    far_high = shift(from_above[half:], "z", -1)
+    far = jnp.concatenate([far_low, far_high], axis=0)
+    return jnp.stack([piece, from_above, far, from_below])
+
+
 def ring_gather(piece):
     other = shift(piece, "xlo", 1)
     first = lax.axis_index("xlo") == 0
@@ -114,7 +130,7 @@
 
 def local(sensitivity, tile_ids, counts, weight_class):
     row_devices = lax.axis_size("xlo") * lax.axis_size("y")
-    chips = lax.axis_size("chip")
+    chips = lax.axis_size("xhi") * lax.axis_size("z")
     cores = lax.axis_size("core")
     me_core = lax.axis_index("core")
     blocks, owners, slots, rows, width = sensitivity.shape
@@ -132,43 +148,51 @@
     band_rows = rows + BAND
 
     left = lax.all_to_all(tagged, ("xlo", "y"), split_axis=1, concat_axis=0, tiled=True)
-    left, tagged = lax.optimization_barrier((left, tagged))
-    left = lax.all_gather(left, ("chip", "core"), axis=1, tiled=True)
-    left = left.reshape(row_devices, chips, cores, slots, band_rows, width)
-    right = lax.all_to_all(tagged, "chip", split_axis=1, concat_axis=1, tiled=True)
+    left = z_ring(left[:, 0])
+    left_own = jnp.stack([left, shift(left, "xhi", 1)])
+    right = lax.all_to_all(tagged, ("xhi", "z"), split_axis=1, concat_axis=1, tiled=True)
     right_own = ring_gather(right[0])
+    left_other = shift(left_own, "core", 1)
     right_other = shift(right_own, "core", 1)
 
     n_y = lax.axis_size("y")
+    n_z = lax.axis_size("z")
+    n_xhi = lax.axis_size("xhi")
     me_y = lax.axis_index("y")
+    me_z = lax.axis_index("z")
+    me_xhi = lax.axis_index("xhi")
     absolute_y = (jnp.arange(n_y, dtype=jnp.int32) - me_y) % n_y
-    band_ids = left[:, :, :, :, rows, 0].astype(jnp.int32)
+    k_rel = jnp.arange(n_xhi * n_z, dtype=jnp.int32)
+    chip_of = ((me_xhi + k_rel // n_z) % n_xhi) * n_z + (me_z + k_rel % n_z) % n_z
 
-    def part(prev, right_half, core):
-        left_ids = band_ids[:, :, core]
+    def part(prev, left_half, right_half):
+        left_ids = left_half[:, :, :, :, rows, 0].astype(jnp.int32)
+        left_ids = jnp.transpose(left_ids, (2, 0, 1, 3))
         right_ids = right_half[:, :, :, :, rows, 0].astype(jnp.int32) - me_core * per_col
-        right_ids = jnp.transpose(right_ids[absolute_y], (1, 0, 2, 3))
+        right_ids = jnp.transpose(right_ids[absolute_y], (1, 0, 2, 3)).reshape(row_devices, chips, slots)
+        right_ids = right_ids[:, chip_of]
         right_ids = jnp.where((right_ids >= 0) & (right_ids < per_col), right_ids, -1)
-        rot = jnp.stack([me_y, core]).astype(jnp.int32)
-        return accumulate(prev, left, left_ids, right_half, right_ids, rot, rows, per_row, per_col)
+        rot = jnp.stack([me_y, me_xhi, me_z]).astype(jnp.int32)
+        return accumulate(prev, left_half, left_ids, right_half, right_ids, rot, rows, per_row, per_col)
 
-    normal = part(None, right_own, me_core)
-    return part(normal, right_other, 1 - me_core)
+    normal = part(None, left_own, right_own)
+    return part(normal, left_other, right_other)
 
 def solution(mesh):
     row_devices, col_devices = mesh.devices.shape
     cores = 2
     x_lo = 2
+    x_hi = 2
     mesh3 = jax.sharding.Mesh(
-        mesh.devices.reshape(x_lo, row_devices // x_lo, col_devices // cores, cores),
-        ("xlo", "y", "chip", "core"),
+        mesh.devices.reshape(x_lo, row_devices // x_lo, x_hi, col_devices // cores // x_hi, cores),
+        ("xlo", "y", "xhi", "z", "core"),
     )
-    blocks = ("xlo", "y", "chip", "core")
+    blocks = ("xlo", "y", "xhi", "z", "core")
     in_specs = (
         P(blocks, None, None, None, None),
         P(blocks, None, None),
         P(blocks, None),
         P(blocks, None),
     )
-    out_specs = P(("xlo", "y"), ("chip", "core"))
+    out_specs = P(("xlo", "y"), ("xhi", "z", "core"))
     return jax.shard_map(local, mesh=mesh3, in_specs=in_specs, out_specs=out_specs, check_vma=False)

time: 263 us -> 254 us (0.966)
  the two profiles are of different devices: /device:TPU:7 before, /device:TPU:1 now
where the time goes in v5:
time: 254 us; the launch traced here: 251 us
  waiting for transfers between devices  89.3 us (35%)
  blocking collectives  56.2 us (22%)
  Pallas kernels  42.7 us (17%)
  starting transfers between devices  27.6 us (11%)
  other arithmetic  26.7 us (11%)
  local copies, waits for them, and re-layouts  8.15 us (3%)
    ppermute x12, waiting for transfers between devices, shift(): return lax.ppermute(x, axis, [(i, (i + step) % n) for i in range(n)])  89.3 us
    pallas_call x2, Pallas kernels, accumulate(): pl.pallas_call(functools.partial(gram_kernel, slots, rows, width, n_chip,...  42.7 us
    all_to_all x1, blocking collectives, local(): lax.all_to_all(tagged, ('xhi', 'z'), split_axis=1, concat_axis=1, tiled=T...  35.2 us
    ppermute x12, starting transfers between devices, shift(): return lax.ppermute(x, axis, [(i, (i + step) % n) for i in range(n)])  27.6 us
    all_to_all x1, blocking collectives, local(): lax.all_to_all(tagged, ('xlo', 'y'), split_axis=1, concat_axis=0, tiled=T...  21 us
    another operation x2, other arithmetic, local(): left_own = jnp.stack([left, shift(left, 'xhi', 1)])  10.4 us
  transfers between devices with their start and end apart: 12, of which 7 were waited for; matrix products, arithmetic and copies ran while one was open for 11% of the time, Pallas kernels for 8%

profile of v5, /device:TPU:1, one launch (start us, length us, event | category | flops | bytes accessed | tf_op | source)
XLA Modules:
  0.0 250.7 jit_solution(13652600366160948794)
XLA Ops:
  0.0 0.7 fusion.6
  0.7 0.7 fusion.11
  1.4 0.1 copy.72
  1.5 0.8 select_reduce_fusion
  2.3 0.1 broadcast_multiply_fusion
  2.4 1.7 multiply_convert_fusion
  4.1 0.1 broadcast.431
  4.2 0.1 fusion.1
  4.3 21.0 %all_to_all.14 = bf16[1,8,2,272,128]{4,3,2,0,1:T(8,128)(2,1)S(1)} all-to-all(bf16[1,8,2,272,128]{4,3,2,0,1:T(8,128)(2,1)S(1)} %fusion.1), channel_id=1, replica_groups=mesh['xlo'=2,'y'=4,'xhi'=2,'z'=4,'core'=2] {'xlo','y'}, dimensions={1} | all-to-all | bytes 2228224 | tf_op jit(solution)/shard_map/all_to_all | solution.py:150
  25.3 1.6 collective-permute-start.1
  26.9 2.1 collective-permute-start
  29.1 35.2 %all_to_all.15 = bf16[1,8,2,272,128]{4,3,2,0,1:T(8,128)(2,1)S(1)} all-to-all(bf16[1,8,2,272,128]{4,3,2,0,1:T(8,128)(2,1)S(1)} %fusion.1), channel_id=1, replica_groups=mesh['xlo'=2,'y'=4,'xhi'=2,'z'=4,'core'=2] {'xhi','z'}, dimensions={1} | all-to-all | bytes 2228224 | tf_op jit(solution)/shard_map/all_to_all | solution.py:153
  64.3 0.6 collective-permute-start.6
  64.9 0.9 slice.69
  65.8 0.5 collective-permute-start.2
  66.3 0.9 slice.70
  67.2 0.3 copy-done.2
  67.5 2.2 collective-permute-start.3
  69.7 8.3 %collective-permute-done.2 = bf16[4,2,272,128]{3,2,1,0:T(8,128)(2,1)} collective-permute-done((bf16[4,2,272,128]{3,2,1,0:T(8,128)(2,1)}, bf16[4,2,272,128]{3,2,1,0:T(8,128)(2,1)}, u32[]{:S(2)}, u32[]{:S(2)}) %collective-permute-start.2) | collective-permute-done | bytes 557088 | tf_op jit(solution)/shard_map/ppermute | solution.py:106
  78.0 0.2 collective-permute-done.3
  78.2 1.3 maximum_bitcast_fusion.1
  79.5 2.5 fusion.18
  82.0 2.5 collective-permute-start.4
  84.5 2.5 %collective-permute-done.6 = bf16[8,2,272,128]{3,2,1,0:T(8,128)(2,1)S(1)} collective-permute-done((bf16[8,2,272,128]{3,2,1,0:T(8,128)(2,1)S(1)}, bf16[8,2,272,128]{3,2,1,0:T(8,128)(2,1)S(1)}, u32[]{:S(2)}, u32[]{:S(2)}) %collective-permute-start.6) | collective-permute-done | bytes 1114144 | tf_op jit(solution)/shard_map/ppermute | solution.py:106
  87.0 0.4 maximum_select_fusion.1
  87.3 1.0 collective-permute-start.7
  88.4 0.5 collective-permute-start.8
  88.9 40.4 %collective-permute-done.7 = bf16[2,8,2,272,128]{4,3,2,1,0:T(8,128)(2,1)S(1)} collective-permute-done((bf16[2,8,2,272,128]{4,3,2,1,0:T(8,128)(2,1)S(1)}, bf16[2,8,2,272,128]{4,3,2,1,0:T(8,128)(2,1)S(1)}, u32[]{:S(2)}, u32[]{:S(2)}) %collective-permute-start.7) | collective-permute-done | bytes 2228256 | tf_op jit(solution)/shard_map/ppermute | solution.py:106
  129.4 2.2 collective-permute-start.10
  131.7 0.1 collective-permute-start.9
  131.8 0.4 maximum_select_fusion
  132.2 20.3 %collective-permute-done.10 = bf16[1,8,2,272,128]{4,3,2,1,0:T(8,128)(2,1)S(1)} collective-permute-done((bf16[1,8,2,272,128]{4,3,2,1,0:T(8,128)(2,1)S(1)}, bf16[1,8,2,272,128]{4,3,2,1,0:T(8,128)(2,1)S(1)}, u32[]{:S(2)}, u32[]{:S(2)}) %collective-permute-start.10) | collective-permute-done | bytes 1114144 | tf_op jit(solution)/shard_map/ppermute | solution.py:106
  152.4 1.8 collective-permute-done.9
  154.2 0.2 maximum_bitcast_fusion
  154.4 4.1 %pad_maximum_fusion.1.refs_1_ = bf16[4,2,8,2,272,128]{5,4,3,2,1,0:T(8,128)(2,1)} fusion(bf16[1,2,8,2,272,128]{5,4,3,2,1,0:T(8,128)(2,1)S(1)} %bitcast.49, bf16[1,2,8,2,272,128]{5,4,3,2,1,0:T(8,128)(2,1)S(1)} %maximum_bitcast_fusion, bf16[1,2,8,2,272,128]{5,4,3,2,1,0:T(8,128)(2,1)S(1)} %bitcast.48, bf16[1,2,8,2,272,128]{5,4,3,2,1,0:T(8,128)(2,1)S(1)} %maximum_select_fusion), kind=kLoop, calls=%fused_computation.7 | loop fusion | flops 13369344 | bytes 17825792 | tf_op jit(solution)/shard_map/stack | solution.py:128
  158.5 10.1 %collective-permute-start.11 = (bf16[4,2,8,2,272,128]{5,4,3,2,1,0:T(8,128)(2,1)}, bf16[4,2,8,2,272,128]{5,4,3,2,1,0:T(8,128)(2,1)}, u32[]{:S(2)}, u32[]{:S(2)}) collective-permute-start(bf16[4,2,8,2,272,128]{5,4,3,2,1,0:T(8,128)(2,1)} %pad_maximum_fusion.1.refs_1_), channel_id=1, source_target_pairs={{0,1},{1,0},{2,3},{3,2},{4,5},{5,4},{6,7},{7,6},{8,9},{9,8},{10,11... | collective-permute-start | bytes 26738696 | tf_op jit(solution)/shard_map/ppermute | solution.py:106
  168.6 15.8 %collective-permute-done.4 = bf16[4,8,2,272,128]{4,3,2,1,0:T(8,128)(2,1)} collective-permute-done((bf16[4,8,2,272,128]{4,3,2,1,0:T(8,128)(2,1)S(1)}, bf16[4,8,2,272,128]{4,3,2,1,0:T(8,128)(2,1)}, u32[]{:S(2)}, u32[]{:S(2)}) %collective-permute-start.4) | collective-permute-done | bytes 4456480 | tf_op jit(solution)/shard_map/ppermute | solution.py:106
  184.4 7.9 %pad_maximum_fusion.refs_0_ = bf16[2,4,8,2,272,128]{5,4,3,2,1,0:T(8,128)(2,1)} fusion(bf16[1,4,8,2,272,128]{5,4,3,2,1,0:T(8,128)(2,1)} %bitcast.10, bf16[1,4,8,2,272,128]{5,4,3,2,1,0:T(8,128)(2,1)} %get-tuple-element.17), kind=kLoop, calls=%fused_computation.5 | loop fusion | flops 4456448 | bytes 17825792 | tf_op jit(solution)/shard_map/stack | solution.py:152
  192.3 4.1 %collective-permute-start.5 = (bf16[2,4,8,2,272,128]{5,4,3,2,1,0:T(8,128)(2,1)}, bf16[2,4,8,2,272,128]{5,4,3,2,1,0:T(8,128)(2,1)}, u32[]{:S(2)}, u32[]{:S(2)}) collective-permute-start(bf16[2,4,8,2,272,128]{5,4,3,2,1,0:T(8,128)(2,1)} %pad_maximum_fusion.refs_0_), channel_id=1, source_target_pairs={{0,1},{1,0},{2,3},{3,2},{4,5},{5,4},{6,7},{7,6},{8,9},{9,8},{10,11... | collective-permute-start | bytes 26738696 | tf_op jit(solution)/shard_map/ppermute | solution.py:106
  196.4 0.6 pad_add_fusion.rot_ref
  197.0 1.0 fusion.3
  198.1 0.2 copy.85
  198.2 0.6 gather_fusion.2
  198.8 0.1 copy.88
  198.9 0.6 gather_fusion.3
  199.5 0.1 copy.89
  199.6 0.1 gather.21
  199.8 0.5 and_select_fusion.rids_ref
  200.3 1.0 fusion.5
  201.3 0.5 copy.91
  201.8 0.7 reshape.466.lids_ref
  202.6 19.4 %shard_map.58.refs_0_ = f32[2048,1024]{1,0:T(8,128)} custom-call(s32[128]{0:T(128)} %reshape.466.lids_ref, s32[128]{0:T(128)} %and_select_fusion.rids_ref, s32[3]{0:T(128)} %pad_add_fusion.rot_ref, bf16[2,4,8,2,272,128]{5,4,3,2,1,0:T(8,128)(2,1)} %pad_maximum_fusion.refs_0_, bf16[4,2,8,2,272,128]{5,4,3,2,1,0:T(8,128)(2,1)} %pad_maximum_fusion.1.refs_1_), custom_call_target="tpu_custom_call" | custom-call | flops 2147483648 | bytes 26214400 | tf_op jit(solution)/shard_map/pallas_call | solution.py:89
  221.9 1.0 fusion.4
  222.9 0.2 copy.78
  223.1 0.6 gather_fusion
  223.7 0.1 copy.81
  223.8 0.6 gather_fusion.1
  224.4 0.1 copy.82
  224.5 0.1 gather.18
  224.6 0.6 and_select_fusion.1.rids_ref
  225.2 1.0 slice_convert_fusion.2
  226.2 0.5 copy.90
  226.7 0.7 reshape.464.lids_ref
  227.4 23.4 %shard_map.59 = f32[2048,1024]{1,0:T(8,128)} custom-call(s32[128]{0:T(128)} %reshape.464.lids_ref, s32[128]{0:T(128)} %and_select_fusion.1.rids_ref, s32[3]{0:T(128)} %pad_add_fusion.rot_ref, f32[2048,1024]{1,0:T(8,128)} %shard_map.58.refs_0_, bf16[2,4,8,2,272,128]{5,4,3,2,1,0:T(8,128)(2,1)} %collective-permute-done.5.refs_1_, ...), custom_call_target="tpu_custom_call", output_to_operand_aliasing={{}: (3, {})} | custom-call | flops 2147483648 | bytes 26214400 | tf_op jit(solution)/shard_map/pallas_call | solution.py:89
  (22 shorter events, 0.2 us)
Async XLA Ops:
  25.3 39.6 %collective-permute-start.1 = (bf16[8,2,272,128]{3,2,1,0:T(8,128)(2,1)S(1)}, bf16[8,2,272,128]{3,2,1,0:T(8,128)(2,1)S(1)}, u32[]{:S(2)}, u32[]{:S(2)}) collective-permute-start(bf16[8,2,272,128]{3,2,1,0:T(8,128)(2,1)S(1)} %bitcast.50), channel_id=1, source_target_pairs={{0,2},{2,4},{4,6},{6,0},{1,3},{3,5},{5,7},{7,1},{8,10},{10,12},{12... | collective-permute-start | bytes 3342344 | tf_op jit(solution)/shard_map/ppermute | solution.py:106
  26.9 39.3 %collective-permute-start = (bf16[8,2,272,128]{3,2,1,0:T(8,128)(2,1)S(1)}, bf16[8,2,272,128]{3,2,1,0:T(8,128)(2,1)S(1)}, u32[]{:S(2)}, u32[]{:S(2)}) collective-permute-start(bf16[8,2,272,128]{3,2,1,0:T(8,128)(2,1)S(1)} %bitcast.51), channel_id=1, source_target_pairs={{0,6},{2,0},{4,2},{6,4},{1,7},{3,1},{5,3},{7,5},{8,14},{10,8},{12,... | collective-permute-start | bytes 3342344 | tf_op jit(solution)/shard_map/ppermute | solution.py:106
  64.3 22.7 %collective-permute-start.6 = (bf16[8,2,272,128]{3,2,1,0:T(8,128)(2,1)S(1)}, bf16[8,2,272,128]{3,2,1,0:T(8,128)(2,1)S(1)}, u32[]{:S(2)}, u32[]{:S(2)}) collective-permute-start(bf16[8,2,272,128]{3,2,1,0:T(8,128)(2,1)S(1)} %bitcast.45), channel_id=1, source_target_pairs={{0,64},{64,0},{1,65},{65,1},{2,66},{66,2},{3,67},{67,3},{4,68},{68... | collective-permute-start | bytes 3342344 | tf_op jit(solution)/shard_map/ppermute | solution.py:106
  64.9 1.4 copy-start
  65.8 12.2 %collective-permute-start.2 = (bf16[4,2,272,128]{3,2,1,0:T(8,128)(2,1)}, bf16[4,2,272,128]{3,2,1,0:T(8,128)(2,1)}, u32[]{:S(2)}, u32[]{:S(2)}) collective-permute-start(bf16[4,2,272,128]{3,2,1,0:T(8,128)(2,1)} %slice.69), channel_id=1, source_target_pairs={{0,2},{2,4},{4,6},{6,0},{1,3},{3,5},{5,7},{7,1},{8,10},{10,12},{12... | collective-permute-start | bytes 1671176 | tf_op jit(solution)/shard_map/ppermute | solution.py:106
  66.3 1.2 copy-start.2
  67.5 10.7 %collective-permute-start.3 = (bf16[4,2,272,128]{3,2,1,0:T(8,128)(2,1)}, bf16[4,2,272,128]{3,2,1,0:T(8,128)(2,1)}, u32[]{:S(2)}, u32[]{:S(2)}) collective-permute-start(bf16[4,2,272,128]{3,2,1,0:T(8,128)(2,1)} %slice.70), channel_id=1, source_target_pairs={{0,6},{2,0},{4,2},{6,4},{1,7},{3,1},{5,3},{7,5},{8,14},{10,8},{12,... | collective-permute-start | bytes 1671176 | tf_op jit(solution)/shard_map/ppermute | solution.py:106
  69.7 9.8 %copy-start.1 = (bf16[8,2,272,128]{3,2,1,0:T(8,128)(2,1)S(1)}, bf16[8,2,272,128]{3,2,1,0:T(8,128)(2,1)}, u32[]{:S(2)}) copy-start(bf16[8,2,272,128]{3,2,1,0:T(8,128)(2,1)} %copy-done) | copy-start | bytes 3342340
  69.7 9.8 %copy-start.3 = (bf16[8,2,272,128]{3,2,1,0:T(8,128)(2,1)S(1)}, bf16[8,2,272,128]{3,2,1,0:T(8,128)(2,1)}, u32[]{:S(2)}) copy-start(bf16[8,2,272,128]{3,2,1,0:T(8,128)(2,1)} %copy-done.2) | copy-start | bytes 3342340
  82.0 102.4 %collective-permute-start.4 = (bf16[4,8,2,272,128]{4,3,2,1,0:T(8,128)(2,1)S(1)}, bf16[4,8,2,272,128]{4,3,2,1,0:T(8,128)(2,1)}, u32[]{:S(2)}, u32[]{:S(2)}) collective-permute-start(bf16[4,8,2,272,128]{4,3,2,1,0:T(8,128)(2,1)S(1)} %get-tuple-element.18), channel_id=1, source_target_pairs={{0,8},{8,0},{1,9},{9,1},{2,10},{10,2},{3,11},{11,3},{4,12},{12,4},... | collective-permute-start | bytes 13369352 | tf_op jit(solution)/shard_map/ppermute | solution.py:106
  87.3 42.0 %collective-permute-start.7 = (bf16[2,8,2,272,128]{4,3,2,1,0:T(8,128)(2,1)S(1)}, bf16[2,8,2,272,128]{4,3,2,1,0:T(8,128)(2,1)S(1)}, u32[]{:S(2)}, u32[]{:S(2)}) collective-permute-start(bf16[2,8,2,272,128]{4,3,2,1,0:T(8,128)(2,1)S(1)} %maximum_select_fusion.1), channel_id=1, source_target_pairs={{0,48},{16,0},{32,16},{48,32},{1,49},{17,1},{33,17},{49,33},{2,50}... | collective-permute-start | bytes 6684680 | tf_op jit(solution)/shard_map/ppermute | solution.py:106
  88.4 43.3 %collective-permute-start.8 = (bf16[2,8,2,272,128]{4,3,2,1,0:T(8,128)(2,1)S(1)}, bf16[2,8,2,272,128]{4,3,2,1,0:T(8,128)(2,1)S(1)}, u32[]{:S(2)}, u32[]{:S(2)}) collective-permute-start(bf16[2,8,2,272,128]{4,3,2,1,0:T(8,128)(2,1)S(1)} %maximum_select_fusion.1), channel_id=1, source_target_pairs={{0,16},{16,32},{32,48},{48,0},{1,17},{17,33},{33,49},{49,1},{2,18}... | collective-permute-start | bytes 6684680 | tf_op jit(solution)/shard_map/ppermute | solution.py:106
  129.4 23.0 %collective-permute-start.10 = (bf16[1,8,2,272,128]{4,3,2,1,0:T(8,128)(2,1)S(1)}, bf16[1,8,2,272,128]{4,3,2,1,0:T(8,128)(2,1)S(1)}, u32[]{:S(2)}, u32[]{:S(2)}) collective-permute-start(bf16[1,8,2,272,128]{4,3,2,1,0:T(8,128)(2,1)S(1)} %slice.73), channel_id=1, source_target_pairs={{0,48},{16,0},{32,16},{48,32},{1,49},{17,1},{33,17},{49,33},{2,50}... | collective-permute-start | bytes 3342344 | tf_op jit(solution)/shard_map/ppermute | solution.py:106
  131.7 22.5 %collective-permute-start.9 = (bf16[1,8,2,272,128]{4,3,2,1,0:T(8,128)(2,1)S(1)}, bf16[1,8,2,272,128]{4,3,2,1,0:T(8,128)(2,1)S(1)}, u32[]{:S(2)}, u32[]{:S(2)}) collective-permute-start(bf16[1,8,2,272,128]{4,3,2,1,0:T(8,128)(2,1)S(1)} %slice.72), channel_id=1, source_target_pairs={{0,16},{16,32},{32,48},{48,0},{1,17},{17,33},{33,49},{49,1},{2,18}... | collective-permute-start | bytes 3342344 | tf_op jit(solution)/shard_map/ppermute | solution.py:106
  158.5 63.4 %collective-permute-start.11 = (bf16[4,2,8,2,272,128]{5,4,3,2,1,0:T(8,128)(2,1)}, bf16[4,2,8,2,272,128]{5,4,3,2,1,0:T(8,128)(2,1)}, u32[]{:S(2)}, u32[]{:S(2)}) collective-permute-start(bf16[4,2,8,2,272,128]{5,4,3,2,1,0:T(8,128)(2,1)} %pad_maximum_fusion.1.refs_1_), channel_id=1, source_target_pairs={{0,1},{1,0},{2,3},{3,2},{4,5},{5,4},{6,7},{7,6},{8,9},{9,8},{10,11... | collective-permute-start | bytes 26738696 | tf_op jit(solution)/shard_map/ppermute | solution.py:106
  192.3 32.9 %collective-permute-start.5 = (bf16[2,4,8,2,272,128]{5,4,3,2,1,0:T(8,128)(2,1)}, bf16[2,4,8,2,272,128]{5,4,3,2,1,0:T(8,128)(2,1)}, u32[]{:S(2)}, u32[]{:S(2)}) collective-permute-start(bf16[2,4,8,2,272,128]{5,4,3,2,1,0:T(8,128)(2,1)} %pad_maximum_fusion.refs_0_), channel_id=1, source_target_pairs={{0,1},{1,0},{2,3},{3,2},{4,5},{5,4},{6,7},{7,6},{8,9},{9,8},{10,11... | collective-permute-start | bytes 26738696 | tf_op jit(solution)/shard_map/ppermute | solution.py:106

commit v6 on v5

--- a/solution.py
+++ b/solution.py
@@ -31,13 +31,14 @@
         else:
             out_ref[...] = jnp.zeros_like(out_ref)
 
-    n_z = left_ref.shape[1]
+    n_z = left_ref.shape[0]
+    n_xhi = left_ref.shape[1]
 
     def body(k, carry):
         b = r * group + k
-        x_rel = k // n_z
-        z_rel = lax.rem(k, n_z)
-        chip = lax.rem(rot_ref[1] + x_rel, 2) * n_z + lax.rem(rot_ref[2] + z_rel, n_z)
+        z_rel = k // n_xhi
+        x_abs = lax.rem(k, n_xhi)
+        chip = x_abs * n_z + lax.rem(rot_ref[2] + z_rel, n_z)
         for i in range(slots):
             li = lids_ref[b * slots + i]
             for j in range(slots):
@@ -46,7 +47,7 @@
                 @pl.when((li >= 0) & (rj >= 0))
                 def _():
                     prod = lax.dot_general(
-                        left_ref[x_rel, z_rel, i, :rows, :],
+                        left_ref[z_rel, x_abs, i, :rows, :],
                         right_ref[chip, j, :rows, :],
                         (((0,), (0,)), ((), ())),
                         preferred_element_type=jnp.float32,
@@ -61,7 +62,7 @@
 
 
 def accumulate(prev, left, left_ids, right, right_ids, rot, rows, per_row, per_col):
-    n_xhi, n_z, n_row, slots, band_rows, width = left.shape
+    n_z, n_row, n_xhi, slots, band_rows, width = left.shape
     n_chip = n_xhi * n_z
     n_y = right.shape[0]
     out_shape = (per_row * width, per_col * width)
@@ -70,7 +71,7 @@
         return (lax.rem(lax.rem(r, n_y) - rot[0] + n_y, n_y), r // n_y, 0, 0, 0, 0)
 
     in_specs = [
-        pl.BlockSpec((n_xhi, n_z, None, slots, band_rows, width), lambda r, lids, rids, rot: (0, 0, r, 0, 0, 0)),
+        pl.BlockSpec((n_z, None, n_xhi, slots, band_rows, width), lambda r, lids, rids, rot: (0, r, 0, 0, 0, 0)),
         pl.BlockSpec((None, None, n_chip, slots, band_rows, width), right_map),
     ]
     operands = [left, right]
@@ -148,8 +149,11 @@
     band_rows = rows + BAND
 
     left = lax.all_to_all(tagged, ("xlo", "y"), split_axis=1, concat_axis=0, tiled=True)
-    left = z_ring(left[:, 0])
-    left_own = jnp.stack([left, shift(left, "xhi", 1)])
+    left = left[:, 0]
+    first = lax.axis_index("xhi") == 0
+    other = shift(left, "xhi", 1)
+    left = jnp.where(first, jnp.stack([left, other], axis=1), jnp.stack([other, left], axis=1))
+    left_own = z_ring(left)
     right = lax.all_to_all(tagged, ("xhi", "z"), split_axis=1, concat_axis=1, tiled=True)
     right_own = ring_gather(right[0])
     left_other = shift(left_own, "core", 1)
@@ -163,11 +167,11 @@
     me_xhi = lax.axis_index("xhi")
     absolute_y = (jnp.arange(n_y, dtype=jnp.int32) - me_y) % n_y
     k_rel = jnp.arange(n_xhi * n_z, dtype=jnp.int32)
-    chip_of = ((me_xhi + k_rel // n_z) % n_xhi) * n_z + (me_z + k_rel % n_z) % n_z
+    chip_of = (k_rel % n_xhi) * n_z + (me_z + k_rel // n_xhi) % n_z
 
     def part(prev, left_half, right_half):
         left_ids = left_half[:, :, :, :, rows, 0].astype(jnp.int32)
-        left_ids = jnp.transpose(left_ids, (2, 0, 1, 3))
+        left_ids = jnp.transpose(left_ids, (1, 0, 2, 3))
         right_ids = right_half[:, :, :, :, rows, 0].astype(jnp.int32) - me_core * per_col
         right_ids = jnp.transpose(right_ids[absolute_y], (1, 0, 2, 3)).reshape(row_devices, chips, slots)
         right_ids = right_ids[:, chip_of]

time: 254 us -> 231 us (0.909)
  blocking collectives: 56.2 us -> 25 us
  waiting for transfers between devices: 89.3 us -> 99.2 us
    all_to_all x1 -> x0, blocking collectives: 21 us -> none  [local(): lax.all_to_all(tagged, ('xlo', 'y'), split_axis=1, concat_axis=0, tiled=T...]
    all_to_all x0 -> x1, waiting for transfers between devices: none -> 10.4 us  [local(): lax.all_to_all(tagged, ('xlo', 'y'), split_axis=1, concat_axis=0, tiled=T...]
    another operation x2 -> x0, other arithmetic: 10.4 us -> none  [local(): left_own = jnp.stack([left, shift(left, 'xhi', 1)])]
    all_to_all x1, blocking collectives: 35.2 us -> 25 us  [local(): lax.all_to_all(tagged, ('xhi', 'z'), split_axis=1, concat_axis=1, tiled=T...]
    ppermute x12, starting transfers between devices: 27.6 us -> 22.6 us  [shift(): return lax.ppermute(x, axis, [(i, (i + step) % n) for i in range(n)])]
    select_n x2, other arithmetic: 0.73 us -> 5.34 us  [ring_gather(): jnp.where(first, jnp.stack([piece, other]), jnp.stack([other, piece]))]
    all_to_all x0 -> x1, starting transfers between devices: none -> 4.31 us  [local(): lax.all_to_all(tagged, ('xlo', 'y'), split_axis=1, concat_axis=0, tiled=T...]
    another operation x1 -> x2, other arithmetic: 1.32 us -> 4.41 us  [z_ring(): return jnp.stack([piece, from_above, far, from_below])]
  transfers between devices with their start and end apart: 12 -> 13, of which waited for: 7 -> 7; matrix products, arithmetic and copies ran while one was open for 11% -> 12% of each run, Pallas kernels for 8% -> 8%
where the time goes in v6:
time: 231 us; the launch traced here: 230 us
  waiting for transfers between devices  99.2 us (43%)
  Pallas kernels  42.5 us (18%)
  other arithmetic  27.6 us (12%)
  starting transfers between devices  26.9 us (12%)
  blocking collectives  25 us (11%)
  local copies, waits for them, and re-layouts  8.33 us (4%)
    ppermute x12, waiting for transfers between devices, shift(): return lax.ppermute(x, axis, [(i, (i + step) % n) for i in range(n)])  88.8 us
    pallas_call x2, Pallas kernels, accumulate(): pl.pallas_call(functools.partial(gram_kernel, slots, rows, width, n_chip,...  42.5 us
    all_to_all x1, blocking collectives, local(): lax.all_to_all(tagged, ('xhi', 'z'), split_axis=1, concat_axis=1, tiled=T...  25 us
    ppermute x12, starting transfers between devices, shift(): return lax.ppermute(x, axis, [(i, (i + step) % n) for i in range(n)])  22.6 us
    all_to_all x1, waiting for transfers between devices, local(): lax.all_to_all(tagged, ('xlo', 'y'), split_axis=1, concat_axis=0, tiled=T...  10.4 us
    another operation x2, other arithmetic, ring_gather(): return jnp.stack([bundle, from_above, far, from_below])  6.58 us
    select_n x2, other arithmetic, ring_gather(): jnp.where(first, jnp.stack([piece, other]), jnp.stack([other, piece]))  5.34 us
  transfers between devices with their start and end apart: 13, of which 7 were waited for; matrix products, arithmetic and copies ran while one was open for 12% of the time, Pallas kernels for 8%

profile of v6, /device:TPU:1, one launch (start us, length us, event | category | flops | bytes accessed | tf_op | source)
XLA Modules:
  0.0 229.6 jit_solution(7084097159947317631)
XLA Ops:
  0.0 0.7 fusion.4
  0.7 0.7 fusion.7
  1.4 0.1 copy.76
  1.5 0.8 select_reduce_fusion
  2.3 0.1 broadcast_multiply_fusion
  2.4 1.7 multiply_convert_fusion
  4.1 0.1 broadcast.396
  4.2 1.1 fusion.1
  5.3 25.0 %all_to_all.17 = bf16[1,8,2,272,128]{4,3,2,0,1:T(8,128)(2,1)S(1)} all-to-all(bf16[1,8,2,272,128]{4,3,2,0,1:T(8,128)(2,1)} %fusion.1), channel_id=1, replica_groups=mesh['xlo'=2,'y'=4,'xhi'=2,'z'=4,'core'=2] {'xhi','z'}, dimensions={1} | all-to-all | bytes 2228224 | tf_op jit(solution)/shard_map/all_to_all | solution.py:157
  30.2 4.3 %all-to-all-start = ((bf16[1,8,2,272,128]{4,3,2,0,1:T(8,128)(2,1)}), bf16[1,8,2,272,128]{4,3,2,0,1:T(8,128)(2,1)S(1)}, u32[]{:S(2)}, u32[]{:S(2)}) async-start(bf16[1,8,2,272,128]{4,3,2,0,1:T(8,128)(2,1)} %fusion.1), calls=%async_computation | async-start | bytes 2228224 | tf_op jit(solution)/shard_map/all_to_all | solution.py:151
  34.6 1.5 collective-permute-start.6
  36.0 10.4 %all-to-all-done = bf16[1,8,2,272,128]{4,3,2,0,1:T(8,128)(2,1)S(1)} async-done(((bf16[1,8,2,272,128]{4,3,2,0,1:T(8,128)(2,1)}), bf16[1,8,2,272,128]{4,3,2,0,1:T(8,128)(2,1)S(1)}, u32[]{:S(2)}, u32[]{:S(2)}) %all-to-all-start) | async-done | bytes 1114144 | tf_op jit(solution)/shard_map/all_to_all | solution.py:151
  46.4 1.0 collective-permute-start
  47.5 22.9 %collective-permute-done.6 = bf16[8,2,272,128]{3,2,1,0:T(8,128)(2,1)} collective-permute-done((bf16[8,2,272,128]{3,2,1,0:T(8,128)(2,1)S(1)}, bf16[8,2,272,128]{3,2,1,0:T(8,128)(2,1)}, u32[]{:S(2)}, u32[]{:S(2)}) %collective-permute-start.6) | collective-permute-done | bytes 1114144 | tf_op jit(solution)/shard_map/ppermute | solution.py:107
  70.4 3.4 %maximum_select_fusion.3 = bf16[2,8,2,272,128]{4,3,2,1,0:T(8,128)(2,1)} fusion(bf16[1,8,2,272,128]{4,3,2,1,0:T(8,128)(2,1)} %bitcast.18, bf16[1,8,2,272,128]{4,3,2,1,0:T(8,128)(2,1)S(1)} %bitcast.49, pred[]{:T(512)S(6)} %eq.36), kind=kLoop, calls=%fused_computation.11 | loop fusion | flops 3342336 | bytes 4456449 | tf_op jit(solution)/shard_map/jit(_where)/select_n | solution.py:123
  73.8 1.1 collective-permute-start.8
  74.9 1.6 collective-permute-start.7
  76.4 17.5 %collective-permute-done = bf16[8,2,272,128]{3,2,1,0:T(8,128)(2,1)S(1)} collective-permute-done((bf16[8,2,272,128]{3,2,1,0:T(8,128)(2,1)S(1)}, bf16[8,2,272,128]{3,2,1,0:T(8,128)(2,1)S(1)}, u32[]{:S(2)}, u32[]{:S(2)}) %collective-permute-start) | collective-permute-done | bytes 1114144 | tf_op jit(solution)/shard_map/ppermute | solution.py:107
  94.0 0.2 maximum_select_fusion.1
  94.2 2.2 collective-permute-start.2
  96.4 0.7 collective-permute-start.1
  97.1 21.7 %collective-permute-done.8 = bf16[2,8,2,272,128]{4,3,2,1,0:T(8,128)(2,1)} collective-permute-done((bf16[2,8,2,272,128]{4,3,2,1,0:T(8,128)(2,1)}, bf16[2,8,2,272,128]{4,3,2,1,0:T(8,128)(2,1)}, u32[]{:S(2)}, u32[]{:S(2)}) %collective-permute-start.8) | collective-permute-done | bytes 2228256 | tf_op jit(solution)/shard_map/ppermute | solution.py:107
  118.7 1.3 slice.72
  120.1 1.3 slice.73
  121.5 2.7 %collective-permute-start.10 = (bf16[1,8,2,272,128]{4,3,2,1,0:T(8,128)(2,1)S(1)}, bf16[1,8,2,272,128]{4,3,2,1,0:T(8,128)(2,1)S(1)}, u32[]{:S(2)}, u32[]{:S(2)}) collective-permute-start(bf16[1,8,2,272,128]{4,3,2,1,0:T(8,128)(2,1)S(1)} %slice.73), channel_id=1, source_target_pairs={{0,48},{16,0},{32,16},{48,32},{1,49},{17,1},{33,17},{49,33},{2,50}... | collective-permute-start | bytes 3342344 | tf_op jit(solution)/shard_map/ppermute | solution.py:107
  124.2 18.2 %collective-permute-done.2 = bf16[8,2,2,272,128]{4,3,2,1,0:T(8,128)(2,1)S(1)} collective-permute-done((bf16[8,2,2,272,128]{4,3,2,1,0:T(8,128)(2,1)S(1)}, bf16[8,2,2,272,128]{4,3,2,1,0:T(8,128)(2,1)S(1)}, u32[]{:S(2)}, u32[]{:S(2)}) %collective-permute-start.2) | collective-permute-done | bytes 2228256 | tf_op jit(solution)/shard_map/ppermute | solution.py:107
  142.5 1.7 collective-permute-start.3
  144.3 1.1 collective-permute-start.4
  145.4 2.0 maximum_select_fusion.2
  147.4 0.2 maximum_bitcast_fusion.1
  147.6 6.4 %pad_maximum_fusion.1.refs_1_ = bf16[4,2,8,2,272,128]{5,4,3,2,1,0:T(8,128)(2,1)} fusion(bf16[1,2,8,2,272,128]{5,4,3,2,1,0:T(8,128)(2,1)} %bitcast.21, bf16[1,2,8,2,272,128]{5,4,3,2,1,0:T(8,128)(2,1)S(1)} %maximum_bitcast_fusion.1, bf16[1,2,8,2,272,128]{5,4,3,2,1,0:T(8,128)(2,1)} %bitcast.19, bf16[1,2,8,2,272,128]{5,4,3,2,1,0:T(8,128)(2,1)S(1)} %maximum_select_fusion.2), kind=kLoop, calls=%fused_computation.5 | loop fusion | flops 13369344 | bytes 17825792 | tf_op jit(solution)/shard_map/stack | solution.py:129
  154.0 4.5 %collective-permute-start.11 = (bf16[4,2,8,2,272,128]{5,4,3,2,1,0:T(8,128)(2,1)}, bf16[4,2,8,2,272,128]{5,4,3,2,1,0:T(8,128)(2,1)}, u32[]{:S(2)}, u32[]{:S(2)}) collective-permute-start(bf16[4,2,8,2,272,128]{5,4,3,2,1,0:T(8,128)(2,1)} %pad_maximum_fusion.1.refs_1_), channel_id=1, source_target_pairs={{0,1},{1,0},{2,3},{3,2},{4,5},{5,4},{6,7},{7,6},{8,9},{9,8},{10,11... | collective-permute-start | bytes 26738696 | tf_op jit(solution)/shard_map/ppermute | solution.py:107
  158.5 7.4 %collective-permute-done.3 = bf16[4,2,2,272,128]{4,3,2,1,0:T(8,128)(2,1)S(1)} collective-permute-done((bf16[4,2,2,272,128]{4,3,2,1,0:T(8,128)(2,1)S(1)}, bf16[4,2,2,272,128]{4,3,2,1,0:T(8,128)(2,1)S(1)}, u32[]{:S(2)}, u32[]{:S(2)}) %collective-permute-start.3) | collective-permute-done | bytes 1114144 | tf_op jit(solution)/shard_map/ppermute | solution.py:107
  165.9 1.1 collective-permute-done.4
  166.9 0.2 maximum_bitcast_fusion
  167.1 4.2 %pad_maximum_fusion.refs_0_ = bf16[4,8,2,2,272,128]{5,4,3,2,1,0:T(8,128)(2,1)} fusion(bf16[1,8,2,2,272,128]{5,4,3,2,1,0:T(8,128)(2,1)S(1)} %bitcast.51, bf16[1,8,2,2,272,128]{5,4,3,2,1,0:T(8,128)(2,1)S(1)} %maximum_bitcast_fusion, bf16[1,8,2,2,272,128]{5,4,3,2,1,0:T(8,128)(2,1)S(1)} %bitcast.52, bf16[1,8,1,2,272,128]{5,4,3,1,2,0:T(8,128)(2,1)S(1)} %bitcast.54, ...), kind=kLoop, calls=%fused_computation.4 | loop fusion | flops 38993920 | bytes 17825792 | tf_op jit(solution)/shard_map/stack | solution.py:117
  171.4 4.4 %collective-permute-start.5 = (bf16[4,8,2,2,272,128]{5,4,3,2,1,0:T(8,128)(2,1)}, bf16[4,8,2,2,272,128]{5,4,3,2,1,0:T(8,128)(2,1)}, u32[]{:S(2)}, u32[]{:S(2)}) collective-permute-start(bf16[4,8,2,2,272,128]{5,4,3,2,1,0:T(8,128)(2,1)} %pad_maximum_fusion.refs_0_), channel_id=1, source_target_pairs={{0,1},{1,0},{2,3},{3,2},{4,5},{5,4},{6,7},{7,6},{8,9},{9,8},{10,11... | collective-permute-start | bytes 26738696 | tf_op jit(solution)/shard_map/ppermute | solution.py:107
  175.8 0.7 pad_add_fusion.rot_ref
  176.4 1.0 slice_convert_fusion.1
  177.5 0.2 copy.87
  177.6 0.1 copy.88
  177.8 0.7 reshape.487.lids_ref
  178.5 1.0 fusion.2
  179.5 0.2 copy.89
  179.7 0.6 gather_fusion.2
  180.3 0.1 copy.92
  180.4 0.6 gather_fusion.3
  180.9 0.1 copy.93
  181.1 0.1 gather.21
  181.2 0.6 and_select_fusion.rids_ref
  181.8 19.5 %shard_map.58.refs_0_ = f32[2048,1024]{1,0:T(8,128)} custom-call(s32[128]{0:T(128)} %reshape.487.lids_ref, s32[128]{0:T(128)} %and_select_fusion.rids_ref, s32[3]{0:T(128)} %pad_add_fusion.rot_ref, bf16[4,8,2,2,272,128]{5,4,3,2,1,0:T(8,128)(2,1)} %pad_maximum_fusion.refs_0_, bf16[4,2,8,2,272,128]{5,4,3,2,1,0:T(8,128)(2,1)} %pad_maximum_fusion.1.refs_1_), custom_call_target="tpu_custom_call" | custom-call | flops 2147483648 | bytes 26214400 | tf_op jit(solution)/shard_map/pallas_call | solution.py:90
  201.3 1.0 fusion.3
  202.3 0.2 copy.82
  202.5 0.6 gather_fusion
  203.1 0.1 copy.85
  203.2 0.6 gather_fusion.1
  203.8 0.1 copy.86
  203.9 0.1 gather.18
  204.0 0.6 and_select_fusion.1.rids_ref
  204.6 1.0 slice_convert_fusion.3
  205.6 0.2 copy.78
  205.8 0.1 copy.79
  205.9 0.7 reshape.485.lids_ref
  206.6 23.0 %shard_map.59 = f32[2048,1024]{1,0:T(8,128)} custom-call(s32[128]{0:T(128)} %reshape.485.lids_ref, s32[128]{0:T(128)} %and_select_fusion.1.rids_ref, s32[3]{0:T(128)} %pad_add_fusion.rot_ref, f32[2048,1024]{1,0:T(8,128)} %shard_map.58.refs_0_, bf16[4,8,2,2,272,128]{5,4,3,2,1,0:T(8,128)(2,1)} %collective-permute-done.5.refs_1_, ...), custom_call_target="tpu_custom_call", output_to_operand_aliasing={{}: (3, {})} | custom-call | flops 2147483648 | bytes 26214400 | tf_op jit(solution)/shard_map/pallas_call | solution.py:90
  (17 shorter events, 0.3 us)
Async XLA Ops:
  30.2 16.2 %all-to-all-start = ((bf16[1,8,2,272,128]{4,3,2,0,1:T(8,128)(2,1)}), bf16[1,8,2,272,128]{4,3,2,0,1:T(8,128)(2,1)S(1)}, u32[]{:S(2)}, u32[]{:S(2)}) async-start(bf16[1,8,2,272,128]{4,3,2,0,1:T(8,128)(2,1)} %fusion.1), calls=%async_computation | async-start | bytes 2228224 | tf_op jit(solution)/shard_map/all_to_all | solution.py:151
  34.6 35.9 %collective-permute-start.6 = (bf16[8,2,272,128]{3,2,1,0:T(8,128)(2,1)S(1)}, bf16[8,2,272,128]{3,2,1,0:T(8,128)(2,1)}, u32[]{:S(2)}, u32[]{:S(2)}) collective-permute-start(bf16[8,2,272,128]{3,2,1,0:T(8,128)(2,1)S(1)} %bitcast.48), channel_id=1, source_target_pairs={{0,64},{64,0},{1,65},{65,1},{2,66},{66,2},{3,67},{67,3},{4,68},{68... | collective-permute-start | bytes 3342344 | tf_op jit(solution)/shard_map/ppermute | solution.py:107
  46.4 47.5 %collective-permute-start = (bf16[8,2,272,128]{3,2,1,0:T(8,128)(2,1)S(1)}, bf16[8,2,272,128]{3,2,1,0:T(8,128)(2,1)S(1)}, u32[]{:S(2)}, u32[]{:S(2)}) collective-permute-start(bf16[8,2,272,128]{3,2,1,0:T(8,128)(2,1)S(1)} %bitcast.45), channel_id=1, source_target_pairs={{0,8},{8,0},{1,9},{9,1},{2,10},{10,2},{3,11},{11,3},{4,12},{12,4},... | collective-permute-start | bytes 3342344 | tf_op jit(solution)/shard_map/ppermute | solution.py:107
  73.8 45.0 %collective-permute-start.8 = (bf16[2,8,2,272,128]{4,3,2,1,0:T(8,128)(2,1)}, bf16[2,8,2,272,128]{4,3,2,1,0:T(8,128)(2,1)}, u32[]{:S(2)}, u32[]{:S(2)}) collective-permute-start(bf16[2,8,2,272,128]{4,3,2,1,0:T(8,128)(2,1)} %maximum_select_fusion.3), channel_id=1, source_target_pairs={{0,16},{16,32},{32,48},{48,0},{1,17},{17,33},{33,49},{49,1},{2,18}... | collective-permute-start | bytes 6684680 | tf_op jit(solution)/shard_map/ppermute | solution.py:107
  74.9 45.3 %collective-permute-start.7 = (bf16[2,8,2,272,128]{4,3,2,1,0:T(8,128)(2,1)}, bf16[2,8,2,272,128]{4,3,2,1,0:T(8,128)(2,1)}, u32[]{:S(2)}, u32[]{:S(2)}) collective-permute-start(bf16[2,8,2,272,128]{4,3,2,1,0:T(8,128)(2,1)} %maximum_select_fusion.3), channel_id=1, source_target_pairs={{0,48},{16,0},{32,16},{48,32},{1,49},{17,1},{33,17},{49,33},{2,50}... | collective-permute-start | bytes 6684680 | tf_op jit(solution)/shard_map/ppermute | solution.py:107
  94.2 48.2 %collective-permute-start.2 = (bf16[8,2,2,272,128]{4,3,2,1,0:T(8,128)(2,1)S(1)}, bf16[8,2,2,272,128]{4,3,2,1,0:T(8,128)(2,1)S(1)}, u32[]{:S(2)}, u32[]{:S(2)}) collective-permute-start(bf16[8,2,2,272,128]{4,3,2,1,0:T(8,128)(2,1)S(1)} %maximum_select_fusion.1), channel_id=1, source_target_pairs={{0,2},{2,4},{4,6},{6,0},{1,3},{3,5},{5,7},{7,1},{8,10},{10,12},{12... | collective-permute-start | bytes 6684680 | tf_op jit(solution)/shard_map/ppermute | solution.py:107
  96.4 47.8 %collective-permute-start.1 = (bf16[8,2,2,272,128]{4,3,2,1,0:T(8,128)(2,1)S(1)}, bf16[8,2,2,272,128]{4,3,2,1,0:T(8,128)(2,1)S(1)}, u32[]{:S(2)}, u32[]{:S(2)}) collective-permute-start(bf16[8,2,2,272,128]{4,3,2,1,0:T(8,128)(2,1)S(1)} %maximum_select_fusion.1), channel_id=1, source_target_pairs={{0,6},{2,0},{4,2},{6,4},{1,7},{3,1},{5,3},{7,5},{8,14},{10,8},{12,... | collective-permute-start | bytes 6684680 | tf_op jit(solution)/shard_map/ppermute | solution.py:107
  120.1 27.3 %collective-permute-start.9 = (bf16[1,8,2,272,128]{4,3,2,1,0:T(8,128)(2,1)S(1)}, bf16[1,8,2,272,128]{4,3,2,1,0:T(8,128)(2,1)S(1)}, u32[]{:S(2)}, u32[]{:S(2)}) collective-permute-start(bf16[1,8,2,272,128]{4,3,2,1,0:T(8,128)(2,1)S(1)} %slice.72), channel_id=1, source_target_pairs={{0,16},{16,32},{32,48},{48,0},{1,17},{17,33},{33,49},{49,1},{2,18}... | collective-permute-start | bytes 3342344 | tf_op jit(solution)/shard_map/ppermute | solution.py:107
  121.5 25.9 %collective-permute-start.10 = (bf16[1,8,2,272,128]{4,3,2,1,0:T(8,128)(2,1)S(1)}, bf16[1,8,2,272,128]{4,3,2,1,0:T(8,128)(2,1)S(1)}, u32[]{:S(2)}, u32[]{:S(2)}) collective-permute-start(bf16[1,8,2,272,128]{4,3,2,1,0:T(8,128)(2,1)S(1)} %slice.73), channel_id=1, source_target_pairs={{0,48},{16,0},{32,16},{48,32},{1,49},{17,1},{33,17},{49,33},{2,50}... | collective-permute-start | bytes 3342344 | tf_op jit(solution)/shard_map/ppermute | solution.py:107
  142.5 23.4 %collective-permute-start.3 = (bf16[4,2,2,272,128]{4,3,2,1,0:T(8,128)(2,1)S(1)}, bf16[4,2,2,272,128]{4,3,2,1,0:T(8,128)(2,1)S(1)}, u32[]{:S(2)}, u32[]{:S(2)}) collective-permute-start(bf16[4,2,2,272,128]{4,3,2,1,0:T(8,128)(2,1)S(1)} %slice.69), channel_id=1, source_target_pairs={{0,2},{2,4},{4,6},{6,0},{1,3},{3,5},{5,7},{7,1},{8,10},{10,12},{12... | collective-permute-start | bytes 3342344 | tf_op jit(solution)/shard_map/ppermute | solution.py:107
  144.3 22.7 %collective-permute-start.4 = (bf16[4,2,2,272,128]{4,3,2,1,0:T(8,128)(2,1)S(1)}, bf16[4,2,2,272,128]{4,3,2,1,0:T(8,128)(2,1)S(1)}, u32[]{:S(2)}, u32[]{:S(2)}) collective-permute-start(bf16[4,2,2,272,128]{4,3,2,1,0:T(8,128)(2,1)S(1)} %slice.70), channel_id=1, source_target_pairs={{0,6},{2,0},{4,2},{6,4},{1,7},{3,1},{5,3},{7,5},{8,14},{10,8},{12,... | collective-permute-start | bytes 3342344 | tf_op jit(solution)/shard_map/ppermute | solution.py:107
  154.0 47.3 %collective-permute-start.11 = (bf16[4,2,8,2,272,128]{5,4,3,2,1,0:T(8,128)(2,1)}, bf16[4,2,8,2,272,128]{5,4,3,2,1,0:T(8,128)(2,1)}, u32[]{:S(2)}, u32[]{:S(2)}) collective-permute-start(bf16[4,2,8,2,272,128]{5,4,3,2,1,0:T(8,128)(2,1)} %pad_maximum_fusion.1.refs_1_), channel_id=1, source_target_pairs={{0,1},{1,0},{2,3},{3,2},{4,5},{5,4},{6,7},{7,6},{8,9},{9,8},{10,11... | collective-permute-start | bytes 26738696 | tf_op jit(solution)/shard_map/ppermute | solution.py:107
  171.4 33.3 %collective-permute-start.5 = (bf16[4,8,2,2,272,128]{5,4,3,2,1,0:T(8,128)(2,1)}, bf16[4,8,2,2,272,128]{5,4,3,2,1,0:T(8,128)(2,1)}, u32[]{:S(2)}, u32[]{:S(2)}) collective-permute-start(bf16[4,8,2,2,272,128]{5,4,3,2,1,0:T(8,128)(2,1)} %pad_maximum_fusion.refs_0_), channel_id=1, source_target_pairs={{0,1},{1,0},{2,3},{3,2},{4,5},{5,4},{6,7},{7,6},{8,9},{9,8},{10,11... | collective-permute-start | bytes 26738696 | tf_op jit(solution)/shard_map/ppermute | solution.py:107

commit v7 on v6

--- a/solution.py
+++ b/solution.py
@@ -39,22 +39,26 @@
         z_rel = k // n_xhi
         x_abs = lax.rem(k, n_xhi)
         chip = x_abs * n_z + lax.rem(rot_ref[2] + z_rel, n_z)
-        for i in range(slots):
-            li = lids_ref[b * slots + i]
-            for j in range(slots):
-                rj = rids_ref[b * slots + j]
-
-                @pl.when((li >= 0) & (rj >= 0))
-                def _():
-                    prod = lax.dot_general(
-                        left_ref[z_rel, x_abs, i, :rows, :],
-                        right_ref[chip, j, :rows, :],
-                        (((0,), (0,)), ((), ())),
-                        preferred_element_type=jnp.float32,
-                    )
-                    out_rows = pl.ds(pl.multiple_of(li * width, width), width)
-                    out_cols = pl.ds(pl.multiple_of(rj * width, width), width)
-                    out_ref[out_rows, out_cols] += prod
+        lids = [lids_ref[b * slots + i] for i in range(slots)]
+        rids = [rids_ref[b * slots + j] for j in range(slots)]
+        any_left = functools.reduce(jnp.logical_or, [li >= 0 for li in lids])
+        any_right = functools.reduce(jnp.logical_or, [rj >= 0 for rj in rids])
+
+        @pl.when(any_left & any_right)
+        def _():
+            lhs = jnp.concatenate([left_ref[z_rel, x_abs, i, :rows, :] for i in range(slots)], axis=1)
+            rhs = jnp.concatenate([right_ref[chip, j, :rows, :] for j in range(slots)], axis=1)
+            gram = lax.dot_general(
+                lhs, rhs, (((0,), (0,)), ((), ())), preferred_element_type=jnp.float32
+            )
+            for i in range(slots):
+                for j in range(slots):
+
+                    @pl.when((lids[i] >= 0) & (rids[j] >= 0))
+                    def _():
+                        out_rows = pl.ds(pl.multiple_of(lids[i] * width, width), width)
+                        out_cols = pl.ds(pl.multiple_of(rids[j] * width, width), width)
+                        out_ref[out_rows, out_cols] += gram[i * width:(i + 1) * width, j * width:(j + 1) * width]
 
         return carry
 

time: 231 us -> 224 us (0.970)
  Pallas kernels: 42.5 us -> 36.4 us
    pallas_call x2, Pallas kernels: 42.5 us -> 36.4 us  [accumulate(): pl.pallas_call(functools.partial(gram_kernel, slots, rows, width, n_chip,...]
  transfers between devices with their start and end apart: 13 -> 13, of which waited for: 7 -> 7; matrix products, arithmetic and copies ran while one was open for 12% -> 13% of each run, Pallas kernels for 8% -> 8%
where the time goes in v7:
time: 224 us
  waiting for transfers between devices  99.2 us (44%)
  Pallas kernels  36.4 us (16%)
  other arithmetic  27.6 us (12%)
  starting transfers between devices  26.9 us (12%)
  blocking collectives  25 us (11%)
  local copies, waits for them, and re-layouts  8.33 us (4%)
    ppermute x12, waiting for transfers between devices, shift(): return lax.ppermute(x, axis, [(i, (i + step) % n) for i in range(n)])  88.8 us
    pallas_call x2, Pallas kernels, accumulate(): pl.pallas_call(functools.partial(gram_kernel, slots, rows, width, n_chip,...  36.4 us
    all_to_all x1, blocking collectives, local(): lax.all_to_all(tagged, ('xhi', 'z'), split_axis=1, concat_axis=1, tiled=T...  25 us
    ppermute x12, starting transfers between devices, shift(): return lax.ppermute(x, axis, [(i, (i + step) % n) for i in range(n)])  22.6 us
    all_to_all x1, waiting for transfers between devices, local(): lax.all_to_all(tagged, ('xlo', 'y'), split_axis=1, concat_axis=0, tiled=T...  10.4 us
    another operation x2, other arithmetic, ring_gather(): return jnp.stack([bundle, from_above, far, from_below])  6.58 us
    select_n x2, other arithmetic, ring_gather(): jnp.where(first, jnp.stack([piece, other]), jnp.stack([other, piece]))  5.34 us
  transfers between devices with their start and end apart: 13, of which 7 were waited for; matrix products, arithmetic and copies ran while one was open for 13% of the time, Pallas kernels for 8%

profile of v7, /device:TPU:1, one launch (start us, length us, event | category | flops | bytes accessed | tf_op | source)
XLA Modules:
  0.0 223.5 jit_solution(15692277066194851348)
XLA Ops:
  0.0 0.7 fusion.4
  0.7 0.7 fusion.7
  1.4 0.1 copy.76
  1.5 0.8 select_reduce_fusion
  2.3 0.1 broadcast_multiply_fusion
  2.4 1.7 multiply_convert_fusion
  4.1 0.1 broadcast.396
  4.2 1.1 fusion.1
  5.3 25.0 %all_to_all.17 = bf16[1,8,2,272,128]{4,3,2,0,1:T(8,128)(2,1)S(1)} all-to-all(bf16[1,8,2,272,128]{4,3,2,0,1:T(8,128)(2,1)} %fusion.1), channel_id=1, replica_groups=mesh['xlo'=2,'y'=4,'xhi'=2,'z'=4,'core'=2] {'xhi','z'}, dimensions={1} | all-to-all | bytes 2228224 | tf_op jit(solution)/shard_map/all_to_all | solution.py:161
  30.2 4.3 %all-to-all-start = ((bf16[1,8,2,272,128]{4,3,2,0,1:T(8,128)(2,1)}), bf16[1,8,2,272,128]{4,3,2,0,1:T(8,128)(2,1)S(1)}, u32[]{:S(2)}, u32[]{:S(2)}) async-start(bf16[1,8,2,272,128]{4,3,2,0,1:T(8,128)(2,1)} %fusion.1), calls=%async_computation | async-start | bytes 2228224 | tf_op jit(solution)/shard_map/all_to_all | solution.py:155
  34.6 1.5 collective-permute-start.6
  36.0 10.4 %all-to-all-done = bf16[1,8,2,272,128]{4,3,2,0,1:T(8,128)(2,1)S(1)} async-done(((bf16[1,8,2,272,128]{4,3,2,0,1:T(8,128)(2,1)}), bf16[1,8,2,272,128]{4,3,2,0,1:T(8,128)(2,1)S(1)}, u32[]{:S(2)}, u32[]{:S(2)}) %all-to-all-start) | async-done | bytes 1114144 | tf_op jit(solution)/shard_map/all_to_all | solution.py:155
  46.4 1.0 collective-permute-start
  47.5 22.9 %collective-permute-done.6 = bf16[8,2,272,128]{3,2,1,0:T(8,128)(2,1)} collective-permute-done((bf16[8,2,272,128]{3,2,1,0:T(8,128)(2,1)S(1)}, bf16[8,2,272,128]{3,2,1,0:T(8,128)(2,1)}, u32[]{:S(2)}, u32[]{:S(2)}) %collective-permute-start.6) | collective-permute-done | bytes 1114144 | tf_op jit(solution)/shard_map/ppermute | solution.py:111
  70.4 3.4 %maximum_select_fusion.3 = bf16[2,8,2,272,128]{4,3,2,1,0:T(8,128)(2,1)} fusion(bf16[1,8,2,272,128]{4,3,2,1,0:T(8,128)(2,1)} %bitcast.18, bf16[1,8,2,272,128]{4,3,2,1,0:T(8,128)(2,1)S(1)} %bitcast.49, pred[]{:T(512)S(6)} %eq.36), kind=kLoop, calls=%fused_computation.11 | loop fusion | flops 3342336 | bytes 4456449 | tf_op jit(solution)/shard_map/jit(_where)/select_n | solution.py:127
  73.8 1.1 collective-permute-start.8
  74.9 1.6 collective-permute-start.7
  76.4 17.5 %collective-permute-done = bf16[8,2,272,128]{3,2,1,0:T(8,128)(2,1)S(1)} collective-permute-done((bf16[8,2,272,128]{3,2,1,0:T(8,128)(2,1)S(1)}, bf16[8,2,272,128]{3,2,1,0:T(8,128)(2,1)S(1)}, u32[]{:S(2)}, u32[]{:S(2)}) %collective-permute-start) | collective-permute-done | bytes 1114144 | tf_op jit(solution)/shard_map/ppermute | solution.py:111
  94.0 0.2 maximum_select_fusion.1
  94.2 2.2 collective-permute-start.2
  96.4 0.7 collective-permute-start.1
  97.1 21.7 %collective-permute-done.8 = bf16[2,8,2,272,128]{4,3,2,1,0:T(8,128)(2,1)} collective-permute-done((bf16[2,8,2,272,128]{4,3,2,1,0:T(8,128)(2,1)}, bf16[2,8,2,272,128]{4,3,2,1,0:T(8,128)(2,1)}, u32[]{:S(2)}, u32[]{:S(2)}) %collective-permute-start.8) | collective-permute-done | bytes 2228256 | tf_op jit(solution)/shard_map/ppermute | solution.py:111
  118.7 1.3 slice.72
  120.1 1.3 slice.73
  121.5 2.7 %collective-permute-start.10 = (bf16[1,8,2,272,128]{4,3,2,1,0:T(8,128)(2,1)S(1)}, bf16[1,8,2,272,128]{4,3,2,1,0:T(8,128)(2,1)S(1)}, u32[]{:S(2)}, u32[]{:S(2)}) collective-permute-start(bf16[1,8,2,272,128]{4,3,2,1,0:T(8,128)(2,1)S(1)} %slice.73), channel_id=1, source_target_pairs={{0,48},{16,0},{32,16},{48,32},{1,49},{17,1},{33,17},{49,33},{2,50}... | collective-permute-start | bytes 3342344 | tf_op jit(solution)/shard_map/ppermute | solution.py:111
  124.2 18.2 %collective-permute-done.2 = bf16[8,2,2,272,128]{4,3,2,1,0:T(8,128)(2,1)S(1)} collective-permute-done((bf16[8,2,2,272,128]{4,3,2,1,0:T(8,128)(2,1)S(1)}, bf16[8,2,2,272,128]{4,3,2,1,0:T(8,128)(2,1)S(1)}, u32[]{:S(2)}, u32[]{:S(2)}) %collective-permute-start.2) | collective-permute-done | bytes 2228256 | tf_op jit(solution)/shard_map/ppermute | solution.py:111
  142.5 1.7 collective-permute-start.3
  144.3 1.1 collective-permute-start.4
  145.4 2.0 maximum_select_fusion.2
  147.4 0.2 maximum_bitcast_fusion.1
  147.6 6.4 %pad_maximum_fusion.1.refs_1_ = bf16[4,2,8,2,272,128]{5,4,3,2,1,0:T(8,128)(2,1)} fusion(bf16[1,2,8,2,272,128]{5,4,3,2,1,0:T(8,128)(2,1)} %bitcast.21, bf16[1,2,8,2,272,128]{5,4,3,2,1,0:T(8,128)(2,1)S(1)} %maximum_bitcast_fusion.1, bf16[1,2,8,2,272,128]{5,4,3,2,1,0:T(8,128)(2,1)} %bitcast.19, bf16[1,2,8,2,272,128]{5,4,3,2,1,0:T(8,128)(2,1)S(1)} %maximum_select_fusion.2), kind=kLoop, calls=%fused_computation.5 | loop fusion | flops 13369344 | bytes 17825792 | tf_op jit(solution)/shard_map/stack | solution.py:133
  154.0 4.5 %collective-permute-start.11 = (bf16[4,2,8,2,272,128]{5,4,3,2,1,0:T(8,128)(2,1)}, bf16[4,2,8,2,272,128]{5,4,3,2,1,0:T(8,128)(2,1)}, u32[]{:S(2)}, u32[]{:S(2)}) collective-permute-start(bf16[4,2,8,2,272,128]{5,4,3,2,1,0:T(8,128)(2,1)} %pad_maximum_fusion.1.refs_1_), channel_id=1, source_target_pairs={{0,1},{1,0},{2,3},{3,2},{4,5},{5,4},{6,7},{7,6},{8,9},{9,8},{10,11... | collective-permute-start | bytes 26738696 | tf_op jit(solution)/shard_map/ppermute | solution.py:111
  158.5 7.4 %collective-permute-done.3 = bf16[4,2,2,272,128]{4,3,2,1,0:T(8,128)(2,1)S(1)} collective-permute-done((bf16[4,2,2,272,128]{4,3,2,1,0:T(8,128)(2,1)S(1)}, bf16[4,2,2,272,128]{4,3,2,1,0:T(8,128)(2,1)S(1)}, u32[]{:S(2)}, u32[]{:S(2)}) %collective-permute-start.3) | collective-permute-done | bytes 1114144 | tf_op jit(solution)/shard_map/ppermute | solution.py:111
  165.9 1.1 collective-permute-done.4
  166.9 0.2 maximum_bitcast_fusion
  167.1 4.2 %pad_maximum_fusion.refs_0_ = bf16[4,8,2,2,272,128]{5,4,3,2,1,0:T(8,128)(2,1)} fusion(bf16[1,8,2,2,272,128]{5,4,3,2,1,0:T(8,128)(2,1)S(1)} %bitcast.51, bf16[1,8,2,2,272,128]{5,4,3,2,1,0:T(8,128)(2,1)S(1)} %maximum_bitcast_fusion, bf16[1,8,2,2,272,128]{5,4,3,2,1,0:T(8,128)(2,1)S(1)} %bitcast.52, bf16[1,8,1,2,272,128]{5,4,3,1,2,0:T(8,128)(2,1)S(1)} %bitcast.54, ...), kind=kLoop, calls=%fused_computation.4 | loop fusion | flops 38993920 | bytes 17825792 | tf_op jit(solution)/shard_map/stack | solution.py:121
  171.4 4.4 %collective-permute-start.5 = (bf16[4,8,2,2,272,128]{5,4,3,2,1,0:T(8,128)(2,1)}, bf16[4,8,2,2,272,128]{5,4,3,2,1,0:T(8,128)(2,1)}, u32[]{:S(2)}, u32[]{:S(2)}) collective-permute-start(bf16[4,8,2,2,272,128]{5,4,3,2,1,0:T(8,128)(2,1)} %pad_maximum_fusion.refs_0_), channel_id=1, source_target_pairs={{0,1},{1,0},{2,3},{3,2},{4,5},{5,4},{6,7},{7,6},{8,9},{9,8},{10,11... | collective-permute-start | bytes 26738696 | tf_op jit(solution)/shard_map/ppermute | solution.py:111
  175.8 0.7 pad_add_fusion.rot_ref
  176.4 1.0 slice_convert_fusion.1
  177.5 0.2 copy.87
  177.6 0.1 copy.88
  177.8 0.7 reshape.487.lids_ref
  178.5 1.0 fusion.2
  179.5 0.2 copy.89
  179.7 0.6 gather_fusion.2
  180.3 0.1 copy.92
  180.4 0.6 gather_fusion.3
  180.9 0.1 copy.93
  181.1 0.1 gather.21
  181.2 0.6 and_select_fusion.rids_ref
  181.8 16.9 %shard_map.58.refs_0_ = f32[2048,1024]{1,0:T(8,128)} custom-call(s32[128]{0:T(128)} %reshape.487.lids_ref, s32[128]{0:T(128)} %and_select_fusion.rids_ref, s32[3]{0:T(128)} %pad_add_fusion.rot_ref, bf16[4,8,2,2,272,128]{5,4,3,2,1,0:T(8,128)(2,1)} %pad_maximum_fusion.refs_0_, bf16[4,2,8,2,272,128]{5,4,3,2,1,0:T(8,128)(2,1)} %pad_maximum_fusion.1.refs_1_), custom_call_target="tpu_custom_call" | custom-call | flops 2147483648 | bytes 26214400 | tf_op jit(solution)/shard_map/pallas_call | solution.py:94
  198.7 1.0 fusion.3
  199.8 0.2 copy.82
  199.9 0.6 gather_fusion
  200.5 0.1 copy.85
  200.6 0.6 gather_fusion.1
  201.2 0.1 copy.86
  201.3 0.1 gather.18
  201.4 0.6 and_select_fusion.1.rids_ref
  202.0 1.0 slice_convert_fusion.3
  203.0 0.2 copy.78
  203.2 0.1 copy.79
  203.3 0.7 reshape.485.lids_ref
  204.0 19.5 %shard_map.59 = f32[2048,1024]{1,0:T(8,128)} custom-call(s32[128]{0:T(128)} %reshape.485.lids_ref, s32[128]{0:T(128)} %and_select_fusion.1.rids_ref, s32[3]{0:T(128)} %pad_add_fusion.rot_ref, f32[2048,1024]{1,0:T(8,128)} %shard_map.58.refs_0_, bf16[4,8,2,2,272,128]{5,4,3,2,1,0:T(8,128)(2,1)} %collective-permute-done.5.refs_1_, ...), custom_call_target="tpu_custom_call", output_to_operand_aliasing={{}: (3, {})} | custom-call | flops 2147483648 | bytes 26214400 | tf_op jit(solution)/shard_map/pallas_call | solution.py:94
  (17 shorter events, 0.3 us)
Async XLA Ops:
  30.2 16.2 %all-to-all-start = ((bf16[1,8,2,272,128]{4,3,2,0,1:T(8,128)(2,1)}), bf16[1,8,2,272,128]{4,3,2,0,1:T(8,128)(2,1)S(1)}, u32[]{:S(2)}, u32[]{:S(2)}) async-start(bf16[1,8,2,272,128]{4,3,2,0,1:T(8,128)(2,1)} %fusion.1), calls=%async_computation | async-start | bytes 2228224 | tf_op jit(solution)/shard_map/all_to_all | solution.py:155
  34.6 35.9 %collective-permute-start.6 = (bf16[8,2,272,128]{3,2,1,0:T(8,128)(2,1)S(1)}, bf16[8,2,272,128]{3,2,1,0:T(8,128)(2,1)}, u32[]{:S(2)}, u32[]{:S(2)}) collective-permute-start(bf16[8,2,272,128]{3,2,1,0:T(8,128)(2,1)S(1)} %bitcast.48), channel_id=1, source_target_pairs={{0,64},{64,0},{1,65},{65,1},{2,66},{66,2},{3,67},{67,3},{4,68},{68... | collective-permute-start | bytes 3342344 | tf_op jit(solution)/shard_map/ppermute | solution.py:111
  46.4 47.5 %collective-permute-start = (bf16[8,2,272,128]{3,2,1,0:T(8,128)(2,1)S(1)}, bf16[8,2,272,128]{3,2,1,0:T(8,128)(2,1)S(1)}, u32[]{:S(2)}, u32[]{:S(2)}) collective-permute-start(bf16[8,2,272,128]{3,2,1,0:T(8,128)(2,1)S(1)} %bitcast.45), channel_id=1, source_target_pairs={{0,8},{8,0},{1,9},{9,1},{2,10},{10,2},{3,11},{11,3},{4,12},{12,4},... | collective-permute-start | bytes 3342344 | tf_op jit(solution)/shard_map/ppermute | solution.py:111
  73.8 45.0 %collective-permute-start.8 = (bf16[2,8,2,272,128]{4,3,2,1,0:T(8,128)(2,1)}, bf16[2,8,2,272,128]{4,3,2,1,0:T(8,128)(2,1)}, u32[]{:S(2)}, u32[]{:S(2)}) collective-permute-start(bf16[2,8,2,272,128]{4,3,2,1,0:T(8,128)(2,1)} %maximum_select_fusion.3), channel_id=1, source_target_pairs={{0,16},{16,32},{32,48},{48,0},{1,17},{17,33},{33,49},{49,1},{2,18}... | collective-permute-start | bytes 6684680 | tf_op jit(solution)/shard_map/ppermute | solution.py:111
  74.9 45.3 %collective-permute-start.7 = (bf16[2,8,2,272,128]{4,3,2,1,0:T(8,128)(2,1)}, bf16[2,8,2,272,128]{4,3,2,1,0:T(8,128)(2,1)}, u32[]{:S(2)}, u32[]{:S(2)}) collective-permute-start(bf16[2,8,2,272,128]{4,3,2,1,0:T(8,128)(2,1)} %maximum_select_fusion.3), channel_id=1, source_target_pairs={{0,48},{16,0},{32,16},{48,32},{1,49},{17,1},{33,17},{49,33},{2,50}... | collective-permute-start | bytes 6684680 | tf_op jit(solution)/shard_map/ppermute | solution.py:111
  94.2 48.2 %collective-permute-start.2 = (bf16[8,2,2,272,128]{4,3,2,1,0:T(8,128)(2,1)S(1)}, bf16[8,2,2,272,128]{4,3,2,1,0:T(8,128)(2,1)S(1)}, u32[]{:S(2)}, u32[]{:S(2)}) collective-permute-start(bf16[8,2,2,272,128]{4,3,2,1,0:T(8,128)(2,1)S(1)} %maximum_select_fusion.1), channel_id=1, source_target_pairs={{0,2},{2,4},{4,6},{6,0},{1,3},{3,5},{5,7},{7,1},{8,10},{10,12},{12... | collective-permute-start | bytes 6684680 | tf_op jit(solution)/shard_map/ppermute | solution.py:111
  96.4 47.8 %collective-permute-start.1 = (bf16[8,2,2,272,128]{4,3,2,1,0:T(8,128)(2,1)S(1)}, bf16[8,2,2,272,128]{4,3,2,1,0:T(8,128)(2,1)S(1)}, u32[]{:S(2)}, u32[]{:S(2)}) collective-permute-start(bf16[8,2,2,272,128]{4,3,2,1,0:T(8,128)(2,1)S(1)} %maximum_select_fusion.1), channel_id=1, source_target_pairs={{0,6},{2,0},{4,2},{6,4},{1,7},{3,1},{5,3},{7,5},{8,14},{10,8},{12,... | collective-permute-start | bytes 6684680 | tf_op jit(solution)/shard_map/ppermute | solution.py:111
  120.1 27.3 %collective-permute-start.9 = (bf16[1,8,2,272,128]{4,3,2,1,0:T(8,128)(2,1)S(1)}, bf16[1,8,2,272,128]{4,3,2,1,0:T(8,128)(2,1)S(1)}, u32[]{:S(2)}, u32[]{:S(2)}) collective-permute-start(bf16[1,8,2,272,128]{4,3,2,1,0:T(8,128)(2,1)S(1)} %slice.72), channel_id=1, source_target_pairs={{0,16},{16,32},{32,48},{48,0},{1,17},{17,33},{33,49},{49,1},{2,18}... | collective-permute-start | bytes 3342344 | tf_op jit(solution)/shard_map/ppermute | solution.py:111
  121.5 25.9 %collective-permute-start.10 = (bf16[1,8,2,272,128]{4,3,2,1,0:T(8,128)(2,1)S(1)}, bf16[1,8,2,272,128]{4,3,2,1,0:T(8,128)(2,1)S(1)}, u32[]{:S(2)}, u32[]{:S(2)}) collective-permute-start(bf16[1,8,2,272,128]{4,3,2,1,0:T(8,128)(2,1)S(1)} %slice.73), channel_id=1, source_target_pairs={{0,48},{16,0},{32,16},{48,32},{1,49},{17,1},{33,17},{49,33},{2,50}... | collective-permute-start | bytes 3342344 | tf_op jit(solution)/shard_map/ppermute | solution.py:111
  142.5 23.4 %collective-permute-start.3 = (bf16[4,2,2,272,128]{4,3,2,1,0:T(8,128)(2,1)S(1)}, bf16[4,2,2,272,128]{4,3,2,1,0:T(8,128)(2,1)S(1)}, u32[]{:S(2)}, u32[]{:S(2)}) collective-permute-start(bf16[4,2,2,272,128]{4,3,2,1,0:T(8,128)(2,1)S(1)} %slice.69), channel_id=1, source_target_pairs={{0,2},{2,4},{4,6},{6,0},{1,3},{3,5},{5,7},{7,1},{8,10},{10,12},{12... | collective-permute-start | bytes 3342344 | tf_op jit(solution)/shard_map/ppermute | solution.py:111
  144.3 22.7 %collective-permute-start.4 = (bf16[4,2,2,272,128]{4,3,2,1,0:T(8,128)(2,1)S(1)}, bf16[4,2,2,272,128]{4,3,2,1,0:T(8,128)(2,1)S(1)}, u32[]{:S(2)}, u32[]{:S(2)}) collective-permute-start(bf16[4,2,2,272,128]{4,3,2,1,0:T(8,128)(2,1)S(1)} %slice.70), channel_id=1, source_target_pairs={{0,6},{2,0},{4,2},{6,4},{1,7},{3,1},{5,3},{7,5},{8,14},{10,8},{12,... | collective-permute-start | bytes 3342344 | tf_op jit(solution)/shard_map/ppermute | solution.py:111
  154.0 44.8 %collective-permute-start.11 = (bf16[4,2,8,2,272,128]{5,4,3,2,1,0:T(8,128)(2,1)}, bf16[4,2,8,2,272,128]{5,4,3,2,1,0:T(8,128)(2,1)}, u32[]{:S(2)}, u32[]{:S(2)}) collective-permute-start(bf16[4,2,8,2,272,128]{5,4,3,2,1,0:T(8,128)(2,1)} %pad_maximum_fusion.1.refs_1_), channel_id=1, source_target_pairs={{0,1},{1,0},{2,3},{3,2},{4,5},{5,4},{6,7},{7,6},{8,9},{9,8},{10,11... | collective-permute-start | bytes 26738696 | tf_op jit(solution)/shard_map/ppermute | solution.py:111
  171.4 30.7 %collective-permute-start.5 = (bf16[4,8,2,2,272,128]{5,4,3,2,1,0:T(8,128)(2,1)}, bf16[4,8,2,2,272,128]{5,4,3,2,1,0:T(8,128)(2,1)}, u32[]{:S(2)}, u32[]{:S(2)}) collective-permute-start(bf16[4,8,2,2,272,128]{5,4,3,2,1,0:T(8,128)(2,1)} %pad_maximum_fusion.refs_0_), channel_id=1, source_target_pairs={{0,1},{1,0},{2,3},{3,2},{4,5},{5,4},{6,7},{7,6},{8,9},{9,8},{10,11... | collective-permute-start | bytes 26738696 | tf_op jit(solution)/shard_map/ppermute | solution.py:111

commit v8 on v7

--- a/solution.py
+++ b/solution.py
@@ -31,14 +31,14 @@
         else:
             out_ref[...] = jnp.zeros_like(out_ref)
 
-    n_z = left_ref.shape[0]
     n_xhi = left_ref.shape[1]
+    n_chip_z = right_ref.shape[0] // n_xhi
 
     def body(k, carry):
         b = r * group + k
-        z_rel = k // n_xhi
+        piece = k // n_xhi
         x_abs = lax.rem(k, n_xhi)
-        chip = x_abs * n_z + lax.rem(rot_ref[2] + z_rel, n_z)
+        chip = x_abs * n_chip_z + lax.rem(rot_ref[2] + rot_ref[3 + piece], n_chip_z)
         lids = [lids_ref[b * slots + i] for i in range(slots)]
         rids = [rids_ref[b * slots + j] for j in range(slots)]
         any_left = functools.reduce(jnp.logical_or, [li >= 0 for li in lids])
@@ -46,7 +46,7 @@
 
         @pl.when(any_left & any_right)
         def _():
-            lhs = jnp.concatenate([left_ref[z_rel, x_abs, i, :rows, :] for i in range(slots)], axis=1)
+            lhs = jnp.concatenate([left_ref[piece, x_abs, i, :rows, :] for i in range(slots)], axis=1)
             rhs = jnp.concatenate([right_ref[chip, j, :rows, :] for j in range(slots)], axis=1)
             gram = lax.dot_general(
                 lhs, rhs, (((0,), (0,)), ((), ())), preferred_element_type=jnp.float32
@@ -66,8 +66,8 @@
 
 
 def accumulate(prev, left, left_ids, right, right_ids, rot, rows, per_row, per_col):
-    n_z, n_row, n_xhi, slots, band_rows, width = left.shape
-    n_chip = n_xhi * n_z
+    n_piece, n_row, n_xhi, slots, band_rows, width = left.shape
+    n_chip = n_xhi * n_piece
     n_y = right.shape[0]
     out_shape = (per_row * width, per_col * width)
 
@@ -75,8 +75,8 @@
         return (lax.rem(lax.rem(r, n_y) - rot[0] + n_y, n_y), r // n_y, 0, 0, 0, 0)
 
     in_specs = [
-        pl.BlockSpec((n_z, None, n_xhi, slots, band_rows, width), lambda r, lids, rids, rot: (0, r, 0, 0, 0, 0)),
-        pl.BlockSpec((None, None, n_chip, slots, band_rows, width), right_map),
+        pl.BlockSpec((n_piece, None, n_xhi, slots, band_rows, width), lambda r, lids, rids, rot: (0, r, 0, 0, 0, 0)),
+        pl.BlockSpec((None, None, right.shape[2], slots, band_rows, width), right_map),
     ]
     operands = [left, right]
     carry_in = prev is not None
@@ -118,7 +118,7 @@
     far_low = shift(from_below[:half], "z", 1)
     far_high = shift(from_above[half:], "z", -1)
     far = jnp.concatenate([far_low, far_high], axis=0)
-    return jnp.stack([piece, from_above, far, from_below])
+    return jnp.stack([piece, from_above, from_below]), far[None]
 
 
 def ring_gather(piece):
@@ -157,10 +157,11 @@
     first = lax.axis_index("xhi") == 0
     other = shift(left, "xhi", 1)
     left = jnp.where(first, jnp.stack([left, other], axis=1), jnp.stack([other, left], axis=1))
-    left_own = z_ring(left)
+    near_own, far_own = z_ring(left)
     right = lax.all_to_all(tagged, ("xhi", "z"), split_axis=1, concat_axis=1, tiled=True)
     right_own = ring_gather(right[0])
-    left_other = shift(left_own, "core", 1)
+    near_other = shift(near_own, "core", 1)
+    far_other = shift(far_own, "core", 1)
     right_other = shift(right_own, "core", 1)
 
     n_y = lax.axis_size("y")
@@ -170,21 +171,27 @@
     me_z = lax.axis_index("z")
     me_xhi = lax.axis_index("xhi")
     absolute_y = (jnp.arange(n_y, dtype=jnp.int32) - me_y) % n_y
-    k_rel = jnp.arange(n_xhi * n_z, dtype=jnp.int32)
-    chip_of = (k_rel % n_xhi) * n_z + (me_z + k_rel // n_xhi) % n_z
-
-    def part(prev, left_half, right_half):
+
+    def part(prev, left_half, steps, right_half):
+        n_piece = len(steps)
         left_ids = left_half[:, :, :, :, rows, 0].astype(jnp.int32)
         left_ids = jnp.transpose(left_ids, (1, 0, 2, 3))
         right_ids = right_half[:, :, :, :, rows, 0].astype(jnp.int32) - me_core * per_col
         right_ids = jnp.transpose(right_ids[absolute_y], (1, 0, 2, 3)).reshape(row_devices, chips, slots)
+        k_rel = jnp.arange(n_xhi * n_piece, dtype=jnp.int32)
+        z_step = jnp.array(steps, jnp.int32)[k_rel // n_xhi]
+        chip_of = (k_rel % n_xhi) * n_z + (me_z + z_step) % n_z
         right_ids = right_ids[:, chip_of]
         right_ids = jnp.where((right_ids >= 0) & (right_ids < per_col), right_ids, -1)
-        rot = jnp.stack([me_y, me_xhi, me_z]).astype(jnp.int32)
+        rot = jnp.concatenate([jnp.stack([me_y, me_xhi, me_z]), jnp.array(steps)]).astype(jnp.int32)
         return accumulate(prev, left_half, left_ids, right_half, right_ids, rot, rows, per_row, per_col)
 
-    normal = part(None, left_own, right_own)
-    return part(normal, left_other, right_other)
+    near_steps = (0, 1, n_z - 1)
+    far_steps = (2,)
+    normal = part(None, near_own, near_steps, right_own)
+    normal = part(normal, far_own, far_steps, right_own)
+    normal = part(normal, near_other, near_steps, right_other)
+    return part(normal, far_other, far_steps, right_other)
 
 def solution(mesh):
     row_devices, col_devices = mesh.devices.shape

time: 224 us -> 304 us (1.36)
  blocking collectives: 25 us -> 82.8 us
  Pallas kernels: 36.4 us -> 61.5 us
  waiting for transfers between devices: 99.2 us -> 93.7 us
  local copies, waits for them, and re-layouts: 8.33 us -> 13.5 us
    all_to_all x0 -> x1, blocking collectives: none -> 58 us  [local(): lax.all_to_all(tagged, ('xlo', 'y'), split_axis=1, concat_axis=0, tiled=T...]
    pallas_call x2 -> x4, Pallas kernels: 36.4 us -> 61.5 us  [accumulate(): pl.pallas_call(functools.partial(gram_kernel, slots, rows, width, n_chip,...]
    all_to_all x1 -> x0, waiting for transfers between devices: 10.4 us -> none  [local(): lax.all_to_all(tagged, ('xlo', 'y'), split_axis=1, concat_axis=0, tiled=T...]
    ppermute x12 -> x13, waiting for transfers between devices: 88.8 us -> 93.7 us  [shift(): return lax.ppermute(x, axis, [(i, (i + step) % n) for i in range(n)])]
    select_n x2, other arithmetic: 5.34 us -> 0.73 us  [ring_gather(): jnp.where(first, jnp.stack([piece, other]), jnp.stack([other, piece]))]
    all_to_all x1 -> x0, starting transfers between devices: 4.31 us -> none  [local(): lax.all_to_all(tagged, ('xlo', 'y'), split_axis=1, concat_axis=0, tiled=T...]
    ppermute x12 -> x13, starting transfers between devices: 22.6 us -> 25.3 us  [shift(): return lax.ppermute(x, axis, [(i, (i + step) % n) for i in range(n)])]
  transfers between devices with their start and end apart: 13 -> 13, of which waited for: 7 -> 6; matrix products, arithmetic and copies ran while one was open for 13% -> 9% of each run, Pallas kernels for 8% -> 10%
where the time goes in v8:
time: 304 us; the launch traced here: 302 us
  waiting for transfers between devices  93.7 us (31%)
  blocking collectives  82.8 us (27%)
  Pallas kernels  61.5 us (20%)
  starting transfers between devices  25.3 us (8%)
  other arithmetic  25.2 us (8%)
  local copies, waits for them, and re-layouts  13.5 us (4%)
    ppermute x13, waiting for transfers between devices, shift(): return lax.ppermute(x, axis, [(i, (i + step) % n) for i in range(n)])  93.7 us
    pallas_call x4, Pallas kernels, accumulate(): pl.pallas_call(functools.partial(gram_kernel, slots, rows, width, n_chip,...  61.5 us
    all_to_all x1, blocking collectives, local(): lax.all_to_all(tagged, ('xlo', 'y'), split_axis=1, concat_axis=0, tiled=T...  58 us
    ppermute x13, starting transfers between devices, shift(): return lax.ppermute(x, axis, [(i, (i + step) % n) for i in range(n)])  25.3 us
    all_to_all x1, blocking collectives, local(): lax.all_to_all(tagged, ('xhi', 'z'), split_axis=1, concat_axis=1, tiled=T...  24.8 us
  transfers between devices with their start and end apart: 13, of which 6 were waited for; matrix products, arithmetic and copies ran while one was open for 9% of the time, Pallas kernels for 10%

profile of v8, /device:TPU:1, one launch (start us, length us, event | category | flops | bytes accessed | tf_op | source)
XLA Modules:
  0.0 302.3 jit_solution(6597199360678373238)
XLA Ops:
  0.0 0.7 fusion.6
  0.7 0.7 fusion.9
  1.5 0.8 select_reduce_fusion
  2.4 1.7 multiply_convert_fusion
  4.3 24.8 %all_to_all.17 = bf16[1,8,2,272,128]{4,3,2,0,1:T(8,128)(2,1)S(1)} all-to-all(bf16[1,8,2,272,128]{4,3,2,0,1:T(8,128)(2,1)S(1)} %fusion.1), channel_id=1, replica_groups=mesh['xlo'=2,'y'=4,'xhi'=2,'z'=4,'core'=2] {'xhi','z'}, dimensions={1} | all-to-all | bytes 2228224 | tf_op jit(solution)/shard_map/all_to_all | solution.py:161
  29.1 0.4 collective-permute-start.6
  29.5 23.3 %collective-permute-done.6 = bf16[8,2,272,128]{3,2,1,0:T(8,128)(2,1)S(1)} collective-permute-done((bf16[8,2,272,128]{3,2,1,0:T(8,128)(2,1)S(1)}, bf16[8,2,272,128]{3,2,1,0:T(8,128)(2,1)S(1)}, u32[]{:S(2)}, u32[]{:S(2)}) %collective-permute-start.6) | collective-permute-done | bytes 1114144 | tf_op jit(solution)/shard_map/ppermute | solution.py:111
  52.8 0.4 maximum_select_fusion.2
  53.1 0.6 copy-done.6
  53.8 2.7 collective-permute-start.7
  56.5 58.0 %all_to_all.18 = bf16[1,8,2,272,128]{4,3,2,0,1:T(8,128)(2,1)S(1)} all-to-all(bf16[1,8,2,272,128]{4,3,2,0,1:T(8,128)(2,1)S(1)} %fusion.1), channel_id=1, replica_groups=mesh['xlo'=2,'y'=4,'xhi'=2,'z'=4,'core'=2] {'xlo','y'}, dimensions={1} | all-to-all | bytes 2228224 | tf_op jit(solution)/shard_map/all_to_all | solution.py:155
  114.5 0.5 collective-permute-start
  115.1 1.2 slice.89
  116.3 0.7 collective-permute-start.10
  117.1 1.4 copy-done.4
  118.4 1.1 slice.88
  119.5 0.7 collective-permute-start.9
  120.2 15.9 %collective-permute-done = bf16[8,2,272,128]{3,2,1,0:T(8,128)(2,1)S(1)} collective-permute-done((bf16[8,2,272,128]{3,2,1,0:T(8,128)(2,1)S(1)}, bf16[8,2,272,128]{3,2,1,0:T(8,128)(2,1)S(1)}, u32[]{:S(2)}, u32[]{:S(2)}) %collective-permute-start) | collective-permute-done | bytes 1114144 | tf_op jit(solution)/shard_map/ppermute | solution.py:111
  136.2 0.2 maximum_select_fusion
  136.4 1.0 collective-permute-start.3
  137.3 0.6 collective-permute-start.1
  137.9 0.4 maximum_select_fusion.1
  138.3 3.0 %collective-permute-done.9 = bf16[1,8,2,272,128]{4,3,2,1,0:T(8,128)(2,1)} collective-permute-done((bf16[1,8,2,272,128]{4,3,2,1,0:T(8,128)(2,1)}, bf16[1,8,2,272,128]{4,3,2,1,0:T(8,128)(2,1)}, u32[]{:S(2)}, u32[]{:S(2)}) %collective-permute-start.9) | collective-permute-done | bytes 1114144 | tf_op jit(solution)/shard_map/ppermute | solution.py:111
  141.3 1.8 maximum_bitcast_fusion.1
  143.2 4.0 %pad_maximum_fusion.refs_1_.refs_2_ = bf16[4,2,8,2,272,128]{5,4,3,2,1,0:T(8,128)(2,1)} fusion(bf16[1,2,8,2,272,128]{5,4,3,2,1,0:T(8,128)(2,1)S(1)} %bitcast.62, bf16[1,2,8,2,272,128]{5,4,3,2,1,0:T(8,128)(2,1)S(1)} %maximum_bitcast_fusion.1, bf16[1,2,8,2,272,128]{5,4,3,2,1,0:T(8,128)(2,1)S(1)} %bitcast.61, ...), kind=kLoop, calls=%fused_computation.7 | loop fusion | flops 13369344 | bytes 17825792 | tf_op jit(solution)/shard_map/stack | solution.py:133
  147.2 6.6 %collective-permute-start.11 = (bf16[4,2,8,2,272,128]{5,4,3,2,1,0:T(8,128)(2,1)}, bf16[4,2,8,2,272,128]{5,4,3,2,1,0:T(8,128)(2,1)}, u32[]{:S(2)}, u32[]{:S(2)}) collective-permute-start(bf16[4,2,8,2,272,128]{5,4,3,2,1,0:T(8,128)(2,1)} %pad_maximum_fusion.refs_1_.refs_2_), channel_id=1, source_target_pairs={{0,1},{1,0},{2,3},{3,2},{4,5},{5,4},{6,7},{7,6},{8,9},{9,8},{10,11... | collective-permute-start | bytes 26738696 | tf_op jit(solution)/shard_map/ppermute | solution.py:111
  153.8 25.7 %collective-permute-done.3 = bf16[8,2,2,272,128]{4,3,2,1,0:T(8,128)(2,1)S(1)} collective-permute-done((bf16[8,2,2,272,128]{4,3,2,1,0:T(8,128)(2,1)S(1)}, bf16[8,2,2,272,128]{4,3,2,1,0:T(8,128)(2,1)S(1)}, u32[]{:S(2)}, u32[]{:S(2)}) %collective-permute-start.3) | collective-permute-done | bytes 2228256 | tf_op jit(solution)/shard_map/ppermute | solution.py:111
  179.5 1.8 collective-permute-done.1
  181.3 3.4 %pad_maximum_fusion.1.refs_0_ = bf16[3,8,2,2,272,128]{5,4,3,2,1,0:T(8,128)(2,1)} fusion(bf16[1,8,2,2,272,128]{5,4,3,2,1,0:T(8,128)(2,1)S(1)} %bitcast.64, bf16[1,8,2,2,272,128]{5,4,3,2,1,0:T(8,128)(2,1)S(1)} %bitcast.63, bf16[1,8,1,2,272,128]{5,4,3,1,2,0:T(8,128)(2,1)S(1)} %bitcast.68, bf16[1,8,1,2,272,128]{5,4,3,1,2,0:T(8,128)(2,1)S(1)} %bitcast.60, pred[]{:T(512)S(6)} %eq.39), kind=kLoop, calls=%fused_computation.8 | loop fusion | flops 23396352 | bytes 13369345 | tf_op jit(solution)/shard_map/stack | solution.py:121
  184.7 8.1 %collective-permute-start.12 = (bf16[3,8,2,2,272,128]{5,4,3,2,1,0:T(8,128)(2,1)}, bf16[3,8,2,2,272,128]{5,4,3,2,1,0:T(8,128)(2,1)}, u32[]{:S(2)}, u32[]{:S(2)}) collective-permute-start(bf16[3,8,2,2,272,128]{5,4,3,2,1,0:T(8,128)(2,1)} %pad_maximum_fusion.1.refs_0_), channel_id=1, source_target_pairs={{0,1},{1,0},{2,3},{3,2},{4,5},{5,4},{6,7},{7,6},{8,9},{9,8},{10,11... | collective-permute-start | bytes 20054024 | tf_op jit(solution)/shard_map/ppermute | solution.py:111
  193.0 2.7 collective-permute-start.4
  195.8 0.6 gather_fusion.2
  196.4 23.9 %collective-permute-done.2 = bf16[4,2,2,272,128]{4,3,2,1,0:T(8,128)(2,1)S(1)} collective-permute-done((bf16[4,2,2,272,128]{4,3,2,1,0:T(8,128)(2,1)S(1)}, bf16[4,2,2,272,128]{4,3,2,1,0:T(8,128)(2,1)S(1)}, u32[]{:S(2)}, u32[]{:S(2)}) %collective-permute-start.2) | collective-permute-done | bytes 1114144 | tf_op jit(solution)/shard_map/ppermute | solution.py:111
  220.3 1.4 maximum_bitcast_fusion.refs_1_
  221.8 1.0 collective-permute-start.5
  222.9 0.7 pad_add_fusion.1.rot_ref
  223.5 0.7 pad_add_fusion.rot_ref
  224.2 1.0 slice_convert_fusion.2
  225.2 0.4 copy.131
  225.6 0.7 reshape.630.lids_ref
  226.3 1.0 fusion.2
  227.3 0.2 copy.121
  227.5 0.6 gather_fusion.4
  228.2 0.6 gather_fusion.6
  229.0 0.6 gather_fusion.5
  229.7 0.7 fusion.4
  230.4 0.7 reshape.628.lids_ref
  231.1 0.5 and_select_fusion.rids_ref
  231.6 15.0 %shard_map.136.refs_0_ = f32[2048,1024]{1,0:T(8,128)} custom-call(s32[96]{0:T(128)} %reshape.630.lids_ref, s32[96]{0:T(128)} %and_select_fusion.rids_ref, s32[6]{0:T(128)} %pad_add_fusion.1.rot_ref, bf16[3,8,2,2,272,128]{5,4,3,2,1,0:T(8,128)(2,1)} %pad_maximum_fusion.1.refs_0_, bf16[4,2,8,2,272,128]{5,4,3,2,1,0:T(8,128)(2,1)} %pad_maximum_fusion.refs_1_.refs_2_), custom_call_target="tpu_custom_call" | custom-call | flops 1610612736 | bytes 26214400 | tf_op jit(solution)/shard_map/pallas_call | solution.py:94
  246.5 0.5 and_select_fusion.1.rids_ref
  247.1 14.0 %shard_map.137.refs_0_ = f32[2048,1024]{1,0:T(8,128)} custom-call(s32[32]{0:T(128)} %reshape.628.lids_ref, s32[32]{0:T(128)} %and_select_fusion.1.rids_ref, s32[4]{0:T(128)} %pad_add_fusion.rot_ref, f32[2048,1024]{1,0:T(8,128)} %shard_map.136.refs_0_, bf16[1,8,2,2,272,128]{5,4,3,2,1,0:T(8,128)(2,1)} %copy-done.1, ...), custom_call_target="tpu_custom_call", output_to_operand_aliasing={{}: (3, {})} | custom-call | flops 536870912 | bytes 26214400 | tf_op jit(solution)/shard_map/pallas_call | solution.py:94
  261.1 1.5 fusion.5
  262.6 0.6 reshape.625.lids_ref
  263.2 1.0 slice_convert_fusion.3
  264.2 0.4 copy.130
  264.6 0.7 reshape.627.lids_ref
  265.3 1.0 fusion.3
  266.5 0.6 gather_fusion
  267.1 0.6 gather_fusion.3
  267.7 0.6 gather_fusion.1
  268.5 0.5 and_select_fusion.2.rids_ref
  269.2 0.5 and_select_fusion.6.rids_ref
  269.7 18.4 %shard_map.138.refs_0_ = f32[2048,1024]{1,0:T(8,128)} custom-call(s32[96]{0:T(128)} %reshape.627.lids_ref, s32[96]{0:T(128)} %and_select_fusion.2.rids_ref, s32[6]{0:T(128)} %pad_add_fusion.1.rot_ref, f32[2048,1024]{1,0:T(8,128)} %shard_map.137.refs_0_, ...), custom_call_target="tpu_custom_call", output_to_operand_aliasing={{}: (3, {})} | custom-call | flops 1610612736 | bytes 26214400 | tf_op jit(solution)/shard_map/pallas_call | solution.py:94
  288.0 14.2 %shard_map.139 = f32[2048,1024]{1,0:T(8,128)} custom-call(s32[32]{0:T(128)} %reshape.625.lids_ref, s32[32]{0:T(128)} %and_select_fusion.6.rids_ref, s32[4]{0:T(128)} %pad_add_fusion.rot_ref, f32[2048,1024]{1,0:T(8,128)} %shard_map.138.refs_0_, bf16[1,8,2,2,272,128]{5,4,3,2,1,0:T(8,128)(2,1)} %collective-permute-done.5.refs_1_, ...), custom_call_target="tpu_custom_call", output_to_operand_aliasing={{}: (3, {})} | custom-call | flops 536870912 | bytes 26214400 | tf_op jit(solution)/shard_map/pallas_call | solution.py:94
  (52 shorter events, 1.9 us)
Async XLA Ops:
  29.1 23.7 %collective-permute-start.6 = (bf16[8,2,272,128]{3,2,1,0:T(8,128)(2,1)S(1)}, bf16[8,2,272,128]{3,2,1,0:T(8,128)(2,1)S(1)}, u32[]{:S(2)}, u32[]{:S(2)}) collective-permute-start(bf16[8,2,272,128]{3,2,1,0:T(8,128)(2,1)S(1)} %bitcast.55), channel_id=1, source_target_pairs={{0,64},{64,0},{1,65},{65,1},{2,66},{66,2},{3,67},{67,3},{4,68},{68... | collective-permute-start | bytes 3342344 | tf_op jit(solution)/shard_map/ppermute | solution.py:111
  52.8 1.0 copy-start.6
  53.8 61.3 %collective-permute-start.7 = (bf16[2,8,2,272,128]{4,3,2,1,0:T(8,128)(2,1)S(1)}, bf16[2,8,2,272,128]{4,3,2,1,0:T(8,128)(2,1)S(1)}, u32[]{:S(2)}, u32[]{:S(2)}) collective-permute-start(bf16[2,8,2,272,128]{4,3,2,1,0:T(8,128)(2,1)S(1)} %maximum_select_fusion.2), channel_id=1, source_target_pairs={{0,48},{16,0},{32,16},{48,32},{1,49},{17,1},{33,17},{49,33},{2,50}... | collective-permute-start | bytes 6684680 | tf_op jit(solution)/shard_map/ppermute | solution.py:111
  56.5 60.6 %collective-permute-start.8 = (bf16[2,8,2,272,128]{4,3,2,1,0:T(8,128)(2,1)S(1)}, bf16[2,8,2,272,128]{4,3,2,1,0:T(8,128)(2,1)S(1)}, u32[]{:S(2)}, u32[]{:S(2)}) collective-permute-start(bf16[2,8,2,272,128]{4,3,2,1,0:T(8,128)(2,1)S(1)} %maximum_select_fusion.2), channel_id=1, source_target_pairs={{0,16},{16,32},{32,48},{48,0},{1,17},{17,33},{33,49},{49,1},{2,18}... | collective-permute-start | bytes 6684680 | tf_op jit(solution)/shard_map/ppermute | solution.py:111
  114.5 21.6 %collective-permute-start = (bf16[8,2,272,128]{3,2,1,0:T(8,128)(2,1)S(1)}, bf16[8,2,272,128]{3,2,1,0:T(8,128)(2,1)S(1)}, u32[]{:S(2)}, u32[]{:S(2)}) collective-permute-start(bf16[8,2,272,128]{3,2,1,0:T(8,128)(2,1)S(1)} %bitcast.58), channel_id=1, source_target_pairs={{0,8},{8,0},{1,9},{9,1},{2,10},{10,2},{3,11},{11,3},{4,12},{12,4},... | collective-permute-start | bytes 3342344 | tf_op jit(solution)/shard_map/ppermute | solution.py:111
  115.1 4.4 %copy-start.2 = (bf16[2,8,2,272,128]{4,3,2,1,0:T(8,128)(2,1)}, bf16[2,8,2,272,128]{4,3,2,1,0:T(8,128)(2,1)S(1)}, u32[]{:S(2)}) copy-start(bf16[2,8,2,272,128]{4,3,2,1,0:T(8,128)(2,1)S(1)} %collective-permute-done.7) | copy-start | bytes 6684676
  116.3 22.0 %collective-permute-start.10 = (bf16[1,8,2,272,128]{4,3,2,1,0:T(8,128)(2,1)}, bf16[1,8,2,272,128]{4,3,2,1,0:T(8,128)(2,1)}, u32[]{:S(2)}, u32[]{:S(2)}) collective-permute-start(bf16[1,8,2,272,128]{4,3,2,1,0:T(8,128)(2,1)} %slice.89), channel_id=1, source_target_pairs={{0,48},{16,0},{32,16},{48,32},{1,49},{17,1},{33,17},{49,33},{2,50}... | collective-permute-start | bytes 3342344 | tf_op jit(solution)/shard_map/ppermute | solution.py:111
  117.1 1.4 copy-start.4
  119.5 21.9 %collective-permute-start.9 = (bf16[1,8,2,272,128]{4,3,2,1,0:T(8,128)(2,1)}, bf16[1,8,2,272,128]{4,3,2,1,0:T(8,128)(2,1)}, u32[]{:S(2)}, u32[]{:S(2)}) collective-permute-start(bf16[1,8,2,272,128]{4,3,2,1,0:T(8,128)(2,1)} %slice.88), channel_id=1, source_target_pairs={{0,16},{16,32},{32,48},{48,0},{1,17},{17,33},{33,49},{49,1},{2,18}... | collective-permute-start | bytes 3342344 | tf_op jit(solution)/shard_map/ppermute | solution.py:111
  136.2 1.7 copy-start.7
  136.4 43.1 %collective-permute-start.3 = (bf16[8,2,2,272,128]{4,3,2,1,0:T(8,128)(2,1)S(1)}, bf16[8,2,2,272,128]{4,3,2,1,0:T(8,128)(2,1)S(1)}, u32[]{:S(2)}, u32[]{:S(2)}) collective-permute-start(bf16[8,2,2,272,128]{4,3,2,1,0:T(8,128)(2,1)S(1)} %maximum_select_fusion), channel_id=1, source_target_pairs={{0,6},{2,0},{4,2},{6,4},{1,7},{3,1},{5,3},{7,5},{8,14},{10,8},{12,... | collective-permute-start | bytes 6684680 | tf_op jit(solution)/shard_map/ppermute | solution.py:111
  137.3 44.0 %collective-permute-start.1 = (bf16[8,2,2,272,128]{4,3,2,1,0:T(8,128)(2,1)S(1)}, bf16[8,2,2,272,128]{4,3,2,1,0:T(8,128)(2,1)S(1)}, u32[]{:S(2)}, u32[]{:S(2)}) collective-permute-start(bf16[8,2,2,272,128]{4,3,2,1,0:T(8,128)(2,1)S(1)} %maximum_select_fusion), channel_id=1, source_target_pairs={{0,2},{2,4},{4,6},{6,0},{1,3},{3,5},{5,7},{7,1},{8,10},{10,12},{12... | collective-permute-start | bytes 6684680 | tf_op jit(solution)/shard_map/ppermute | solution.py:111
  138.3 4.9 %copy-start.3 = (bf16[2,8,2,272,128]{4,3,2,1,0:T(8,128)(2,1)S(1)}, bf16[2,8,2,272,128]{4,3,2,1,0:T(8,128)(2,1)}, u32[]{:S(2)}) copy-start(bf16[2,8,2,272,128]{4,3,2,1,0:T(8,128)(2,1)} %copy-done.2) | copy-start | bytes 6684676
  138.3 4.9 %copy-start.5 = (bf16[2,8,2,272,128]{4,3,2,1,0:T(8,128)(2,1)S(1)}, bf16[2,8,2,272,128]{4,3,2,1,0:T(8,128)(2,1)}, u32[]{:S(2)}) copy-start(bf16[2,8,2,272,128]{4,3,2,1,0:T(8,128)(2,1)} %copy-done.4) | copy-start | bytes 6684676
  147.2 118.1 %collective-permute-start.11 = (bf16[4,2,8,2,272,128]{5,4,3,2,1,0:T(8,128)(2,1)}, bf16[4,2,8,2,272,128]{5,4,3,2,1,0:T(8,128)(2,1)}, u32[]{:S(2)}, u32[]{:S(2)}) collective-permute-start(bf16[4,2,8,2,272,128]{5,4,3,2,1,0:T(8,128)(2,1)} %pad_maximum_fusion.refs_1_.refs_2_), channel_id=1, source_target_pairs={{0,1},{1,0},{2,3},{3,2},{4,5},{5,4},{6,7},{7,6},{8,9},{9,8},{10,11... | collective-permute-start | bytes 26738696 | tf_op jit(solution)/shard_map/ppermute | solution.py:111
  184.7 11.1 %copy-start = (s32[3]{0:T(128)S(1)}, s32[3]{0:T(128)}, u32[]{:S(2)}) copy-start(s32[3]{0:T(128)} %constant.163.clone) | copy-start | bytes 40
  184.7 78.5 %collective-permute-start.12 = (bf16[3,8,2,2,272,128]{5,4,3,2,1,0:T(8,128)(2,1)}, bf16[3,8,2,2,272,128]{5,4,3,2,1,0:T(8,128)(2,1)}, u32[]{:S(2)}, u32[]{:S(2)}) collective-permute-start(bf16[3,8,2,2,272,128]{5,4,3,2,1,0:T(8,128)(2,1)} %pad_maximum_fusion.1.refs_0_), channel_id=1, source_target_pairs={{0,1},{1,0},{2,3},{3,2},{4,5},{5,4},{6,7},{7,6},{8,9},{9,8},{10,11... | collective-permute-start | bytes 20054024 | tf_op jit(solution)/shard_map/ppermute | solution.py:111
  192.9 27.5 %collective-permute-start.2 = (bf16[4,2,2,272,128]{4,3,2,1,0:T(8,128)(2,1)S(1)}, bf16[4,2,2,272,128]{4,3,2,1,0:T(8,128)(2,1)S(1)}, u32[]{:S(2)}, u32[]{:S(2)}) collective-permute-start(bf16[4,2,2,272,128]{4,3,2,1,0:T(8,128)(2,1)S(1)} %slice.85), channel_id=1, source_target_pairs={{0,2},{2,4},{4,6},{6,0},{1,3},{3,5},{5,7},{7,1},{8,10},{10,12},{12... | collective-permute-start | bytes 3342344 | tf_op jit(solution)/shard_map/ppermute | solution.py:111
  193.0 27.3 %collective-permute-start.4 = (bf16[4,2,2,272,128]{4,3,2,1,0:T(8,128)(2,1)S(1)}, bf16[4,2,2,272,128]{4,3,2,1,0:T(8,128)(2,1)}, u32[]{:S(2)}, u32[]{:S(2)}) collective-permute-start(bf16[4,2,2,272,128]{4,3,2,1,0:T(8,128)(2,1)S(1)} %slice.86), channel_id=1, source_target_pairs={{0,6},{2,0},{4,2},{6,4},{1,7},{3,1},{5,3},{7,5},{8,14},{10,8},{12,... | collective-permute-start | bytes 3342344 | tf_op jit(solution)/shard_map/ppermute | solution.py:111
  221.8 24.7 %copy-start.1 = (bf16[1,8,2,2,272,128]{5,4,3,2,1,0:T(8,128)(2,1)}, bf16[1,8,2,2,272,128]{5,4,3,2,1,0:T(8,128)(2,1)S(1)}, u32[]{:S(2)}) copy-start(bf16[1,8,2,2,272,128]{5,4,3,2,1,0:T(8,128)(2,1)S(1)} %maximum_bitcast_fusion.refs_1_) | copy-start | bytes 6684676
  221.8 39.3 %collective-permute-start.5 = (bf16[1,8,2,2,272,128]{5,4,3,2,1,0:T(8,128)(2,1)S(1)}, bf16[1,8,2,2,272,128]{5,4,3,2,1,0:T(8,128)(2,1)}, u32[]{:S(2)}, u32[]{:S(2)}) collective-permute-start(bf16[1,8,2,2,272,128]{5,4,3,2,1,0:T(8,128)(2,1)S(1)} %maximum_bitcast_fusion.refs_1_), channel_id=1, source_target_pairs={{0,1},{1,0},{2,3},{3,2},{4,5},{5,4},{6,7},{7,6},{8,9},{9,8},{10,11... | collective-permute-start | bytes 6684680 | tf_op jit(solution)/shard_map/ppermute | solution.py:111

commit v9 on v7

--- a/solution.py
+++ b/solution.py
@@ -121,10 +121,7 @@
     return jnp.stack([piece, from_above, far, from_below])
 
 
-def ring_gather(piece):
-    other = shift(piece, "xlo", 1)
-    first = lax.axis_index("xlo") == 0
-    bundle = jnp.where(first, jnp.stack([piece, other]), jnp.stack([other, piece]))
+def ring_gather(bundle):
     from_below = shift(bundle, "y", 1)
     from_above = shift(bundle, "y", -1)
     far_low = shift(from_below[:1], "y", 1)
@@ -152,20 +149,20 @@
     tagged = jnp.concatenate([weighted, band], axis=3)
     band_rows = rows + BAND
 
-    left = lax.all_to_all(tagged, ("xlo", "y"), split_axis=1, concat_axis=0, tiled=True)
-    left = left[:, 0]
-    first = lax.axis_index("xhi") == 0
-    other = shift(left, "xhi", 1)
-    left = jnp.where(first, jnp.stack([left, other], axis=1), jnp.stack([other, left], axis=1))
+    n_xhi = lax.axis_size("xhi")
+    n_xlo = lax.axis_size("xlo")
+    doubled = jnp.repeat(tagged, n_xhi, axis=1)
+    left = lax.all_to_all(doubled, ("xlo", "y", "xhi"), split_axis=1, concat_axis=0, tiled=True)
+    left = left.reshape(row_devices, n_xhi, slots, band_rows, width)
     left_own = z_ring(left)
-    right = lax.all_to_all(tagged, ("xhi", "z"), split_axis=1, concat_axis=1, tiled=True)
-    right_own = ring_gather(right[0])
+    doubled = jnp.concatenate([tagged] * n_xlo, axis=1)
+    right = lax.all_to_all(doubled, ("xlo", "xhi", "z"), split_axis=1, concat_axis=0, tiled=True)
+    right_own = ring_gather(right.reshape(n_xlo, chips, slots, band_rows, width))
     left_other = shift(left_own, "core", 1)
     right_other = shift(right_own, "core", 1)
 
     n_y = lax.axis_size("y")
     n_z = lax.axis_size("z")
-    n_xhi = lax.axis_size("xhi")
     me_y = lax.axis_index("y")
     me_z = lax.axis_index("z")
     me_xhi = lax.axis_index("xhi")

time: 224 us -> 221 us (0.987)
  blocking collectives: 25 us -> 0 us
  waiting for transfers between devices: 99.2 us -> 118 us
  other arithmetic: 27.6 us -> 23.5 us
  local copies, waits for them, and re-layouts: 8.33 us -> 12 us
    all_to_all x1 -> x2, waiting for transfers between devices: 10.4 us -> 54 us  [the longest x1 28.1 us: local(): lax.all_to_all(doubled, ('xlo', 'y', 'xhi'), split_axis=1, concat_axis=0,...]
    all_to_all x1 -> x0, blocking collectives: 25 us -> none  [local(): lax.all_to_all(tagged, ('xhi', 'z'), split_axis=1, concat_axis=1, tiled=T...]
    ppermute x12 -> x10, waiting for transfers between devices: 88.8 us -> 64.3 us  [shift(): return lax.ppermute(x, axis, [(i, (i + step) % n) for i in range(n)])]
    all_to_all x1 -> x2, starting transfers between devices: 4.31 us -> 16 us  [the longest x1 8.43 us: local(): lax.all_to_all(doubled, ('xlo', 'xhi', 'z'), split_axis=1, concat_axis=0,...]
    ppermute x12 -> x10, starting transfers between devices: 22.6 us -> 11.7 us  [shift(): return lax.ppermute(x, axis, [(i, (i + step) % n) for i in range(n)])]
    select_n x3 -> x0, other arithmetic: 5.54 us -> none  [the longest x2 5.34 us: ring_gather(): jnp.where(first, jnp.stack([piece, other]), jnp.stack([other, piece]))]
    broadcast_in_dim x0 -> x1, local copies, waits for them, and re-layouts: none -> 3.71 us  [local(): doubled = jnp.repeat(tagged, n_xhi, axis=1)]
  transfers between devices with their start and end apart: 13 -> 12, of which waited for: 7 -> 6; matrix products, arithmetic and copies ran while one was open for 13% -> 11% of each run, Pallas kernels for 8% -> 8%
where the time goes in v9:
time: 221 us; the launch traced here: 219 us
  waiting for transfers between devices  118 us (53%)
  Pallas kernels  37.3 us (17%)
  starting transfers between devices  27.7 us (13%)
  other arithmetic  23.5 us (11%)
  local copies, waits for them, and re-layouts  12 us (5%)
    ppermute x10, waiting for transfers between devices, shift(): return lax.ppermute(x, axis, [(i, (i + step) % n) for i in range(n)])  64.3 us
    pallas_call x2, Pallas kernels, accumulate(): pl.pallas_call(functools.partial(gram_kernel, slots, rows, width, n_chip,...  37.3 us
    all_to_all x1, waiting for transfers between devices, local(): lax.all_to_all(doubled, ('xlo', 'y', 'xhi'), split_axis=1, concat_axis=0,...  28.1 us
    all_to_all x1, waiting for transfers between devices, local(): lax.all_to_all(doubled, ('xlo', 'xhi', 'z'), split_axis=1, concat_axis=0,...  25.8 us
    ppermute x10, starting transfers between devices, shift(): return lax.ppermute(x, axis, [(i, (i + step) % n) for i in range(n)])  11.7 us
    all_to_all x1, starting transfers between devices, local(): lax.all_to_all(doubled, ('xlo', 'xhi', 'z'), split_axis=1, concat_axis=0,...  8.43 us
    all_to_all x1, starting transfers between devices, local(): lax.all_to_all(doubled, ('xlo', 'y', 'xhi'), split_axis=1, concat_axis=0,...  7.54 us
    another operation x2, other arithmetic, ring_gather(): return jnp.stack([bundle, from_above, far, from_below])  6.58 us
  transfers between devices with their start and end apart: 12, of which 6 were waited for; matrix products, arithmetic and copies ran while one was open for 11% of the time, Pallas kernels for 8%

profile of v9, /device:TPU:1, one launch (start us, length us, event | category | flops | bytes accessed | tf_op | source)
XLA Modules:
  0.0 219.1 jit_solution(412300829815691848)
XLA Ops:
  0.0 0.7 fusion.2
  0.7 0.7 fusion.5
  1.4 0.1 copy.66
  1.5 0.8 select_reduce_fusion
  2.3 0.1 broadcast_multiply_fusion
  2.4 0.1 broadcast.385
  2.5 1.7 multiply_convert_fusion
  4.2 1.7 maximum_maximum_fusion
  5.9 8.4 %all-to-all-start.1 = ((bf16[1,16,2,272,128]{4,3,2,0,1:T(8,128)(2,1)}), bf16[1,16,2,272,128]{4,3,2,0,1:T(8,128)(2,1)S(1)}, u32[]{:S(2)}, u32[]{:S(2)}) async-start(bf16[1,16,2,272,128]{4,3,2,0,1:T(8,128)(2,1)} %maximum_maximum_fusion), calls=%async_computation.1 | async-start | bytes 4456448 | tf_op jit(solution)/shard_map/all_to_all | solution.py:159
  14.3 1.1 maximum_bitcast_fusion.2
  15.4 25.8 %all-to-all-done.1 = bf16[1,16,2,272,128]{4,3,2,0,1:T(8,128)(2,1)S(1)} async-done(((bf16[1,16,2,272,128]{4,3,2,0,1:T(8,128)(2,1)}), bf16[1,16,2,272,128]{4,3,2,0,1:T(8,128)(2,1)S(1)}, u32[]{:S(2)}, u32[]{:S(2)}) %all-to-all-start.1) | async-done | bytes 2228256 | tf_op jit(solution)/shard_map/all_to_all | solution.py:159
  41.3 3.7 %broadcast_in_dim.43 = bf16[8,2,2,272,128]{4,3,2,1,0:T(8,128)(2,1)} broadcast(bf16[8,2,272,128]{3,2,1,0:T(8,128)(2,1)} %maximum_bitcast_fusion.2), dimensions={0,2,3,4} | broadcast | bytes 3342336 | tf_op jit(solution)/shard_map/broadcast_in_dim | solution.py:154
  45.0 7.5 %all-to-all-start = ((bf16[1,16,2,272,128]{4,3,2,0,1:T(8,128)(2,1)}), bf16[1,16,2,272,128]{4,3,2,0,1:T(8,128)(2,1)S(1)}, u32[]{:S(2)}, u32[]{:S(2)}) async-start(bf16[1,16,2,272,128]{4,3,2,0,1:T(8,128)(2,1)} %bitcast.48), calls=%async_computation | async-start | bytes 4456448 | tf_op jit(solution)/shard_map/all_to_all | solution.py:155
  52.5 1.4 collective-permute-start.6
  53.9 1.4 collective-permute-start.5
  55.3 28.1 %all-to-all-done = bf16[1,16,2,272,128]{4,3,2,0,1:T(8,128)(2,1)S(1)} async-done(((bf16[1,16,2,272,128]{4,3,2,0,1:T(8,128)(2,1)}), bf16[1,16,2,272,128]{4,3,2,0,1:T(8,128)(2,1)S(1)}, u32[]{:S(2)}, u32[]{:S(2)}) %all-to-all-start) | async-done | bytes 2228256 | tf_op jit(solution)/shard_map/all_to_all | solution.py:155
  83.4 0.3 collective-permute-start.1
  83.7 2.4 %collective-permute-start = (bf16[8,2,2,272,128]{4,3,2,1,0:T(8,128)(2,1)S(1)}, bf16[8,2,2,272,128]{4,3,2,1,0:T(8,128)(2,1)S(1)}, u32[]{:S(2)}, u32[]{:S(2)}) collective-permute-start(bf16[8,2,2,272,128]{4,3,2,1,0:T(8,128)(2,1)S(1)} %bitcast.43), channel_id=1, source_target_pairs={{0,6},{2,0},{4,2},{6,4},{1,7},{3,1},{5,3},{7,5},{8,14},{10,8},{12,... | collective-permute-start | bytes 6684680 | tf_op jit(solution)/shard_map/ppermute | solution.py:111
  86.1 41.7 %collective-permute-done.6 = bf16[2,8,2,272,128]{4,3,2,1,0:T(8,128)(2,1)} collective-permute-done((bf16[2,8,2,272,128]{4,3,2,1,0:T(8,128)(2,1)}, bf16[2,8,2,272,128]{4,3,2,1,0:T(8,128)(2,1)}, u32[]{:S(2)}, u32[]{:S(2)}) %collective-permute-start.6) | collective-permute-done | bytes 2228256 | tf_op jit(solution)/shard_map/ppermute | solution.py:111
  127.8 1.3 slice.72
  129.2 0.1 collective-permute-start.7
  129.2 1.9 collective-permute-done.5
  131.2 1.3 slice.73
  132.5 1.0 collective-permute-start.8
  133.5 0.1 slice.69
  133.6 0.3 collective-permute-start.2
  134.0 0.0 collective-permute-done
  134.0 0.1 slice.70
  134.0 2.5 %collective-permute-start.3 = (bf16[4,2,2,272,128]{4,3,2,1,0:T(8,128)(2,1)S(1)}, bf16[4,2,2,272,128]{4,3,2,1,0:T(8,128)(2,1)S(1)}, u32[]{:S(2)}, u32[]{:S(2)}) collective-permute-start(bf16[4,2,2,272,128]{4,3,2,1,0:T(8,128)(2,1)S(1)} %slice.70), channel_id=1, source_target_pairs={{0,6},{2,0},{4,2},{6,4},{1,7},{3,1},{5,3},{7,5},{8,14},{10,8},{12,... | collective-permute-start | bytes 3342344 | tf_op jit(solution)/shard_map/ppermute | solution.py:111
  136.5 19.0 %collective-permute-done.7 = bf16[1,8,2,272,128]{4,3,2,1,0:T(8,128)(2,1)S(1)} collective-permute-done((bf16[1,8,2,272,128]{4,3,2,1,0:T(8,128)(2,1)S(1)}, bf16[1,8,2,272,128]{4,3,2,1,0:T(8,128)(2,1)S(1)}, u32[]{:S(2)}, u32[]{:S(2)}) %collective-permute-start.7) | collective-permute-done | bytes 1114144 | tf_op jit(solution)/shard_map/ppermute | solution.py:111
  155.5 1.6 collective-permute-done.8
  157.2 0.2 maximum_bitcast_fusion.1
  157.4 6.4 %pad_maximum_fusion.1.refs_1_ = bf16[4,2,8,2,272,128]{5,4,3,2,1,0:T(8,128)(2,1)} fusion(bf16[1,2,8,2,272,128]{5,4,3,2,1,0:T(8,128)(2,1)} %bitcast.17, bf16[1,2,8,2,272,128]{5,4,3,2,1,0:T(8,128)(2,1)S(1)} %maximum_bitcast_fusion.1, bf16[1,2,8,2,272,128]{5,4,3,2,1,0:T(8,128)(2,1)} %bitcast.15, bf16[1,2,8,2,272,128]{5,4,3,2,1,0:T(8,128)(2,1)S(1)} %bitcast.47), kind=kLoop, calls=%fused_computation.5 | loop fusion | flops 13369344 | bytes 17825792 | tf_op jit(solution)/shard_map/stack | solution.py:130
  163.8 2.4 %collective-permute-start.9 = (bf16[4,2,8,2,272,128]{5,4,3,2,1,0:T(8,128)(2,1)}, bf16[4,2,8,2,272,128]{5,4,3,2,1,0:T(8,128)(2,1)}, u32[]{:S(2)}, u32[]{:S(2)}) collective-permute-start(bf16[4,2,8,2,272,128]{5,4,3,2,1,0:T(8,128)(2,1)} %pad_maximum_fusion.1.refs_1_), channel_id=1, source_target_pairs={{0,1},{1,0},{2,3},{3,2},{4,5},{5,4},{6,7},{7,6},{8,9},{9,8},{10,11... | collective-permute-start | bytes 26738696 | tf_op jit(solution)/shard_map/ppermute | solution.py:111
  166.1 0.2 maximum_bitcast_fusion
  166.3 4.1 %pad_maximum_fusion.refs_0_ = bf16[4,8,2,2,272,128]{5,4,3,2,1,0:T(8,128)(2,1)} fusion(bf16[1,8,2,2,272,128]{5,4,3,2,1,0:T(8,128)(2,1)S(1)} %bitcast.49, bf16[1,8,2,2,272,128]{5,4,3,2,1,0:T(8,128)(2,1)S(1)} %maximum_bitcast_fusion, bf16[1,8,2,2,272,128]{5,4,3,2,1,0:T(8,128)(2,1)S(1)} %bitcast.50, bf16[1,8,2,2,272,128]{5,4,3,2,1,0:T(8,128)(2,1)S(1)} %bitcast.44), kind=kLoop, calls=%fused_computation.4 | loop fusion | flops 13369344 | bytes 17825792 | tf_op jit(solution)/shard_map/stack | solution.py:121
  170.4 0.0 collective-permute-start.4
  170.5 0.7 pad_add_fusion.rot_ref
  171.2 1.0 slice_convert_fusion.1
  172.2 0.2 copy.74
  172.3 0.1 copy.75
  172.5 0.7 reshape.392.lids_ref
  173.2 1.0 fusion
  174.2 0.2 copy.76
  174.4 0.6 gather_fusion.2
  175.0 0.1 copy.79
  175.1 0.6 gather_fusion.3
  175.6 0.1 copy.80
  175.8 0.1 gather.21
  175.9 0.5 and_select_fusion.rids_ref
  176.4 17.0 %shard_map.58.refs_0_ = f32[2048,1024]{1,0:T(8,128)} custom-call(s32[128]{0:T(128)} %reshape.392.lids_ref, s32[128]{0:T(128)} %and_select_fusion.rids_ref, s32[3]{0:T(128)} %pad_add_fusion.rot_ref, bf16[4,8,2,2,272,128]{5,4,3,2,1,0:T(8,128)(2,1)} %pad_maximum_fusion.refs_0_, bf16[4,2,8,2,272,128]{5,4,3,2,1,0:T(8,128)(2,1)} %pad_maximum_fusion.1.refs_1_), custom_call_target="tpu_custom_call" | custom-call | flops 2147483648 | bytes 26214400 | tf_op jit(solution)/shard_map/pallas_call | solution.py:94
  193.5 1.0 fusion.1
  194.5 0.2 copy.69
  194.7 0.6 gather_fusion
  195.3 0.1 copy.72
  195.4 0.6 gather_fusion.1
  195.9 0.1 copy.73
  196.1 0.1 gather.18
  196.2 0.6 and_select_fusion.1.rids_ref
  196.8 1.0 slice_convert_fusion.3
  197.8 0.2 copy.67
  198.0 0.1 copy.68
  198.1 0.7 reshape.390.lids_ref
  198.8 20.3 %shard_map.59 = f32[2048,1024]{1,0:T(8,128)} custom-call(s32[128]{0:T(128)} %reshape.390.lids_ref, s32[128]{0:T(128)} %and_select_fusion.1.rids_ref, s32[3]{0:T(128)} %pad_add_fusion.rot_ref, f32[2048,1024]{1,0:T(8,128)} %shard_map.58.refs_0_, bf16[4,8,2,2,272,128]{5,4,3,2,1,0:T(8,128)(2,1)} %collective-permute-done.4.refs_1_, ...), custom_call_target="tpu_custom_call", output_to_operand_aliasing={{}: (3, {})} | custom-call | flops 2147483648 | bytes 26214400 | tf_op jit(solution)/shard_map/pallas_call | solution.py:94
  (18 shorter events, 0.1 us)
Async XLA Ops:
  5.9 35.4 %all-to-all-start.1 = ((bf16[1,16,2,272,128]{4,3,2,0,1:T(8,128)(2,1)}), bf16[1,16,2,272,128]{4,3,2,0,1:T(8,128)(2,1)S(1)}, u32[]{:S(2)}, u32[]{:S(2)}) async-start(bf16[1,16,2,272,128]{4,3,2,0,1:T(8,128)(2,1)} %maximum_maximum_fusion), calls=%async_computation.1 | async-start | bytes 4456448 | tf_op jit(solution)/shard_map/all_to_all | solution.py:159
  41.3 3.7 %copy-start = (bf16[1,16,2,272,128]{4,3,2,0,1:T(8,128)(2,1)}, bf16[1,16,2,272,128]{4,3,2,0,1:T(8,128)(2,1)S(1)}, u32[]{:S(2)}) copy-start(bf16[1,16,2,272,128]{4,3,2,0,1:T(8,128)(2,1)S(1)} %all-to-all-done.1) | copy-start | bytes 6684676
  45.0 38.4 %all-to-all-start = ((bf16[1,16,2,272,128]{4,3,2,0,1:T(8,128)(2,1)}), bf16[1,16,2,272,128]{4,3,2,0,1:T(8,128)(2,1)S(1)}, u32[]{:S(2)}, u32[]{:S(2)}) async-start(bf16[1,16,2,272,128]{4,3,2,0,1:T(8,128)(2,1)} %bitcast.48), calls=%async_computation | async-start | bytes 4456448 | tf_op jit(solution)/shard_map/all_to_all | solution.py:155
  52.5 75.3 %collective-permute-start.6 = (bf16[2,8,2,272,128]{4,3,2,1,0:T(8,128)(2,1)}, bf16[2,8,2,272,128]{4,3,2,1,0:T(8,128)(2,1)}, u32[]{:S(2)}, u32[]{:S(2)}) collective-permute-start(bf16[2,8,2,272,128]{4,3,2,1,0:T(8,128)(2,1)} %bitcast.45), channel_id=1, source_target_pairs={{0,16},{16,32},{32,48},{48,0},{1,17},{17,33},{33,49},{49,1},{2,18}... | collective-permute-start | bytes 6684680 | tf_op jit(solution)/shard_map/ppermute | solution.py:111
  53.9 77.3 %collective-permute-start.5 = (bf16[2,8,2,272,128]{4,3,2,1,0:T(8,128)(2,1)}, bf16[2,8,2,272,128]{4,3,2,1,0:T(8,128)(2,1)}, u32[]{:S(2)}, u32[]{:S(2)}) collective-permute-start(bf16[2,8,2,272,128]{4,3,2,1,0:T(8,128)(2,1)} %bitcast.46), channel_id=1, source_target_pairs={{0,48},{16,0},{32,16},{48,32},{1,49},{17,1},{33,17},{49,33},{2,50}... | collective-permute-start | bytes 6684680 | tf_op jit(solution)/shard_map/ppermute | solution.py:111
  83.4 50.1 %collective-permute-start.1 = (bf16[8,2,2,272,128]{4,3,2,1,0:T(8,128)(2,1)S(1)}, bf16[8,2,2,272,128]{4,3,2,1,0:T(8,128)(2,1)S(1)}, u32[]{:S(2)}, u32[]{:S(2)}) collective-permute-start(bf16[8,2,2,272,128]{4,3,2,1,0:T(8,128)(2,1)S(1)} %bitcast.42), channel_id=1, source_target_pairs={{0,2},{2,4},{4,6},{6,0},{1,3},{3,5},{5,7},{7,1},{8,10},{10,12},{12... | collective-permute-start | bytes 6684680 | tf_op jit(solution)/shard_map/ppermute | solution.py:111
  83.7 50.3 %collective-permute-start = (bf16[8,2,2,272,128]{4,3,2,1,0:T(8,128)(2,1)S(1)}, bf16[8,2,2,272,128]{4,3,2,1,0:T(8,128)(2,1)S(1)}, u32[]{:S(2)}, u32[]{:S(2)}) collective-permute-start(bf16[8,2,2,272,128]{4,3,2,1,0:T(8,128)(2,1)S(1)} %bitcast.43), channel_id=1, source_target_pairs={{0,6},{2,0},{4,2},{6,4},{1,7},{3,1},{5,3},{7,5},{8,14},{10,8},{12,... | collective-permute-start | bytes 6684680 | tf_op jit(solution)/shard_map/ppermute | solution.py:111
  129.2 26.4 %collective-permute-start.7 = (bf16[1,8,2,272,128]{4,3,2,1,0:T(8,128)(2,1)S(1)}, bf16[1,8,2,272,128]{4,3,2,1,0:T(8,128)(2,1)S(1)}, u32[]{:S(2)}, u32[]{:S(2)}) collective-permute-start(bf16[1,8,2,272,128]{4,3,2,1,0:T(8,128)(2,1)S(1)} %slice.72), channel_id=1, source_target_pairs={{0,16},{16,32},{32,48},{48,0},{1,17},{17,33},{33,49},{49,1},{2,18}... | collective-permute-start | bytes 3342344 | tf_op jit(solution)/shard_map/ppermute | solution.py:111
  132.5 24.7 %collective-permute-start.8 = (bf16[1,8,2,272,128]{4,3,2,1,0:T(8,128)(2,1)S(1)}, bf16[1,8,2,272,128]{4,3,2,1,0:T(8,128)(2,1)S(1)}, u32[]{:S(2)}, u32[]{:S(2)}) collective-permute-start(bf16[1,8,2,272,128]{4,3,2,1,0:T(8,128)(2,1)S(1)} %slice.73), channel_id=1, source_target_pairs={{0,48},{16,0},{32,16},{48,32},{1,49},{17,1},{33,17},{49,33},{2,50}... | collective-permute-start | bytes 3342344 | tf_op jit(solution)/shard_map/ppermute | solution.py:111
  133.6 32.5 %collective-permute-start.2 = (bf16[4,2,2,272,128]{4,3,2,1,0:T(8,128)(2,1)S(1)}, bf16[4,2,2,272,128]{4,3,2,1,0:T(8,128)(2,1)S(1)}, u32[]{:S(2)}, u32[]{:S(2)}) collective-permute-start(bf16[4,2,2,272,128]{4,3,2,1,0:T(8,128)(2,1)S(1)} %slice.69), channel_id=1, source_target_pairs={{0,2},{2,4},{4,6},{6,0},{1,3},{3,5},{5,7},{7,1},{8,10},{10,12},{12... | collective-permute-start | bytes 3342344 | tf_op jit(solution)/shard_map/ppermute | solution.py:111
  134.0 23.3 %copy-start.1 = (bf16[1,16,2,272,128]{4,3,2,0,1:T(8,128)(2,1)S(1)}, bf16[1,16,2,272,128]{4,3,2,0,1:T(8,128)(2,1)}, u32[]{:S(2)}) copy-start(bf16[1,16,2,272,128]{4,3,2,0,1:T(8,128)(2,1)} %copy-done) | copy-start | bytes 6684676
  134.0 32.1 %collective-permute-start.3 = (bf16[4,2,2,272,128]{4,3,2,1,0:T(8,128)(2,1)S(1)}, bf16[4,2,2,272,128]{4,3,2,1,0:T(8,128)(2,1)S(1)}, u32[]{:S(2)}, u32[]{:S(2)}) collective-permute-start(bf16[4,2,2,272,128]{4,3,2,1,0:T(8,128)(2,1)S(1)} %slice.70), channel_id=1, source_target_pairs={{0,6},{2,0},{4,2},{6,4},{1,7},{3,1},{5,3},{7,5},{8,14},{10,8},{12,... | collective-permute-start | bytes 3342344 | tf_op jit(solution)/shard_map/ppermute | solution.py:111
  163.8 29.7 %collective-permute-start.9 = (bf16[4,2,8,2,272,128]{5,4,3,2,1,0:T(8,128)(2,1)}, bf16[4,2,8,2,272,128]{5,4,3,2,1,0:T(8,128)(2,1)}, u32[]{:S(2)}, u32[]{:S(2)}) collective-permute-start(bf16[4,2,8,2,272,128]{5,4,3,2,1,0:T(8,128)(2,1)} %pad_maximum_fusion.1.refs_1_), channel_id=1, source_target_pairs={{0,1},{1,0},{2,3},{3,2},{4,5},{5,4},{6,7},{7,6},{8,9},{9,8},{10,11... | collective-permute-start | bytes 26738696 | tf_op jit(solution)/shard_map/ppermute | solution.py:111
  170.4 26.4 %collective-permute-start.4 = (bf16[4,8,2,2,272,128]{5,4,3,2,1,0:T(8,128)(2,1)}, bf16[4,8,2,2,272,128]{5,4,3,2,1,0:T(8,128)(2,1)}, u32[]{:S(2)}, u32[]{:S(2)}) collective-permute-start(bf16[4,8,2,2,272,128]{5,4,3,2,1,0:T(8,128)(2,1)} %pad_maximum_fusion.refs_0_), channel_id=1, source_target_pairs={{0,1},{1,0},{2,3},{3,2},{4,5},{5,4},{6,7},{7,6},{8,9},{9,8},{10,11... | collective-permute-start | bytes 26738696 | tf_op jit(solution)/shard_map/ppermute | solution.py:111

commit v10 on v9

v10 whole, which is shorter than its diff:
```python
import functools

import jax
import jax.numpy as jnp
from jax import lax
from jax.experimental import pallas as pl
from jax.experimental.pallas import tpu as pltpu
from jax.sharding import PartitionSpec as P

TILES = 128
BAND = 16


def station_scale(weight_class):
    levels = jnp.array([1.0, 0.5, 0.25, 0.125], jnp.float32)
    hits = weight_class[..., None] == jnp.arange(4, dtype=jnp.int32)
    return jnp.sum(jnp.where(hits, levels, jnp.float32(0.0)), axis=-1)


def gram_kernel(slots, rows, width, group, lids_ref, rids_ref, rot_ref,
                left_own, right_own, left_other, right_other, out_ref):
    h = pl.program_id(0)
    r = pl.program_id(1)

    @pl.when((h == 0) & (r == 0))
    def _():
        out_ref[...] = jnp.zeros_like(out_ref)

    n_z = left_own.shape[0]
    n_xhi = left_own.shape[1]

    def run(left_ref, right_ref):
        def body(k, carry):
            b = (h * pl.num_programs(1) + r) * group + k
            z_rel = k // n_xhi
            x_abs = lax.rem(k, n_xhi)
            chip = x_abs * n_z + lax.rem(rot_ref[2] + z_rel, n_z)
            lids = [lids_ref[b * slots + i] for i in range(slots)]
            rids = [rids_ref[b * slots + j] for j in range(slots)]
            any_left = functools.reduce(jnp.logical_or, [li >= 0 for li in lids])
            any_right = functools.reduce(jnp.logical_or, [rj >= 0 for rj in rids])

            @pl.when(any_left & any_right)
            def _():
                lhs = jnp.concatenate([left_ref[z_rel, x_abs, i, :rows, :] for i in range(slots)], axis=1)
                rhs = jnp.concatenate([right_ref[chip, j, :rows, :] for j in range(slots)], axis=1)
                gram = lax.dot_general(
                    lhs, rhs, (((0,), (0,)), ((), ())), preferred_element_type=jnp.float32
                )
                for i in range(slots):
                    for j in range(slots):

                        @pl.when((lids[i] >= 0) & (rids[j] >= 0))
                        def _():
                            out_rows = pl.ds(pl.multiple_of(lids[i] * width, width), width)
                            out_cols = pl.ds(pl.multiple_of(rids[j] * width, width), width)
                            out_ref[out_rows, out_cols] += gram[i * width:(i + 1) * width, j * width:(j + 1) * width]

            return carry

        lax.fori_loop(0, group, body, 0)

    @pl.when(h == 0)
    def _():
        run(left_own, right_own)

    @pl.when(h == 1)
    def _():
        run(left_other, right_other)


def accumulate(left_own, right_own, left_other, right_other, left_ids, right_ids, rot, rows, per_row, per_col):
    n_z, n_row, n_xhi, slots, band_rows, width = left_own.shape
    n_chip = n_xhi * n_z
    n_y = right_own.shape[0]
    last = n_row - 1
    out_shape = (per_row * width, per_col * width)

    def right_block(r, rot):
        return (lax.rem(lax.rem(r, n_y) - rot[0] + n_y, n_y), r // n_y, 0, 0, 0, 0)

    left_block = (n_z, None, n_xhi, slots, band_rows, width)
    right_spec = (None, None, n_chip, slots, band_rows, width)
    in_specs = [
        pl.BlockSpec(left_block, lambda h, r, lids, rids, rot: (0, jnp.where(h == 0, r, last), 0, 0, 0, 0)),
        pl.BlockSpec(right_spec, lambda h, r, lids, rids, rot: right_block(jnp.where(h == 0, r, last), rot)),
        pl.BlockSpec(left_block, lambda h, r, lids, rids, rot: (0, jnp.where(h == 0, 0, r), 0, 0, 0, 0)),
        pl.BlockSpec(right_spec, lambda h, r, lids, rids, rot: right_block(jnp.where(h == 0, 0, r), rot)),
    ]
    grid_spec = pltpu.PrefetchScalarGridSpec(
        num_scalar_prefetch=3,
        grid=(2, n_row),
        in_specs=in_specs,
        out_specs=pl.BlockSpec(out_shape, lambda h, r, lids, rids, rot: (0, 0)),
    )
    stations = 2 * n_row * n_chip
    flops = 2 * stations * slots * slots * rows * width * width
    return pl.pallas_call(
        functools.partial(gram_kernel, slots, rows, width, n_chip),
        grid_spec=grid_spec,
        out_shape=jax.ShapeDtypeStruct(out_shape, jnp.float32),
        compiler_params=pltpu.CompilerParams(
            dimension_semantics=("arbitrary", "arbitrary"), vmem_limit_bytes=56 * 1024 * 1024
        ),
        cost_estimate=pl.CostEstimate(
            flops=flops,
            bytes_accessed=4 * right_own.size * 2 + per_row * per_col * width * width * 4,
            transcendentals=0,
        ),
    )(left_ids.reshape(-1), right_ids.reshape(-1), rot, left_own, right_own, left_other, right_other)


def shift(x, axis, step):
    n = lax.axis_size(axis)
    return lax.ppermute(x, axis, [(i, (i + step) % n) for i in range(n)])


def z_ring(piece):
    from_above = shift(piece, "z", -1)
    from_below = shift(piece, "z", 1)
    half = piece.shape[0] // 2
    far_low = shift(from_below[:half], "z", 1)
    far_high = shift(from_above[half:], "z", -1)
    far = jnp.concatenate([far_low, far_high], axis=0)
    return jnp.stack([piece, from_above, far, from_below])


def ring_gather(bundle):
    from_below = shift(bundle, "y", 1)
    from_above = shift(bundle, "y", -1)
    far_low = shift(from_below[:1], "y", 1)
    far_high = shift(from_above[1:], "y", -1)
    far = jnp.concatenate([far_low, far_high], axis=0)
    return jnp.stack([bundle, from_above, far, from_below])


def local(sensitivity, tile_ids, counts, weight_class):
    row_devices = lax.axis_size("xlo") * lax.axis_size("y")
    chips = lax.axis_size("xhi") * lax.axis_size("z")
    cores = lax.axis_size("core")
    me_core = lax.axis_index("core")
    blocks, owners, slots, rows, width = sensitivity.shape
    per_row = TILES // row_devices
    per_col = per_row // cores
    live = jnp.arange(slots, dtype=jnp.int32)[None, None, :] < counts[:, :, None]
    factor = station_scale(weight_class)[:, None, None, :, None] * live[:, :, :, None, None].astype(
        jnp.float32
    )
    weighted = (sensitivity.astype(jnp.float32) * factor).astype(jnp.bfloat16)
    live_ids = jnp.where(live, tile_ids, -1).astype(jnp.bfloat16)
    band = jnp.zeros((blocks, owners, slots, BAND, width), jnp.bfloat16)
    band = band.at[:, :, :, 0, :].set(live_ids[..., None])
    tagged = jnp.concatenate([weighted, band], axis=3)
    band_rows = rows + BAND

    n_xhi = lax.axis_size("xhi")
    n_xlo = lax.axis_size("xlo")
    doubled = jnp.repeat(tagged, n_xhi, axis=1)
    left = lax.all_to_all(doubled, ("xlo", "y", "xhi"), split_axis=1, concat_axis=0, tiled=True)
    left = left.reshape(row_devices, n_xhi, slots, band_rows, width)
    left_own = z_ring(left)
    doubled = jnp.concatenate([tagged] * n_xlo, axis=1)
    right = lax.all_to_all(doubled, ("xlo", "xhi", "z"), split_axis=1, concat_axis=0, tiled=True)
    right_own = ring_gather(right.reshape(n_xlo, chips, slots, band_rows, width))
    left_other = shift(left_own, "core", 1)
    right_other = shift(right_own, "core", 1)

    n_y = lax.axis_size("y")
    n_z = lax.axis_size("z")
    me_y = lax.axis_index("y")
    me_z = lax.axis_index("z")
    me_xhi = lax.axis_index("xhi")
    absolute_y = (jnp.arange(n_y, dtype=jnp.int32) - me_y) % n_y
    k_rel = jnp.arange(n_xhi * n_z, dtype=jnp.int32)
    chip_of = (k_rel % n_xhi) * n_z + (me_z + k_rel // n_xhi) % n_z

    def ids(left_half, right_half):
        left_ids = left_half[:, :, :, :, rows, 0].astype(jnp.int32)
        left_ids = jnp.transpose(left_ids, (1, 0, 2, 3))
        right_ids = right_half[:, :, :, :, rows, 0].astype(jnp.int32) - me_core * per_col
        right_ids = jnp.transpose(right_ids[absolute_y], (1, 0, 2, 3)).reshape(row_devices, chips, slots)
        right_ids = right_ids[:, chip_of]
        right_ids = jnp.where((right_ids >= 0) & (right_ids < per_col), right_ids, -1)
        return left_ids, right_ids

    own_left_ids, own_right_ids = ids(left_own, right_own)
    other_left_ids, other_right_ids = ids(left_other, right_other)
    left_ids = jnp.stack([own_left_ids, other_left_ids])
    right_ids = jnp.stack([own_right_ids, other_right_ids])
    rot = jnp.stack([me_y, me_xhi, me_z]).astype(jnp.int32)
    return accumulate(
        left_own, right_own, left_other, right_other, left_ids, right_ids, rot, rows, per_row, per_col
    )

def solution(mesh):
    row_devices, col_devices = mesh.devices.shape
    cores = 2
    x_lo = 2
    x_hi = 2
    mesh3 = jax.sharding.Mesh(
        mesh.devices.reshape(x_lo, row_devices // x_lo, x_hi, col_devices // cores // x_hi, cores),
        ("xlo", "y", "xhi", "z", "core"),
    )
    blocks = ("xlo", "y", "xhi", "z", "core")
    in_specs = (
        P(blocks, None, None, None, None),
        P(blocks, None, None),
        P(blocks, None),
        P(blocks, None),
    )
    out_specs = P(("xlo", "y"), ("xhi", "z", "core"))
    return jax.shard_map(local, mesh=mesh3, in_specs=in_specs, out_specs=out_specs, check_vma=False)
```

time: 221 us -> 224 us (1.014)
  waiting for transfers between devices: 118 us -> 133 us
  Pallas kernels: 37.3 us -> 28.1 us
  other arithmetic: 23.5 us -> 20.3 us
    ppermute x10, waiting for transfers between devices: 64.3 us -> 79 us  [shift(): return lax.ppermute(x, axis, [(i, (i + step) % n) for i in range(n)])]
    pallas_call x2 -> x1, Pallas kernels: 37.3 us -> 28.1 us  [accumulate(): pl.pallas_call(functools.partial(gram_kernel, slots, rows, width, n_chip)...]
    slice x0 -> x4, local copies, waits for them, and re-layouts: none -> 2.34 us  [ids(): left_ids = left_half[:, :, :, :, rows, 0].astype(jnp.int32)]
  transfers between devices with their start and end apart: 12 -> 12, of which waited for: 6 -> 8; matrix products, arithmetic and copies ran while one was open for 11% -> 10% of each run, Pallas kernels for 8% -> 0%
where the time goes in v10:
time: 224 us; the launch traced here: 223 us
  waiting for transfers between devices  133 us (59%)
  Pallas kernels  28.1 us (13%)
  starting transfers between devices  27.7 us (12%)
  other arithmetic  20.3 us (9%)
  local copies, waits for them, and re-layouts  13.8 us (6%)
    ppermute x10, waiting for transfers between devices, shift(): return lax.ppermute(x, axis, [(i, (i + step) % n) for i in range(n)])  79 us
    all_to_all x1, waiting for transfers between devices, local(): lax.all_to_all(doubled, ('xlo', 'y', 'xhi'), split_axis=1, concat_axis=0,...  28.1 us
    pallas_call x1, Pallas kernels, accumulate(): pl.pallas_call(functools.partial(gram_kernel, slots, rows, width, n_chip)...  28.1 us
    all_to_all x1, waiting for transfers between devices, local(): lax.all_to_all(doubled, ('xlo', 'xhi', 'z'), split_axis=1, concat_axis=0,...  25.9 us
    ppermute x10, starting transfers between devices, shift(): return lax.ppermute(x, axis, [(i, (i + step) % n) for i in range(n)])  11.7 us
    all_to_all x1, starting transfers between devices, local(): lax.all_to_all(doubled, ('xlo', 'xhi', 'z'), split_axis=1, concat_axis=0,...  8.43 us
    all_to_all x1, starting transfers between devices, local(): lax.all_to_all(doubled, ('xlo', 'y', 'xhi'), split_axis=1, concat_axis=0,...  7.54 us
    another operation x2, other arithmetic, ring_gather(): return jnp.stack([bundle, from_above, far, from_below])  6.59 us
  transfers between devices with their start and end apart: 12, of which 8 were waited for; matrix products, arithmetic and copies ran while one was open for 10% of the time, Pallas kernels for 0%

profile of v10, /device:TPU:1, one launch (start us, length us, event | category | flops | bytes accessed | tf_op | source)
XLA Modules:
  0.0 223.0 jit_solution(17396973360524467097)
XLA Ops:
  0.0 0.7 fusion.4
  0.7 0.7 fusion.7
  1.4 0.1 copy.61
  1.5 0.8 select_reduce_fusion
  2.3 0.1 broadcast_multiply_fusion
  2.4 0.1 broadcast.421
  2.5 1.7 multiply_convert_fusion
  4.2 1.7 maximum_maximum_fusion
  5.9 8.4 %all-to-all-start.1 = ((bf16[1,16,2,272,128]{4,3,2,0,1:T(8,128)(2,1)}), bf16[1,16,2,272,128]{4,3,2,0,1:T(8,128)(2,1)S(1)}, u32[]{:S(2)}, u32[]{:S(2)}) async-start(bf16[1,16,2,272,128]{4,3,2,0,1:T(8,128)(2,1)} %maximum_maximum_fusion), calls=%async_computation.1 | async-start | bytes 4456448 | tf_op jit(solution)/shard_map/all_to_all | solution.py:163
  14.3 1.1 maximum_bitcast_fusion.2
  15.4 25.9 %all-to-all-done.1 = bf16[1,16,2,272,128]{4,3,2,0,1:T(8,128)(2,1)S(1)} async-done(((bf16[1,16,2,272,128]{4,3,2,0,1:T(8,128)(2,1)}), bf16[1,16,2,272,128]{4,3,2,0,1:T(8,128)(2,1)S(1)}, u32[]{:S(2)}, u32[]{:S(2)}) %all-to-all-start.1) | async-done | bytes 2228256 | tf_op jit(solution)/shard_map/all_to_all | solution.py:163
  41.3 3.7 %broadcast_in_dim.43 = bf16[8,2,2,272,128]{4,3,2,1,0:T(8,128)(2,1)} broadcast(bf16[8,2,272,128]{3,2,1,0:T(8,128)(2,1)} %maximum_bitcast_fusion.2), dimensions={0,2,3,4} | broadcast | bytes 3342336 | tf_op jit(solution)/shard_map/broadcast_in_dim | solution.py:158
  45.0 7.5 %all-to-all-start = ((bf16[1,16,2,272,128]{4,3,2,0,1:T(8,128)(2,1)}), bf16[1,16,2,272,128]{4,3,2,0,1:T(8,128)(2,1)S(1)}, u32[]{:S(2)}, u32[]{:S(2)}) async-start(bf16[1,16,2,272,128]{4,3,2,0,1:T(8,128)(2,1)} %bitcast.74), calls=%async_computation | async-start | bytes 4456448 | tf_op jit(solution)/shard_map/all_to_all | solution.py:159
  52.5 1.4 collective-permute-start.6
  53.9 1.4 collective-permute-start.5
  55.3 28.1 %all-to-all-done = bf16[1,16,2,272,128]{4,3,2,0,1:T(8,128)(2,1)S(1)} async-done(((bf16[1,16,2,272,128]{4,3,2,0,1:T(8,128)(2,1)}), bf16[1,16,2,272,128]{4,3,2,0,1:T(8,128)(2,1)S(1)}, u32[]{:S(2)}, u32[]{:S(2)}) %all-to-all-start) | async-done | bytes 2228256 | tf_op jit(solution)/shard_map/all_to_all | solution.py:159
  83.4 0.3 collective-permute-start.1
  83.7 2.4 %collective-permute-start = (bf16[8,2,2,272,128]{4,3,2,1,0:T(8,128)(2,1)S(1)}, bf16[8,2,2,272,128]{4,3,2,1,0:T(8,128)(2,1)S(1)}, u32[]{:S(2)}, u32[]{:S(2)}) collective-permute-start(bf16[8,2,2,272,128]{4,3,2,1,0:T(8,128)(2,1)S(1)} %bitcast.69), channel_id=1, source_target_pairs={{0,6},{2,0},{4,2},{6,4},{1,7},{3,1},{5,3},{7,5},{8,14},{10,8},{12,... | collective-permute-start | bytes 6684680 | tf_op jit(solution)/shard_map/ppermute | solution.py:115
  86.1 41.7 %collective-permute-done.6 = bf16[2,8,2,272,128]{4,3,2,1,0:T(8,128)(2,1)} collective-permute-done((bf16[2,8,2,272,128]{4,3,2,1,0:T(8,128)(2,1)}, bf16[2,8,2,272,128]{4,3,2,1,0:T(8,128)(2,1)}, u32[]{:S(2)}, u32[]{:S(2)}) %collective-permute-start.6) | collective-permute-done | bytes 2228256 | tf_op jit(solution)/shard_map/ppermute | solution.py:115
  127.8 1.3 slice.73
  129.2 0.1 collective-permute-start.7
  129.2 1.9 collective-permute-done.5
  131.2 1.3 slice.74
  132.5 1.0 collective-permute-start.8
  133.5 0.0 collective-permute-done.1
  133.5 0.1 slice.69
  133.6 0.3 collective-permute-start.2
  134.0 0.0 collective-permute-done
  134.0 0.1 slice.70
  134.0 2.5 %collective-permute-start.3 = (bf16[4,2,2,272,128]{4,3,2,1,0:T(8,128)(2,1)S(1)}, bf16[4,2,2,272,128]{4,3,2,1,0:T(8,128)(2,1)S(1)}, u32[]{:S(2)}, u32[]{:S(2)}) collective-permute-start(bf16[4,2,2,272,128]{4,3,2,1,0:T(8,128)(2,1)S(1)} %slice.70), channel_id=1, source_target_pairs={{0,6},{2,0},{4,2},{6,4},{1,7},{3,1},{5,3},{7,5},{8,14},{10,8},{12,... | collective-permute-start | bytes 3342344 | tf_op jit(solution)/shard_map/ppermute | solution.py:115
  136.5 19.0 %collective-permute-done.7 = bf16[1,8,2,272,128]{4,3,2,1,0:T(8,128)(2,1)S(1)} collective-permute-done((bf16[1,8,2,272,128]{4,3,2,1,0:T(8,128)(2,1)S(1)}, bf16[1,8,2,272,128]{4,3,2,1,0:T(8,128)(2,1)S(1)}, u32[]{:S(2)}, u32[]{:S(2)}) %collective-permute-start.7) | collective-permute-done | bytes 1114144 | tf_op jit(solution)/shard_map/ppermute | solution.py:115
  155.5 1.6 collective-permute-done.8
  157.2 0.2 maximum_bitcast_fusion.1
  157.4 6.4 %pad_maximum_fusion.1.right_own = bf16[4,2,8,2,272,128]{5,4,3,2,1,0:T(8,128)(2,1)} fusion(bf16[1,2,8,2,272,128]{5,4,3,2,1,0:T(8,128)(2,1)} %bitcast.21, bf16[1,2,8,2,272,128]{5,4,3,2,1,0:T(8,128)(2,1)S(1)} %maximum_bitcast_fusion.1, bf16[1,2,8,2,272,128]{5,4,3,2,1,0:T(8,128)(2,1)} %bitcast.19, bf16[1,2,8,2,272,128]{5,4,3,2,1,0:T(8,128)(2,1)S(1)} %bitcast.73), kind=kLoop, calls=%fused_computation.5 | loop fusion | flops 13369344 | bytes 17825792 | tf_op jit(solution)/shard_map/stack | solution.py:134
  163.8 2.4 %collective-permute-start.9 = (bf16[4,2,8,2,272,128]{5,4,3,2,1,0:T(8,128)(2,1)}, bf16[4,2,8,2,272,128]{5,4,3,2,1,0:T(8,128)(2,1)}, u32[]{:S(2)}, u32[]{:S(2)}) collective-permute-start(bf16[4,2,8,2,272,128]{5,4,3,2,1,0:T(8,128)(2,1)} %pad_maximum_fusion.1.right_own), channel_id=1, source_target_pairs={{0,1},{1,0},{2,3},{3,2},{4,5},{5,4},{6,7},{7,6},{8,9},{9,8},{10,11... | collective-permute-start | bytes 26738696 | tf_op jit(solution)/shard_map/ppermute | solution.py:115
  166.1 0.0 collective-permute-done.2
  166.2 0.0 collective-permute-done.3
  166.2 0.2 maximum_bitcast_fusion
  166.4 4.0 %pad_maximum_fusion.left_own = bf16[4,8,2,2,272,128]{5,4,3,2,1,0:T(8,128)(2,1)} fusion(bf16[1,8,2,2,272,128]{5,4,3,2,1,0:T(8,128)(2,1)S(1)} %bitcast.75, bf16[1,8,2,2,272,128]{5,4,3,2,1,0:T(8,128)(2,1)S(1)} %maximum_bitcast_fusion, bf16[1,8,2,2,272,128]{5,4,3,2,1,0:T(8,128)(2,1)S(1)} %bitcast.76, bf16[1,8,2,2,272,128]{5,4,3,2,1,0:T(8,128)(2,1)S(1)} %bitcast.70), kind=kLoop, calls=%fused_computation.4 | loop fusion | flops 13369344 | bytes 17825792 | tf_op jit(solution)/shard_map/stack | solution.py:125
  170.4 0.0 collective-permute-start.4
  170.4 0.6 pad_add_fusion.1.rot_ref
  171.0 1.0 slice.71
  172.0 0.2 copy.62
  172.2 1.0 fusion.1
  173.2 0.2 copy.65
  173.4 0.6 gather_fusion
  174.0 0.1 copy.68
  174.1 0.6 gather_fusion.1
  174.7 0.1 copy.69
  174.7 5.3 %collective-permute-done.9.right_other = bf16[4,2,8,2,272,128]{5,4,3,2,1,0:T(8,128)(2,1)} collective-permute-done((bf16[4,2,8,2,272,128]{5,4,3,2,1,0:T(8,128)(2,1)}, bf16[4,2,8,2,272,128]{5,4,3,2,1,0:T(8,128)(2,1)}, u32[]{:S(2)}, u32[]{:S(2)}) %collective-permute-start.9) | collective-permute-done | bytes 8912928 | tf_op jit(solution)/shard_map/ppermute | solution.py:115
  180.0 1.0 fusion
  181.0 0.2 copy.70
  181.2 0.6 gather_fusion.2
  181.8 0.1 copy.73
  181.9 0.6 gather_fusion.3
  182.5 0.1 copy.74
  182.6 0.2 copy.75
  182.7 0.7 reshape.413.rids_ref
  183.4 9.4 %collective-permute-done.4.left_other = bf16[4,8,2,2,272,128]{5,4,3,2,1,0:T(8,128)(2,1)} collective-permute-done((bf16[4,8,2,2,272,128]{5,4,3,2,1,0:T(8,128)(2,1)}, bf16[4,8,2,2,272,128]{5,4,3,2,1,0:T(8,128)(2,1)}, u32[]{:S(2)}, u32[]{:S(2)}) %collective-permute-start.4) | collective-permute-done | bytes 8912928 | tf_op jit(solution)/shard_map/ppermute | solution.py:115
  192.8 1.0 slice.72
  193.8 0.2 copy.63
  194.0 0.2 copy.64
  194.1 0.7 reshape.415.lids_ref
  194.9 28.1 %shard_map.58 = f32[2048,1024]{1,0:T(8,128)} custom-call(s32[256]{0:T(256)} %reshape.415.lids_ref, s32[256]{0:T(256)} %reshape.413.rids_ref, s32[3]{0:T(128)} %pad_add_fusion.1.rot_ref, bf16[4,8,2,2,272,128]{5,4,3,2,1,0:T(8,128)(2,1)} %pad_maximum_fusion.left_own, bf16[4,2,8,2,272,128]{5,4,3,2,1,0:T(8,128)(2,1)} %pad_maximum_fusion.1.right_own, ...), custom_call_target="tpu_custom_call" | custom-call | flops 4294967296 | bytes 44040192 | tf_op jit(solution)/shard_map/pallas_call | solution.py:98
  (16 shorter events, 0.1 us)
Async XLA Ops:
  5.9 35.4 %all-to-all-start.1 = ((bf16[1,16,2,272,128]{4,3,2,0,1:T(8,128)(2,1)}), bf16[1,16,2,272,128]{4,3,2,0,1:T(8,128)(2,1)S(1)}, u32[]{:S(2)}, u32[]{:S(2)}) async-start(bf16[1,16,2,272,128]{4,3,2,0,1:T(8,128)(2,1)} %maximum_maximum_fusion), calls=%async_computation.1 | async-start | bytes 4456448 | tf_op jit(solution)/shard_map/all_to_all | solution.py:163
  41.3 3.7 %copy-start = (bf16[1,16,2,272,128]{4,3,2,0,1:T(8,128)(2,1)}, bf16[1,16,2,272,128]{4,3,2,0,1:T(8,128)(2,1)S(1)}, u32[]{:S(2)}) copy-start(bf16[1,16,2,272,128]{4,3,2,0,1:T(8,128)(2,1)S(1)} %all-to-all-done.1) | copy-start | bytes 6684676
  45.0 38.4 %all-to-all-start = ((bf16[1,16,2,272,128]{4,3,2,0,1:T(8,128)(2,1)}), bf16[1,16,2,272,128]{4,3,2,0,1:T(8,128)(2,1)S(1)}, u32[]{:S(2)}, u32[]{:S(2)}) async-start(bf16[1,16,2,272,128]{4,3,2,0,1:T(8,128)(2,1)} %bitcast.74), calls=%async_computation | async-start | bytes 4456448 | tf_op jit(solution)/shard_map/all_to_all | solution.py:159
  52.5 75.3 %collective-permute-start.6 = (bf16[2,8,2,272,128]{4,3,2,1,0:T(8,128)(2,1)}, bf16[2,8,2,272,128]{4,3,2,1,0:T(8,128)(2,1)}, u32[]{:S(2)}, u32[]{:S(2)}) collective-permute-start(bf16[2,8,2,272,128]{4,3,2,1,0:T(8,128)(2,1)} %bitcast.71), channel_id=1, source_target_pairs={{0,16},{16,32},{32,48},{48,0},{1,17},{17,33},{33,49},{49,1},{2,18}... | collective-permute-start | bytes 6684680 | tf_op jit(solution)/shard_map/ppermute | solution.py:115
  53.9 77.3 %collective-permute-start.5 = (bf16[2,8,2,272,128]{4,3,2,1,0:T(8,128)(2,1)}, bf16[2,8,2,272,128]{4,3,2,1,0:T(8,128)(2,1)}, u32[]{:S(2)}, u32[]{:S(2)}) collective-permute-start(bf16[2,8,2,272,128]{4,3,2,1,0:T(8,128)(2,1)} %bitcast.72), channel_id=1, source_target_pairs={{0,48},{16,0},{32,16},{48,32},{1,49},{17,1},{33,17},{49,33},{2,50}... | collective-permute-start | bytes 6684680 | tf_op jit(solution)/shard_map/ppermute | solution.py:115
  83.4 50.1 %collective-permute-start.1 = (bf16[8,2,2,272,128]{4,3,2,1,0:T(8,128)(2,1)S(1)}, bf16[8,2,2,272,128]{4,3,2,1,0:T(8,128)(2,1)S(1)}, u32[]{:S(2)}, u32[]{:S(2)}) collective-permute-start(bf16[8,2,2,272,128]{4,3,2,1,0:T(8,128)(2,1)S(1)} %bitcast.68), channel_id=1, source_target_pairs={{0,2},{2,4},{4,6},{6,0},{1,3},{3,5},{5,7},{7,1},{8,10},{10,12},{12... | collective-permute-start | bytes 6684680 | tf_op jit(solution)/shard_map/ppermute | solution.py:115
  83.7 50.3 %collective-permute-start = (bf16[8,2,2,272,128]{4,3,2,1,0:T(8,128)(2,1)S(1)}, bf16[8,2,2,272,128]{4,3,2,1,0:T(8,128)(2,1)S(1)}, u32[]{:S(2)}, u32[]{:S(2)}) collective-permute-start(bf16[8,2,2,272,128]{4,3,2,1,0:T(8,128)(2,1)S(1)} %bitcast.69), channel_id=1, source_target_pairs={{0,6},{2,0},{4,2},{6,4},{1,7},{3,1},{5,3},{7,5},{8,14},{10,8},{12,... | collective-permute-start | bytes 6684680 | tf_op jit(solution)/shard_map/ppermute | solution.py:115
  129.2 26.4 %collective-permute-start.7 = (bf16[1,8,2,272,128]{4,3,2,1,0:T(8,128)(2,1)S(1)}, bf16[1,8,2,272,128]{4,3,2,1,0:T(8,128)(2,1)S(1)}, u32[]{:S(2)}, u32[]{:S(2)}) collective-permute-start(bf16[1,8,2,272,128]{4,3,2,1,0:T(8,128)(2,1)S(1)} %slice.73), channel_id=1, source_target_pairs={{0,16},{16,32},{32,48},{48,0},{1,17},{17,33},{33,49},{49,1},{2,18}... | collective-permute-start | bytes 3342344 | tf_op jit(solution)/shard_map/ppermute | solution.py:115
  132.5 24.7 %collective-permute-start.8 = (bf16[1,8,2,272,128]{4,3,2,1,0:T(8,128)(2,1)S(1)}, bf16[1,8,2,272,128]{4,3,2,1,0:T(8,128)(2,1)S(1)}, u32[]{:S(2)}, u32[]{:S(2)}) collective-permute-start(bf16[1,8,2,272,128]{4,3,2,1,0:T(8,128)(2,1)S(1)} %slice.74), channel_id=1, source_target_pairs={{0,48},{16,0},{32,16},{48,32},{1,49},{17,1},{33,17},{49,33},{2,50}... | collective-permute-start | bytes 3342344 | tf_op jit(solution)/shard_map/ppermute | solution.py:115
  133.6 32.5 %collective-permute-start.2 = (bf16[4,2,2,272,128]{4,3,2,1,0:T(8,128)(2,1)S(1)}, bf16[4,2,2,272,128]{4,3,2,1,0:T(8,128)(2,1)S(1)}, u32[]{:S(2)}, u32[]{:S(2)}) collective-permute-start(bf16[4,2,2,272,128]{4,3,2,1,0:T(8,128)(2,1)S(1)} %slice.69), channel_id=1, source_target_pairs={{0,2},{2,4},{4,6},{6,0},{1,3},{3,5},{5,7},{7,1},{8,10},{10,12},{12... | collective-permute-start | bytes 3342344 | tf_op jit(solution)/shard_map/ppermute | solution.py:115
  134.0 23.3 %copy-start.1 = (bf16[1,16,2,272,128]{4,3,2,0,1:T(8,128)(2,1)S(1)}, bf16[1,16,2,272,128]{4,3,2,0,1:T(8,128)(2,1)}, u32[]{:S(2)}) copy-start(bf16[1,16,2,272,128]{4,3,2,0,1:T(8,128)(2,1)} %copy-done) | copy-start | bytes 6684676
  134.0 32.1 %collective-permute-start.3 = (bf16[4,2,2,272,128]{4,3,2,1,0:T(8,128)(2,1)S(1)}, bf16[4,2,2,272,128]{4,3,2,1,0:T(8,128)(2,1)S(1)}, u32[]{:S(2)}, u32[]{:S(2)}) collective-permute-start(bf16[4,2,2,272,128]{4,3,2,1,0:T(8,128)(2,1)S(1)} %slice.70), channel_id=1, source_target_pairs={{0,6},{2,0},{4,2},{6,4},{1,7},{3,1},{5,3},{7,5},{8,14},{10,8},{12,... | collective-permute-start | bytes 3342344 | tf_op jit(solution)/shard_map/ppermute | solution.py:115
  163.8 16.3 %collective-permute-start.9 = (bf16[4,2,8,2,272,128]{5,4,3,2,1,0:T(8,128)(2,1)}, bf16[4,2,8,2,272,128]{5,4,3,2,1,0:T(8,128)(2,1)}, u32[]{:S(2)}, u32[]{:S(2)}) collective-permute-start(bf16[4,2,8,2,272,128]{5,4,3,2,1,0:T(8,128)(2,1)} %pad_maximum_fusion.1.right_own), channel_id=1, source_target_pairs={{0,1},{1,0},{2,3},{3,2},{4,5},{5,4},{6,7},{7,6},{8,9},{9,8},{10,11... | collective-permute-start | bytes 26738696 | tf_op jit(solution)/shard_map/ppermute | solution.py:115
  170.4 22.4 %collective-permute-start.4 = (bf16[4,8,2,2,272,128]{5,4,3,2,1,0:T(8,128)(2,1)}, bf16[4,8,2,2,272,128]{5,4,3,2,1,0:T(8,128)(2,1)}, u32[]{:S(2)}, u32[]{:S(2)}) collective-permute-start(bf16[4,8,2,2,272,128]{5,4,3,2,1,0:T(8,128)(2,1)} %pad_maximum_fusion.left_own), channel_id=1, source_target_pairs={{0,1},{1,0},{2,3},{3,2},{4,5},{5,4},{6,7},{7,6},{8,9},{9,8},{10,11... | collective-permute-start | bytes 26738696 | tf_op jit(solution)/shard_map/ppermute | solution.py:115

commit v11 on v10

--- a/solution.py
+++ b/solution.py
@@ -115,14 +115,29 @@
     return lax.ppermute(x, axis, [(i, (i + step) % n) for i in range(n)])
 
 
+def place(pieces, shape, dtype):
+    own = jnp.zeros(shape, dtype)
+    other = jnp.zeros(shape, dtype)
+    for index, piece in pieces:
+        own = own.at[index].set(piece)
+        other = other.at[index].set(shift(piece, "core", 1))
+    return own, other
+
+
 def z_ring(piece):
     from_above = shift(piece, "z", -1)
     from_below = shift(piece, "z", 1)
     half = piece.shape[0] // 2
     far_low = shift(from_below[:half], "z", 1)
     far_high = shift(from_above[half:], "z", -1)
-    far = jnp.concatenate([far_low, far_high], axis=0)
-    return jnp.stack([piece, from_above, far, from_below])
+    pieces = [
+        (0, piece),
+        (1, from_above),
+        (3, from_below),
+        ((2, slice(0, half)), far_low),
+        ((2, slice(half, None)), far_high),
+    ]
+    return place(pieces, (4,) + piece.shape, piece.dtype)
 
 
 def ring_gather(bundle):
@@ -130,9 +145,14 @@
     from_above = shift(bundle, "y", -1)
     far_low = shift(from_below[:1], "y", 1)
     far_high = shift(from_above[1:], "y", -1)
-    far = jnp.concatenate([far_low, far_high], axis=0)
-    return jnp.stack([bundle, from_above, far, from_below])
-
+    pieces = [
+        (0, bundle),
+        (1, from_above),
+        (3, from_below),
+        ((2, slice(0, 1)), far_low),
+        ((2, slice(1, None)), far_high),
+    ]
+    return place(pieces, (4,) + bundle.shape, bundle.dtype)
 
 def local(sensitivity, tile_ids, counts, weight_class):
     row_devices = lax.axis_size("xlo") * lax.axis_size("y")
@@ -158,12 +178,10 @@
     doubled = jnp.repeat(tagged, n_xhi, axis=1)
     left = lax.all_to_all(doubled, ("xlo", "y", "xhi"), split_axis=1, concat_axis=0, tiled=True)
     left = left.reshape(row_devices, n_xhi, slots, band_rows, width)
-    left_own = z_ring(left)
+    left_own, left_other = z_ring(left)
     doubled = jnp.concatenate([tagged] * n_xlo, axis=1)
     right = lax.all_to_all(doubled, ("xlo", "xhi", "z"), split_axis=1, concat_axis=0, tiled=True)
-    right_own = ring_gather(right.reshape(n_xlo, chips, slots, band_rows, width))
-    left_other = shift(left_own, "core", 1)
-    right_other = shift(right_own, "core", 1)
+    right_own, right_other = ring_gather(right.reshape(n_xlo, chips, slots, band_rows, width))
 
     n_y = lax.axis_size("y")
     n_z = lax.axis_size("z")

time: 224 us -> 273 us (1.22)
  local copies, waits for them, and re-layouts: 13.8 us -> 74.3 us
  other arithmetic: 20.3 us -> 8.61 us
  waiting for transfers between devices: 133 us -> 122 us
  starting transfers between devices: 27.7 us -> 37.8 us
    scatter x0 -> x20, local copies, waits for them, and re-layouts: none -> 58.1 us  [the longest x10 33.5 us: place(): other = other.at[index].set(shift(piece, 'core', 1))]
    another operation x4 -> x0, other arithmetic: 10.8 us -> none  [the longest x2 6.59 us: ring_gather(): return jnp.stack([bundle, from_above, far, from_below])]
    ppermute x10 -> x18, starting transfers between devices: 11.7 us -> 21.8 us  [shift(): return lax.ppermute(x, axis, [(i, (i + step) % n) for i in range(n)])]
    ppermute x10 -> x18, waiting for transfers between devices: 79 us -> 70.6 us  [shift(): return lax.ppermute(x, axis, [(i, (i + step) % n) for i in range(n)])]
    all_to_all x1, waiting for transfers between devices: 28.1 us -> 25.2 us  [local(): lax.all_to_all(doubled, ('xlo', 'y', 'xhi'), split_axis=1, concat_axis=0,...]
  transfers between devices with their start and end apart: 12 -> 20, of which waited for: 8 -> 6; matrix products, arithmetic and copies ran while one was open for 10% -> 25% of each run, Pallas kernels for 0% -> 0%
where the time goes in v11:
time: 273 us; the launch traced here: 271 us
  waiting for transfers between devices  122 us (45%)
  local copies, waits for them, and re-layouts  74.3 us (27%)
  starting transfers between devices  37.8 us (14%)
  Pallas kernels  28.1 us (10%)
  other arithmetic  8.61 us (3%)
    ppermute x18, waiting for transfers between devices, shift(): return lax.ppermute(x, axis, [(i, (i + step) % n) for i in range(n)])  70.6 us
    scatter x10, local copies, waits for them, and re-layouts, place(): other = other.at[index].set(shift(piece, 'core', 1))  33.5 us
    pallas_call x1, Pallas kernels, accumulate(): pl.pallas_call(functools.partial(gram_kernel, slots, rows, width, n_chip)...  28.1 us
    all_to_all x1, waiting for transfers between devices, local(): lax.all_to_all(doubled, ('xlo', 'xhi', 'z'), split_axis=1, concat_axis=0,...  25.8 us
    all_to_all x1, waiting for transfers between devices, local(): lax.all_to_all(doubled, ('xlo', 'y', 'xhi'), split_axis=1, concat_axis=0,...  25.2 us
    scatter x10, local copies, waits for them, and re-layouts, place(): own = own.at[index].set(piece)  24.6 us
    ppermute x18, starting transfers between devices, shift(): return lax.ppermute(x, axis, [(i, (i + step) % n) for i in range(n)])  21.8 us
    all_to_all x1, starting transfers between devices, local(): lax.all_to_all(doubled, ('xlo', 'xhi', 'z'), split_axis=1, concat_axis=0,...  8.43 us
  transfers between devices with their start and end apart: 20, of which 6 were waited for; matrix products, arithmetic and copies ran while one was open for 25% of the time, Pallas kernels for 0%

profile of v11, /device:TPU:1, one launch (start us, length us, event | category | flops | bytes accessed | tf_op | source)
XLA Modules:
  0.0 270.7 jit_solution(14514716229388725493)
XLA Ops:
  0.0 0.7 fusion.4
  0.7 0.7 fusion.7
  1.5 0.8 select_reduce_fusion
  2.4 1.7 multiply_convert_fusion
  4.2 1.7 maximum_maximum_fusion
  5.9 8.4 %all-to-all-start.1 = ((bf16[1,16,2,272,128]{4,3,2,0,1:T(8,128)(2,1)}), bf16[1,16,2,272,128]{4,3,2,0,1:T(8,128)(2,1)S(1)}, u32[]{:S(2)}, u32[]{:S(2)}) async-start(bf16[1,16,2,272,128]{4,3,2,0,1:T(8,128)(2,1)} %maximum_maximum_fusion), calls=%async_computation.1 | async-start | bytes 4456448 | tf_op jit(solution)/shard_map/all_to_all | solution.py:183
  14.3 1.1 maximum_bitcast_fusion
  15.4 25.8 %all-to-all-done.1 = bf16[1,16,2,272,128]{4,3,2,0,1:T(8,128)(2,1)S(1)} async-done(((bf16[1,16,2,272,128]{4,3,2,0,1:T(8,128)(2,1)}), bf16[1,16,2,272,128]{4,3,2,0,1:T(8,128)(2,1)S(1)}, u32[]{:S(2)}, u32[]{:S(2)}) %all-to-all-start.1) | async-done | bytes 2228256 | tf_op jit(solution)/shard_map/all_to_all | solution.py:183
  41.3 3.7 %broadcast_in_dim.43 = bf16[8,2,2,272,128]{4,3,2,1,0:T(8,128)(2,1)} broadcast(bf16[8,2,272,128]{3,2,1,0:T(8,128)(2,1)} %maximum_bitcast_fusion), dimensions={0,2,3,4} | broadcast | bytes 3342336 | tf_op jit(solution)/shard_map/broadcast_in_dim | solution.py:178
  45.0 7.5 %all-to-all-start = ((bf16[1,16,2,272,128]{4,3,2,0,1:T(8,128)(2,1)}), bf16[1,16,2,272,128]{4,3,2,0,1:T(8,128)(2,1)S(1)}, u32[]{:S(2)}, u32[]{:S(2)}) async-start(bf16[1,16,2,272,128]{4,3,2,0,1:T(8,128)(2,1)} %bitcast.102), calls=%async_computation | async-start | bytes 4456448 | tf_op jit(solution)/shard_map/all_to_all | solution.py:179
  52.5 1.4 collective-permute-start.10
  53.9 1.4 collective-permute-start.9
  55.3 2.9 %collective-permute-start.13 = (bf16[2,8,2,272,128]{4,3,2,1,0:T(8,128)(2,1)}, bf16[2,8,2,272,128]{4,3,2,1,0:T(8,128)(2,1)}, u32[]{:S(2)}, u32[]{:S(2)}) collective-permute-start(bf16[2,8,2,272,128]{4,3,2,1,0:T(8,128)(2,1)} %bitcast.100), channel_id=1, source_target_pairs={{0,1},{1,0},{2,3},{3,2},{4,5},{5,4},{6,7},{7,6},{8,9},{9,8},{10,11... | collective-permute-start | bytes 6684680 | tf_op jit(solution)/shard_map/ppermute | solution.py:115
  58.2 25.2 %all-to-all-done = bf16[1,16,2,272,128]{4,3,2,0,1:T(8,128)(2,1)S(1)} async-done(((bf16[1,16,2,272,128]{4,3,2,0,1:T(8,128)(2,1)}), bf16[1,16,2,272,128]{4,3,2,0,1:T(8,128)(2,1)S(1)}, u32[]{:S(2)}, u32[]{:S(2)}) %all-to-all-start) | async-done | bytes 2228256 | tf_op jit(solution)/shard_map/all_to_all | solution.py:179
  83.4 2.4 collective-permute-start.4
  85.8 0.3 collective-permute-start.1
  86.1 41.7 %collective-permute-done.10 = bf16[2,8,2,272,128]{4,3,2,1,0:T(8,128)(2,1)} collective-permute-done((bf16[2,8,2,272,128]{4,3,2,1,0:T(8,128)(2,1)}, bf16[2,8,2,272,128]{4,3,2,1,0:T(8,128)(2,1)}, u32[]{:S(2)}, u32[]{:S(2)}) %collective-permute-start.10) | collective-permute-done | bytes 2228256 | tf_op jit(solution)/shard_map/ppermute | solution.py:115
  127.8 1.8 collective-permute-start
  129.7 1.3 slice.807
  131.0 0.2 collective-permute-done.9
  131.2 0.7 pad_add_fusion.1.rot_ref
  131.8 2.8 %scatter.89 = bf16[4,2,8,2,272,128]{5,4,3,2,1,0:T(8,128)(2,1)S(1)} pad(bf16[1,2,8,2,272,128]{5,4,3,2,1,0:T(8,128)(2,1)} %bitcast.101, bf16[]{:T(256)} %constant.552.clone.1), padding=0_3x0_0x0_0x0_0x0_0x0_0 | pad | bytes 11141122 | tf_op jit(solution)/shard_map/scatter | solution.py:122
  134.7 5.1 %scatter.71 = bf16[4,8,2,2,272,128]{5,4,3,2,1,0:T(8,128)(2,1)} pad(bf16[1,8,2,2,272,128]{5,4,3,2,1,0:T(8,128)(2,1)S(1)} %bitcast.97, bf16[]{:T(256)} %constant.552.clone.1), padding=0_3x0_0x0_0x0_0x0_0x0_0 | pad | bytes 11141122 | tf_op jit(solution)/shard_map/scatter | solution.py:122
  139.8 2.5 collective-permute-start.14
  142.2 1.9 bitcast_dynamic-update-slice_fusion.3
  144.2 1.3 slice.808
  145.5 2.2 collective-permute-start.12
  147.7 1.9 bitcast_dynamic-update-slice_fusion.2
  149.7 6.3 %scatter.96 = bf16[4,2,8,2,272,128]{5,4,3,2,1,0:T(8,128)(2,1)} pad(bf16[1,2,8,2,272,128]{5,4,3,2,1,0:T(8,128)(2,1)} %bitcast.36, bf16[]{:T(256)} %constant.552.clone.1), padding=0_3x0_0x0_0x0_0x0_0x0_0 | pad | bytes 11141122 | tf_op jit(solution)/shard_map/scatter | solution.py:123
  156.0 6.7 %scatter.80 = bf16[4,8,2,2,272,128]{5,4,3,2,1,0:T(8,128)(2,1)} pad(bf16[1,8,2,2,272,128]{5,4,3,2,1,0:T(8,128)(2,1)} %bitcast.15, bf16[]{:T(256)} %constant.552.clone.1), padding=0_3x0_0x0_0x0_0x0_0x0_0 | pad | bytes 11141122 | tf_op jit(solution)/shard_map/scatter | solution.py:123
  162.7 1.3 slice.803
  164.2 12.9 %collective-permute-done = bf16[8,2,2,272,128]{4,3,2,1,0:T(8,128)(2,1)} collective-permute-done((bf16[8,2,2,272,128]{4,3,2,1,0:T(8,128)(2,1)S(1)}, bf16[8,2,2,272,128]{4,3,2,1,0:T(8,128)(2,1)}, u32[]{:S(2)}, u32[]{:S(2)}) %collective-permute-start) | collective-permute-done | bytes 2228256 | tf_op jit(solution)/shard_map/ppermute | solution.py:115
  177.0 1.8 collective-permute-start.15
  178.8 1.3 slice.804
  180.1 3.2 %bitcast_dynamic-update-slice_fusion.7 = bf16[4,8,2,2,272,128]{5,4,3,2,1,0:T(8,128)(2,1)} fusion(bf16[4,8,2,2,272,128]{5,4,3,2,1,0:T(8,128)(2,1)} %scatter.71, bf16[8,2,2,272,128]{4,3,2,1,0:T(8,128)(2,1)} %collective-permute-done), kind=kLoop, calls=%fused_computation.12 | loop fusion | bytes 4456448 | tf_op jit(solution)/shard_map/scatter | solution.py:122
  183.3 3.0 %collective-permute-start.3 = (bf16[4,2,2,272,128]{4,3,2,1,0:T(8,128)(2,1)S(1)}, bf16[4,2,2,272,128]{4,3,2,1,0:T(8,128)(2,1)}, u32[]{:S(2)}, u32[]{:S(2)}) collective-permute-start(bf16[4,2,2,272,128]{4,3,2,1,0:T(8,128)(2,1)S(1)} %slice.804), channel_id=1, source_target_pairs={{0,6},{2,0},{4,2},{6,4},{1,7},{3,1},{5,3},{7,5},{8,14},{10,8},{12,... | collective-permute-start | bytes 3342344 | tf_op jit(solution)/shard_map/ppermute | solution.py:115
  186.3 3.1 %bitcast_dynamic-update-slice_fusion.6 = bf16[4,8,2,2,272,128]{5,4,3,2,1,0:T(8,128)(2,1)} fusion(bf16[4,8,2,2,272,128]{5,4,3,2,1,0:T(8,128)(2,1)} %bitcast_dynamic-update-slice_fusion.7, bf16[8,2,2,272,128]{4,3,2,1,0:T(8,128)(2,1)} %collective-permute-done.1), kind=kLoop, calls=%fused_computation.11 | loop fusion | bytes 4456448 | tf_op jit(solution)/shard_map/scatter | solution.py:122
  189.4 1.4 bitcast_dynamic-update-slice_fusion.11
  190.8 0.5 collective-permute-start.5
  191.4 1.4 bitcast_dynamic-update-slice_fusion.10.right_own
  192.8 0.3 collective-permute-start.6
  193.1 1.4 bitcast_dynamic-update-slice_fusion.15
  194.5 15.8 %collective-permute-done.3 = bf16[4,2,2,272,128]{4,3,2,1,0:T(8,128)(2,1)} collective-permute-done((bf16[4,2,2,272,128]{4,3,2,1,0:T(8,128)(2,1)S(1)}, bf16[4,2,2,272,128]{4,3,2,1,0:T(8,128)(2,1)}, u32[]{:S(2)}, u32[]{:S(2)}) %collective-permute-start.3) | collective-permute-done | bytes 1114144 | tf_op jit(solution)/shard_map/ppermute | solution.py:115
  210.3 0.8 collective-permute-start.16
  211.1 2.3 bitcast_dynamic-update-slice_fusion.14.left_own
  213.7 0.6 gather_fusion
  214.3 0.6 gather_fusion.1
  215.0 1.0 slice.805
  216.2 3.2 %bitcast_dynamic-update-slice_fusion.1 = bf16[4,2,8,2,272,128]{5,4,3,2,1,0:T(8,128)(2,1)} fusion(bf16[4,2,8,2,272,128]{5,4,3,2,1,0:T(8,128)(2,1)} %scatter.96, bf16[2,8,2,272,128]{4,3,2,1,0:T(8,128)(2,1)} %collective-permute-done.14), kind=kLoop, calls=%fused_computation.6 | loop fusion | bytes 4456448 | tf_op jit(solution)/shard_map/scatter | solution.py:123
  219.3 0.5 collective-permute-start.7
  219.8 3.2 %bitcast_dynamic-update-slice_fusion = bf16[4,2,8,2,272,128]{5,4,3,2,1,0:T(8,128)(2,1)} fusion(bf16[4,2,8,2,272,128]{5,4,3,2,1,0:T(8,128)(2,1)} %bitcast_dynamic-update-slice_fusion.1, bf16[2,8,2,272,128]{4,3,2,1,0:T(8,128)(2,1)} %collective-permute-done.15), kind=kLoop, calls=%fused_computation.5 | loop fusion | bytes 4456448 | tf_op jit(solution)/shard_map/scatter | solution.py:123
  223.1 2.3 bitcast_dynamic-update-slice_fusion.9
  225.4 2.3 bitcast_dynamic-update-slice_fusion.8.right_other
  227.7 1.0 fusion
  228.9 0.6 gather_fusion.2
  229.6 0.6 gather_fusion.3
  230.4 0.7 reshape.1358.rids_ref
  231.1 1.6 bitcast_dynamic-update-slice_fusion.5
  232.7 3.2 %bitcast_dynamic-update-slice_fusion.4 = bf16[4,8,2,2,272,128]{5,4,3,2,1,0:T(8,128)(2,1)} fusion(bf16[4,8,2,2,272,128]{5,4,3,2,1,0:T(8,128)(2,1)} %bitcast_dynamic-update-slice_fusion.5, bf16[8,2,2,272,128]{4,3,2,1,0:T(8,128)(2,1)} %collective-permute-done.6), kind=kLoop, calls=%fused_computation.9 | loop fusion | bytes 4456448 | tf_op jit(solution)/shard_map/scatter | solution.py:123
  235.9 2.3 bitcast_dynamic-update-slice_fusion.13
  238.2 2.3 bitcast_dynamic-update-slice_fusion.12.left_other
  240.6 1.0 slice.806
  242.0 0.7 reshape.1360.lids_ref
  242.6 28.1 %shard_map.58 = f32[2048,1024]{1,0:T(8,128)} custom-call(s32[256]{0:T(256)} %reshape.1360.lids_ref, s32[256]{0:T(256)} %reshape.1358.rids_ref, s32[3]{0:T(128)} %pad_add_fusion.1.rot_ref, bf16[4,8,2,2,272,128]{5,4,3,2,1,0:T(8,128)(2,1)} %bitcast_dynamic-update-slice_fusion.14.left_own, bf16[4,2,8,2,272,128]{5,4,3,2,1,0:T(8,128)(2,1)} %copy-done, ...), custom_call_target="tpu_custom_call" | custom-call | flops 4294967296 | bytes 44040192 | tf_op jit(solution)/shard_map/pallas_call | solution.py:98
  (48 shorter events, 2.0 us)
Async XLA Ops:
  5.9 35.4 %all-to-all-start.1 = ((bf16[1,16,2,272,128]{4,3,2,0,1:T(8,128)(2,1)}), bf16[1,16,2,272,128]{4,3,2,0,1:T(8,128)(2,1)S(1)}, u32[]{:S(2)}, u32[]{:S(2)}) async-start(bf16[1,16,2,272,128]{4,3,2,0,1:T(8,128)(2,1)} %maximum_maximum_fusion), calls=%async_computation.1 | async-start | bytes 4456448 | tf_op jit(solution)/shard_map/all_to_all | solution.py:183
  41.3 3.7 %copy-start.1 = (bf16[1,16,2,272,128]{4,3,2,0,1:T(8,128)(2,1)}, bf16[1,16,2,272,128]{4,3,2,0,1:T(8,128)(2,1)S(1)}, u32[]{:S(2)}) copy-start(bf16[1,16,2,272,128]{4,3,2,0,1:T(8,128)(2,1)S(1)} %all-to-all-done.1) | copy-start | bytes 6684676
  45.0 38.4 %all-to-all-start = ((bf16[1,16,2,272,128]{4,3,2,0,1:T(8,128)(2,1)}), bf16[1,16,2,272,128]{4,3,2,0,1:T(8,128)(2,1)S(1)}, u32[]{:S(2)}, u32[]{:S(2)}) async-start(bf16[1,16,2,272,128]{4,3,2,0,1:T(8,128)(2,1)} %bitcast.102), calls=%async_computation | async-start | bytes 4456448 | tf_op jit(solution)/shard_map/all_to_all | solution.py:179
  52.5 75.3 %collective-permute-start.10 = (bf16[2,8,2,272,128]{4,3,2,1,0:T(8,128)(2,1)}, bf16[2,8,2,272,128]{4,3,2,1,0:T(8,128)(2,1)}, u32[]{:S(2)}, u32[]{:S(2)}) collective-permute-start(bf16[2,8,2,272,128]{4,3,2,1,0:T(8,128)(2,1)} %bitcast.98), channel_id=1, source_target_pairs={{0,16},{16,32},{32,48},{48,0},{1,17},{17,33},{33,49},{49,1},{2,18}... | collective-permute-start | bytes 6684680 | tf_op jit(solution)/shard_map/ppermute | solution.py:115
  53.9 77.3 %collective-permute-start.9 = (bf16[2,8,2,272,128]{4,3,2,1,0:T(8,128)(2,1)}, bf16[2,8,2,272,128]{4,3,2,1,0:T(8,128)(2,1)}, u32[]{:S(2)}, u32[]{:S(2)}) collective-permute-start(bf16[2,8,2,272,128]{4,3,2,1,0:T(8,128)(2,1)} %bitcast.99), channel_id=1, source_target_pairs={{0,48},{16,0},{32,16},{48,32},{1,49},{17,1},{33,17},{49,33},{2,50}... | collective-permute-start | bytes 6684680 | tf_op jit(solution)/shard_map/ppermute | solution.py:115
  55.3 84.5 %collective-permute-start.13 = (bf16[2,8,2,272,128]{4,3,2,1,0:T(8,128)(2,1)}, bf16[2,8,2,272,128]{4,3,2,1,0:T(8,128)(2,1)}, u32[]{:S(2)}, u32[]{:S(2)}) collective-permute-start(bf16[2,8,2,272,128]{4,3,2,1,0:T(8,128)(2,1)} %bitcast.100), channel_id=1, source_target_pairs={{0,1},{1,0},{2,3},{3,2},{4,5},{5,4},{6,7},{7,6},{8,9},{9,8},{10,11... | collective-permute-start | bytes 6684680 | tf_op jit(solution)/shard_map/ppermute | solution.py:115
  83.4 62.1 %collective-permute-start.4 = (bf16[8,2,2,272,128]{4,3,2,1,0:T(8,128)(2,1)S(1)}, bf16[8,2,2,272,128]{4,3,2,1,0:T(8,128)(2,1)}, u32[]{:S(2)}, u32[]{:S(2)}) collective-permute-start(bf16[8,2,2,272,128]{4,3,2,1,0:T(8,128)(2,1)S(1)} %bitcast.94), channel_id=1, source_target_pairs={{0,1},{1,0},{2,3},{3,2},{4,5},{5,4},{6,7},{7,6},{8,9},{9,8},{10,11... | collective-permute-start | bytes 6684680 | tf_op jit(solution)/shard_map/ppermute | solution.py:115
  85.8 76.9 %collective-permute-start.1 = (bf16[8,2,2,272,128]{4,3,2,1,0:T(8,128)(2,1)S(1)}, bf16[8,2,2,272,128]{4,3,2,1,0:T(8,128)(2,1)}, u32[]{:S(2)}, u32[]{:S(2)}) collective-permute-start(bf16[8,2,2,272,128]{4,3,2,1,0:T(8,128)(2,1)S(1)} %bitcast.95), channel_id=1, source_target_pairs={{0,2},{2,4},{4,6},{6,0},{1,3},{3,5},{5,7},{7,1},{8,10},{10,12},{12... | collective-permute-start | bytes 6684680 | tf_op jit(solution)/shard_map/ppermute | solution.py:115
  127.8 49.2 %collective-permute-start = (bf16[8,2,2,272,128]{4,3,2,1,0:T(8,128)(2,1)S(1)}, bf16[8,2,2,272,128]{4,3,2,1,0:T(8,128)(2,1)}, u32[]{:S(2)}, u32[]{:S(2)}) collective-permute-start(bf16[8,2,2,272,128]{4,3,2,1,0:T(8,128)(2,1)S(1)} %bitcast.96), channel_id=1, source_target_pairs={{0,6},{2,0},{4,2},{6,4},{1,7},{3,1},{5,3},{7,5},{8,14},{10,8},{12,... | collective-permute-start | bytes 6684680 | tf_op jit(solution)/shard_map/ppermute | solution.py:115
  131.2 52.2 %collective-permute-start.11 = (bf16[1,8,2,272,128]{4,3,2,1,0:T(8,128)(2,1)S(1)}, bf16[1,8,2,272,128]{4,3,2,1,0:T(8,128)(2,1)}, u32[]{:S(2)}, u32[]{:S(2)}) collective-permute-start(bf16[1,8,2,272,128]{4,3,2,1,0:T(8,128)(2,1)S(1)} %slice.807), channel_id=1, source_target_pairs={{0,16},{16,32},{32,48},{48,0},{1,17},{17,33},{33,49},{49,1},{2,18}... | collective-permute-start | bytes 3342344 | tf_op jit(solution)/shard_map/ppermute | solution.py:115
  139.8 73.6 %collective-permute-start.14 = (bf16[2,8,2,272,128]{4,3,2,1,0:T(8,128)(2,1)}, bf16[2,8,2,272,128]{4,3,2,1,0:T(8,128)(2,1)}, u32[]{:S(2)}, u32[]{:S(2)}) collective-permute-start(bf16[2,8,2,272,128]{4,3,2,1,0:T(8,128)(2,1)} %collective-permute-done.9), channel_id=1, source_target_pairs={{0,1},{1,0},{2,3},{3,2},{4,5},{5,4},{6,7},{7,6},{8,9},{9,8},{10,11... | collective-permute-start | bytes 6684680 | tf_op jit(solution)/shard_map/ppermute | solution.py:115
  145.5 45.3 %collective-permute-start.12 = (bf16[1,8,2,272,128]{4,3,2,1,0:T(8,128)(2,1)S(1)}, bf16[1,8,2,272,128]{4,3,2,1,0:T(8,128)(2,1)}, u32[]{:S(2)}, u32[]{:S(2)}) collective-permute-start(bf16[1,8,2,272,128]{4,3,2,1,0:T(8,128)(2,1)S(1)} %slice.808), channel_id=1, source_target_pairs={{0,48},{16,0},{32,16},{48,32},{1,49},{17,1},{33,17},{49,33},{2,50}... | collective-permute-start | bytes 3342344 | tf_op jit(solution)/shard_map/ppermute | solution.py:115
  164.1 28.7 %collective-permute-start.2 = (bf16[4,2,2,272,128]{4,3,2,1,0:T(8,128)(2,1)S(1)}, bf16[4,2,2,272,128]{4,3,2,1,0:T(8,128)(2,1)S(1)}, u32[]{:S(2)}, u32[]{:S(2)}) collective-permute-start(bf16[4,2,2,272,128]{4,3,2,1,0:T(8,128)(2,1)S(1)} %slice.803), channel_id=1, source_target_pairs={{0,2},{2,4},{4,6},{6,0},{1,3},{3,5},{5,7},{7,1},{8,10},{10,12},{12... | collective-permute-start | bytes 3342344 | tf_op jit(solution)/shard_map/ppermute | solution.py:115
  177.0 42.3 %collective-permute-start.15 = (bf16[2,8,2,272,128]{4,3,2,1,0:T(8,128)(2,1)}, bf16[2,8,2,272,128]{4,3,2,1,0:T(8,128)(2,1)}, u32[]{:S(2)}, u32[]{:S(2)}) collective-permute-start(bf16[2,8,2,272,128]{4,3,2,1,0:T(8,128)(2,1)} %collective-permute-done.10), channel_id=1, source_target_pairs={{0,1},{1,0},{2,3},{3,2},{4,5},{5,4},{6,7},{7,6},{8,9},{9,8},{10,11... | collective-permute-start | bytes 6684680 | tf_op jit(solution)/shard_map/ppermute | solution.py:115
  183.3 27.0 %collective-permute-start.3 = (bf16[4,2,2,272,128]{4,3,2,1,0:T(8,128)(2,1)S(1)}, bf16[4,2,2,272,128]{4,3,2,1,0:T(8,128)(2,1)}, u32[]{:S(2)}, u32[]{:S(2)}) collective-permute-start(bf16[4,2,2,272,128]{4,3,2,1,0:T(8,128)(2,1)S(1)} %slice.804), channel_id=1, source_target_pairs={{0,6},{2,0},{4,2},{6,4},{1,7},{3,1},{5,3},{7,5},{8,14},{10,8},{12,... | collective-permute-start | bytes 3342344 | tf_op jit(solution)/shard_map/ppermute | solution.py:115
  190.8 40.3 %collective-permute-start.5 = (bf16[8,2,2,272,128]{4,3,2,1,0:T(8,128)(2,1)}, bf16[8,2,2,272,128]{4,3,2,1,0:T(8,128)(2,1)S(1)}, u32[]{:S(2)}, u32[]{:S(2)}) collective-permute-start(bf16[8,2,2,272,128]{4,3,2,1,0:T(8,128)(2,1)} %collective-permute-done), channel_id=1, source_target_pairs={{0,1},{1,0},{2,3},{3,2},{4,5},{5,4},{6,7},{7,6},{8,9},{9,8},{10,11... | collective-permute-start | bytes 6684680 | tf_op jit(solution)/shard_map/ppermute | solution.py:115
  192.8 20.6 %copy-start = (bf16[4,2,8,2,272,128]{5,4,3,2,1,0:T(8,128)(2,1)}, bf16[4,2,8,2,272,128]{5,4,3,2,1,0:T(8,128)(2,1)S(1)}, u32[]{:S(2)}) copy-start(bf16[4,2,8,2,272,128]{5,4,3,2,1,0:T(8,128)(2,1)S(1)} %bitcast_dynamic-update-slice_fusion.10.right_own) | copy-start | bytes 26738692
  192.8 39.9 %collective-permute-start.6 = (bf16[8,2,2,272,128]{4,3,2,1,0:T(8,128)(2,1)}, bf16[8,2,2,272,128]{4,3,2,1,0:T(8,128)(2,1)}, u32[]{:S(2)}, u32[]{:S(2)}) collective-permute-start(bf16[8,2,2,272,128]{4,3,2,1,0:T(8,128)(2,1)} %collective-permute-done.1), channel_id=1, source_target_pairs={{0,1},{1,0},{2,3},{3,2},{4,5},{5,4},{6,7},{7,6},{8,9},{9,8},{10,11... | collective-permute-start | bytes 6684680 | tf_op jit(solution)/shard_map/ppermute | solution.py:115
  210.3 12.8 %collective-permute-start.16 = (bf16[1,8,2,272,128]{4,3,2,1,0:T(8,128)(2,1)}, bf16[1,8,2,272,128]{4,3,2,1,0:T(8,128)(2,1)}, u32[]{:S(2)}, u32[]{:S(2)}) collective-permute-start(bf16[1,8,2,272,128]{4,3,2,1,0:T(8,128)(2,1)} %collective-permute-done.11), channel_id=1, source_target_pairs={{0,1},{1,0},{2,3},{3,2},{4,5},{5,4},{6,7},{7,6},{8,9},{9,8},{10,11... | collective-permute-start | bytes 3342344 | tf_op jit(solution)/shard_map/ppermute | solution.py:115
  213.4 12.0 %collective-permute-start.17 = (bf16[1,8,2,272,128]{4,3,2,1,0:T(8,128)(2,1)}, bf16[1,8,2,272,128]{4,3,2,1,0:T(8,128)(2,1)}, u32[]{:S(2)}, u32[]{:S(2)}) collective-permute-start(bf16[1,8,2,272,128]{4,3,2,1,0:T(8,128)(2,1)} %collective-permute-done.12), channel_id=1, source_target_pairs={{0,1},{1,0},{2,3},{3,2},{4,5},{5,4},{6,7},{7,6},{8,9},{9,8},{10,11... | collective-permute-start | bytes 3342344 | tf_op jit(solution)/shard_map/ppermute | solution.py:115
  219.3 16.6 %collective-permute-start.7 = (bf16[4,2,2,272,128]{4,3,2,1,0:T(8,128)(2,1)S(1)}, bf16[4,2,2,272,128]{4,3,2,1,0:T(8,128)(2,1)}, u32[]{:S(2)}, u32[]{:S(2)}) collective-permute-start(bf16[4,2,2,272,128]{4,3,2,1,0:T(8,128)(2,1)S(1)} %collective-permute-done.2), channel_id=1, source_target_pairs={{0,1},{1,0},{2,3},{3,2},{4,5},{5,4},{6,7},{7,6},{8,9},{9,8},{10,11... | collective-permute-start | bytes 3342344 | tf_op jit(solution)/shard_map/ppermute | solution.py:115
  223.0 15.2 %collective-permute-start.8 = (bf16[4,2,2,272,128]{4,3,2,1,0:T(8,128)(2,1)}, bf16[4,2,2,272,128]{4,3,2,1,0:T(8,128)(2,1)}, u32[]{:S(2)}, u32[]{:S(2)}) collective-permute-start(bf16[4,2,2,272,128]{4,3,2,1,0:T(8,128)(2,1)} %collective-permute-done.3), channel_id=1, source_target_pairs={{0,1},{1,0},{2,3},{3,2},{4,5},{5,4},{6,7},{7,6},{8,9},{9,8},{10,11... | collective-permute-start | bytes 3342344 | tf_op jit(solution)/shard_map/ppermute | solution.py:115

commit v12 on v9

--- a/solution.py
+++ b/solution.py
@@ -130,6 +130,19 @@
     return jnp.stack([bundle, from_above, far, from_below])
 
 
+def exchange(slices, axes, size, kinds):
+    me = 0
+    for axis in axes:
+        me = me * lax.axis_size(axis) + lax.axis_index(axis)
+    received = [slices[lax.rem(me, kinds)]]
+    for s in range(1, size):
+        chunk = slices[lax.rem(me + s, kinds)]
+        received.append(lax.ppermute(chunk, axes, [(i, (i + s) % size) for i in range(size)]))
+    by_shift = jnp.stack(received)
+    sources = jnp.arange(size, dtype=jnp.int32)
+    return by_shift[lax.rem(me - sources + size, size)]
+
+
 def local(sensitivity, tile_ids, counts, weight_class):
     row_devices = lax.axis_size("xlo") * lax.axis_size("y")
     chips = lax.axis_size("xhi") * lax.axis_size("z")
@@ -155,8 +168,7 @@
     left = lax.all_to_all(doubled, ("xlo", "y", "xhi"), split_axis=1, concat_axis=0, tiled=True)
     left = left.reshape(row_devices, n_xhi, slots, band_rows, width)
     left_own = z_ring(left)
-    doubled = jnp.concatenate([tagged] * n_xlo, axis=1)
-    right = lax.all_to_all(doubled, ("xlo", "xhi", "z"), split_axis=1, concat_axis=0, tiled=True)
+    right = exchange(tagged[0], ("xlo", "xhi", "z"), n_xlo * chips, chips)
     right_own = ring_gather(right.reshape(n_xlo, chips, slots, band_rows, width))
     left_other = shift(left_own, "core", 1)
     right_other = shift(right_own, "core", 1)

time: 221 us -> 222 us (level)
  waiting for transfers between devices: 118 us -> 74.2 us
  starting transfers between devices: 27.7 us -> 58.1 us
  local copies, waits for them, and re-layouts: 12 us -> 29.6 us
  other arithmetic: 23.5 us -> 21.1 us
    all_to_all x1, waiting for transfers between devices: 28.1 us -> 0.01 us  [local(): lax.all_to_all(doubled, ('xlo', 'y', 'xhi'), split_axis=1, concat_axis=0,...]
    ppermute x0 -> x15, starting transfers between devices: none -> 26.8 us  [exchange(): lax.ppermute(chunk, axes, [(i, (i + s) % size) for i in range(size)])]
    all_to_all x1 -> x0, waiting for transfers between devices: 25.8 us -> none  [local(): lax.all_to_all(doubled, ('xlo', 'xhi', 'z'), split_axis=1, concat_axis=0,...]
    ppermute x0 -> x15, waiting for transfers between devices: none -> 21.6 us  [exchange(): lax.ppermute(chunk, axes, [(i, (i + s) % size) for i in range(size)])]
    ppermute x10, starting transfers between devices: 11.7 us -> 26.1 us  [shift(): return lax.ppermute(x, axis, [(i, (i + step) % n) for i in range(n)])]
    unnamed x4 -> x23, local copies, waits for them, and re-layouts: 0.01 us -> 13.6 us
    ppermute x10, waiting for transfers between devices: 64.3 us -> 52.6 us  [shift(): return lax.ppermute(x, axis, [(i, (i + step) % n) for i in range(n)])]
    all_to_all x1 -> x0, starting transfers between devices: 8.43 us -> none  [local(): lax.all_to_all(doubled, ('xlo', 'xhi', 'z'), split_axis=1, concat_axis=0,...]
  transfers between devices with their start and end apart: 12 -> 26, of which waited for: 6 -> 7; matrix products, arithmetic and copies ran while one was open for 11% -> 20% of each run, Pallas kernels for 8% -> 8%
where the time goes in v12:
time: 222 us; the launch traced here: 219 us
  waiting for transfers between devices  74.2 us (33%)
  starting transfers between devices  58.1 us (26%)
  Pallas kernels  35.7 us (16%)
  local copies, waits for them, and re-layouts  29.6 us (13%)
  other arithmetic  21.1 us (10%)
    ppermute x10, waiting for transfers between devices, shift(): return lax.ppermute(x, axis, [(i, (i + step) % n) for i in range(n)])  52.6 us
    pallas_call x2, Pallas kernels, accumulate(): pl.pallas_call(functools.partial(gram_kernel, slots, rows, width, n_chip,...  35.7 us
    ppermute x15, starting transfers between devices, exchange(): lax.ppermute(chunk, axes, [(i, (i + s) % size) for i in range(size)])  26.8 us
    ppermute x10, starting transfers between devices, shift(): return lax.ppermute(x, axis, [(i, (i + step) % n) for i in range(n)])  26.1 us
    ppermute x15, waiting for transfers between devices, exchange(): lax.ppermute(chunk, axes, [(i, (i + s) % size) for i in range(size)])  21.6 us
    unnamed x23, local copies, waits for them, and re-layouts  13.6 us
    another operation x2, other arithmetic, ring_gather(): return jnp.stack([bundle, from_above, far, from_below])  6.56 us
    all_to_all x1, starting transfers between devices, local(): lax.all_to_all(doubled, ('xlo', 'y', 'xhi'), split_axis=1, concat_axis=0,...  5.17 us
  transfers between devices with their start and end apart: 26, of which 7 were waited for; matrix products, arithmetic and copies ran while one was open for 20% of the time, Pallas kernels for 8%

profile of v12, /device:TPU:1, one launch (start us, length us, event | category | flops | bytes accessed | tf_op | source)
XLA Modules:
  0.0 218.9 jit_solution(16100732509060537697)
XLA Ops:
  0.0 0.7 fusion.4
  0.7 0.7 fusion.7
  1.5 0.8 select_reduce_fusion
  2.4 1.7 multiply_convert_fusion
  4.5 1.4 dynamic-slice_bitcast_fusion
  5.9 2.5 %collective-permute-start.5 = (bf16[2,272,128]{2,1,0:T(8,128)(2,1)}, bf16[2,272,128]{2,1,0:T(8,128)(2,1)}, u32[]{:S(2)}, u32[]{:S(2)}) collective-permute-start(bf16[2,272,128]{2,1,0:T(8,128)(2,1)} %get-tuple-element.31), channel_id=1, source_target_pairs={{0,2},{2,4},{4,6},{6,8},{8,10},{10,12},{12,14},{14,64},{64,66},{66... | collective-permute-start | bytes 417800 | tf_op jit(solution)/shard_map/ppermute | solution.py:140
  8.4 3.3 %collective-permute-start.6 = (bf16[2,272,128]{2,1,0:T(8,128)(2,1)}, bf16[2,272,128]{2,1,0:T(8,128)(2,1)}, u32[]{:S(2)}, u32[]{:S(2)}) collective-permute-start(bf16[2,272,128]{2,1,0:T(8,128)(2,1)} %get-tuple-element.30), channel_id=1, source_target_pairs={{0,4},{2,6},{4,8},{6,10},{8,12},{10,14},{12,64},{14,66},{64,68},{6... | collective-permute-start | bytes 417800 | tf_op jit(solution)/shard_map/ppermute | solution.py:140
  11.7 3.2 %collective-permute-start.7 = (bf16[2,272,128]{2,1,0:T(8,128)(2,1)}, bf16[2,272,128]{2,1,0:T(8,128)(2,1)}, u32[]{:S(2)}, u32[]{:S(2)}) collective-permute-start(bf16[2,272,128]{2,1,0:T(8,128)(2,1)} %get-tuple-element.29), channel_id=1, source_target_pairs={{0,6},{2,8},{4,10},{6,12},{8,14},{10,64},{12,66},{14,68},{64,70},{... | collective-permute-start | bytes 417800 | tf_op jit(solution)/shard_map/ppermute | solution.py:140
  15.2 2.3 %collective-permute-start.9 = (bf16[2,272,128]{2,1,0:T(8,128)(2,1)}, bf16[2,272,128]{2,1,0:T(8,128)(2,1)S(1)}, u32[]{:S(2)}, u32[]{:S(2)}) collective-permute-start(bf16[2,272,128]{2,1,0:T(8,128)(2,1)} %get-tuple-element.27), channel_id=1, source_target_pairs={{0,10},{2,12},{4,14},{6,64},{8,66},{10,68},{12,70},{14,72},{64,74}... | collective-permute-start | bytes 417800 | tf_op jit(solution)/shard_map/ppermute | solution.py:140
  17.5 1.7 broadcast_in_dim.44
  19.1 5.2 %all-to-all-start = ((bf16[1,16,2,272,128]{4,3,2,0,1:T(8,128)(2,1)}), bf16[1,16,2,272,128]{4,3,2,0,1:T(8,128)(2,1)S(1)}, u32[]{:S(2)}, u32[]{:S(2)}) async-start(bf16[1,16,2,272,128]{4,3,2,0,1:T(8,128)(2,1)} %bitcast.110), calls=%async_computation | async-start | bytes 4456448 | tf_op jit(solution)/shard_map/all_to_all | solution.py:168
  24.4 0.7 bitcast_dynamic-update-slice_fusion.15
  25.0 3.8 %collective-permute-start.10 = (bf16[2,272,128]{2,1,0:T(8,128)(2,1)}, bf16[2,272,128]{2,1,0:T(8,128)(2,1)S(1)}, u32[]{:S(2)}, u32[]{:S(2)}) collective-permute-start(bf16[2,272,128]{2,1,0:T(8,128)(2,1)} %get-tuple-element.26), channel_id=1, source_target_pairs={{0,12},{2,14},{4,64},{6,66},{8,68},{10,70},{12,72},{14,74},{64,76}... | collective-permute-start | bytes 417800 | tf_op jit(solution)/shard_map/ppermute | solution.py:140
  28.8 1.6 bitcast_dynamic-update-slice_fusion.14
  30.4 1.6 collective-permute-start.11
  32.0 1.6 bitcast_dynamic-update-slice_fusion.13
  33.6 1.6 bitcast_dynamic-update-slice_fusion.12
  35.2 1.5 collective-permute-start.13
  36.6 1.6 bitcast_dynamic-update-slice_fusion.11
  38.2 1.8 collective-permute-start.14
  40.0 0.7 bitcast_dynamic-update-slice_fusion.10
  40.7 13.7 %collective-permute-done.10 = bf16[2,272,128]{2,1,0:T(8,128)(2,1)S(1)} collective-permute-done((bf16[2,272,128]{2,1,0:T(8,128)(2,1)}, bf16[2,272,128]{2,1,0:T(8,128)(2,1)S(1)}, u32[]{:S(2)}, u32[]{:S(2)}) %collective-permute-start.10) | collective-permute-done | bytes 139296 | tf_op jit(solution)/shard_map/ppermute | solution.py:140
  54.3 0.8 collective-permute-start.15
  55.2 0.7 bitcast_dynamic-update-slice_fusion.9
  55.8 3.0 %collective-permute-start.16 = (bf16[2,272,128]{2,1,0:T(8,128)(2,1)}, bf16[2,272,128]{2,1,0:T(8,128)(2,1)S(1)}, u32[]{:S(2)}, u32[]{:S(2)}) collective-permute-start(bf16[2,272,128]{2,1,0:T(8,128)(2,1)} %get-tuple-element.20), channel_id=1, source_target_pairs={{0,72},{2,74},{4,76},{6,78},{8,0},{10,2},{12,4},{14,6},{64,8},{66,... | collective-permute-start | bytes 417800 | tf_op jit(solution)/shard_map/ppermute | solution.py:140
  58.9 0.7 bitcast_dynamic-update-slice_fusion.8
  59.5 2.8 %collective-permute-start.17 = (bf16[2,272,128]{2,1,0:T(8,128)(2,1)S(1)}, bf16[2,272,128]{2,1,0:T(8,128)(2,1)S(1)}, u32[]{:S(2)}, u32[]{:S(2)}) collective-permute-start(bf16[2,272,128]{2,1,0:T(8,128)(2,1)S(1)} %copy-done.3), channel_id=1, source_target_pairs={{0,74},{2,76},{4,78},{6,0},{8,2},{10,4},{12,6},{14,8},{64,10},{66,... | collective-permute-start | bytes 417800 | tf_op jit(solution)/shard_map/ppermute | solution.py:140
  62.3 0.7 bitcast_dynamic-update-slice_fusion.7
  63.0 3.8 %collective-permute-done.13 = bf16[2,272,128]{2,1,0:T(8,128)(2,1)S(1)} collective-permute-done((bf16[2,272,128]{2,1,0:T(8,128)(2,1)}, bf16[2,272,128]{2,1,0:T(8,128)(2,1)S(1)}, u32[]{:S(2)}, u32[]{:S(2)}) %collective-permute-start.13) | collective-permute-done | bytes 139296 | tf_op jit(solution)/shard_map/ppermute | solution.py:140
  66.8 0.7 bitcast_dynamic-update-slice_fusion.6
  67.4 2.1 collective-permute-done.14
  69.5 0.7 bitcast_dynamic-update-slice_fusion.5
  70.2 0.7 bitcast_dynamic-update-slice_fusion.4
  70.9 0.7 bitcast_dynamic-update-slice_fusion.3
  71.6 0.7 bitcast_dynamic-update-slice_fusion.2
  72.2 2.0 collective-permute-done.18
  74.3 0.7 bitcast_dynamic-update-slice_fusion.1
  74.9 0.7 bitcast_dynamic-update-slice_fusion
  75.6 3.8 %gather_fusion = bf16[16,2,272,128]{3,2,1,0:T(8,128)(2,1)} fusion(bf16[16,2,272,128]{3,2,1,0:T(8,128)(2,1)} %bitcast_dynamic-update-slice_fusion, s32[1024]{0:T(1024)S(1)} %pad_clamp_fusion.2), kind=kCustom, calls=%fused_computation | custom fusion | bytes 4456512 | tf_op jit(solution)/shard_map/gather | solution.py:143
  79.4 1.4 collective-permute-start.21
  80.8 3.5 %collective-permute-start.20 = (bf16[2,8,2,272,128]{4,3,2,1,0:T(8,128)(2,1)}, bf16[2,8,2,272,128]{4,3,2,1,0:T(8,128)(2,1)}, u32[]{:S(2)}, u32[]{:S(2)}) collective-permute-start(bf16[2,8,2,272,128]{4,3,2,1,0:T(8,128)(2,1)} %bitcast.108), channel_id=1, source_target_pairs={{0,48},{16,0},{32,16},{48,32},{1,49},{17,1},{33,17},{49,33},{2,50}... | collective-permute-start | bytes 6684680 | tf_op jit(solution)/shard_map/ppermute | solution.py:111
  84.3 2.2 %collective-permute-start.1 = (bf16[8,2,2,272,128]{4,3,2,1,0:T(8,128)(2,1)S(1)}, bf16[8,2,2,272,128]{4,3,2,1,0:T(8,128)(2,1)S(1)}, u32[]{:S(2)}, u32[]{:S(2)}) collective-permute-start(bf16[8,2,2,272,128]{4,3,2,1,0:T(8,128)(2,1)S(1)} %bitcast.104), channel_id=1, source_target_pairs={{0,2},{2,4},{4,6},{6,0},{1,3},{3,5},{5,7},{7,1},{8,10},{10,12},{12... | collective-permute-start | bytes 6684680 | tf_op jit(solution)/shard_map/ppermute | solution.py:111
  86.5 2.3 %collective-permute-start = (bf16[8,2,2,272,128]{4,3,2,1,0:T(8,128)(2,1)S(1)}, bf16[8,2,2,272,128]{4,3,2,1,0:T(8,128)(2,1)S(1)}, u32[]{:S(2)}, u32[]{:S(2)}) collective-permute-start(bf16[8,2,2,272,128]{4,3,2,1,0:T(8,128)(2,1)S(1)} %bitcast.105), channel_id=1, source_target_pairs={{0,6},{2,0},{4,2},{6,4},{1,7},{3,1},{5,3},{7,5},{8,14},{10,8},{12,... | collective-permute-start | bytes 6684680 | tf_op jit(solution)/shard_map/ppermute | solution.py:111
  88.8 39.2 %collective-permute-done.21 = bf16[2,8,2,272,128]{4,3,2,1,0:T(8,128)(2,1)} collective-permute-done((bf16[2,8,2,272,128]{4,3,2,1,0:T(8,128)(2,1)}, bf16[2,8,2,272,128]{4,3,2,1,0:T(8,128)(2,1)}, u32[]{:S(2)}, u32[]{:S(2)}) %collective-permute-start.21) | collective-permute-done | bytes 2228256 | tf_op jit(solution)/shard_map/ppermute | solution.py:111
  128.0 1.3 slice.74
  129.4 1.7 collective-permute-start.22
  131.0 1.3 slice.75
  132.4 1.3 collective-permute-start.23
  133.7 3.1 %collective-permute-start.2 = (bf16[4,2,2,272,128]{4,3,2,1,0:T(8,128)(2,1)S(1)}, bf16[4,2,2,272,128]{4,3,2,1,0:T(8,128)(2,1)S(1)}, u32[]{:S(2)}, u32[]{:S(2)}) collective-permute-start(bf16[4,2,2,272,128]{4,3,2,1,0:T(8,128)(2,1)S(1)} %slice.71), channel_id=1, source_target_pairs={{0,2},{2,4},{4,6},{6,0},{1,3},{3,5},{5,7},{7,1},{8,10},{10,12},{12... | collective-permute-start | bytes 3342344 | tf_op jit(solution)/shard_map/ppermute | solution.py:111
  136.9 3.1 %collective-permute-start.3 = (bf16[4,2,2,272,128]{4,3,2,1,0:T(8,128)(2,1)S(1)}, bf16[4,2,2,272,128]{4,3,2,1,0:T(8,128)(2,1)S(1)}, u32[]{:S(2)}, u32[]{:S(2)}) collective-permute-start(bf16[4,2,2,272,128]{4,3,2,1,0:T(8,128)(2,1)S(1)} %slice.72), channel_id=1, source_target_pairs={{0,6},{2,0},{4,2},{6,4},{1,7},{3,1},{5,3},{7,5},{8,14},{10,8},{12,... | collective-permute-start | bytes 3342344 | tf_op jit(solution)/shard_map/ppermute | solution.py:111
  140.0 11.0 %collective-permute-done.22 = bf16[1,8,2,272,128]{4,3,2,1,0:T(8,128)(2,1)S(1)} collective-permute-done((bf16[1,8,2,272,128]{4,3,2,1,0:T(8,128)(2,1)S(1)}, bf16[1,8,2,272,128]{4,3,2,1,0:T(8,128)(2,1)S(1)}, u32[]{:S(2)}, u32[]{:S(2)}) %collective-permute-start.22) | collective-permute-done | bytes 1114144 | tf_op jit(solution)/shard_map/ppermute | solution.py:111
  151.0 2.3 %collective-permute-done.23 = bf16[1,8,2,272,128]{4,3,2,1,0:T(8,128)(2,1)S(1)} collective-permute-done((bf16[1,8,2,272,128]{4,3,2,1,0:T(8,128)(2,1)S(1)}, bf16[1,8,2,272,128]{4,3,2,1,0:T(8,128)(2,1)S(1)}, u32[]{:S(2)}, u32[]{:S(2)}) %collective-permute-start.23) | collective-permute-done | bytes 1114144 | tf_op jit(solution)/shard_map/ppermute | solution.py:111
  153.6 6.4 %pad_maximum_fusion.1.refs_1_ = bf16[4,2,8,2,272,128]{5,4,3,2,1,0:T(8,128)(2,1)} fusion(bf16[1,2,8,2,272,128]{5,4,3,2,1,0:T(8,128)(2,1)} %bitcast.48, bf16[1,2,8,2,272,128]{5,4,3,2,1,0:T(8,128)(2,1)S(1)} %maximum_bitcast_fusion.1, bf16[1,2,8,2,272,128]{5,4,3,2,1,0:T(8,128)(2,1)} %bitcast.46, bf16[1,2,8,2,272,128]{5,4,3,2,1,0:T(8,128)(2,1)S(1)} %bitcast.109), kind=kLoop, calls=%fused_computation.6 | loop fusion | flops 13369344 | bytes 17825792 | tf_op jit(solution)/shard_map/stack | solution.py:130
  159.9 6.8 %collective-permute-start.24 = (bf16[4,2,8,2,272,128]{5,4,3,2,1,0:T(8,128)(2,1)}, bf16[4,2,8,2,272,128]{5,4,3,2,1,0:T(8,128)(2,1)}, u32[]{:S(2)}, u32[]{:S(2)}) collective-permute-start(bf16[4,2,8,2,272,128]{5,4,3,2,1,0:T(8,128)(2,1)} %pad_maximum_fusion.1.refs_1_), channel_id=1, source_target_pairs={{0,1},{1,0},{2,3},{3,2},{4,5},{5,4},{6,7},{7,6},{8,9},{9,8},{10,11... | collective-permute-start | bytes 26738696 | tf_op jit(solution)/shard_map/ppermute | solution.py:111
  166.9 4.2 %pad_maximum_fusion.refs_0_ = bf16[4,8,2,2,272,128]{5,4,3,2,1,0:T(8,128)(2,1)} fusion(bf16[1,8,2,2,272,128]{5,4,3,2,1,0:T(8,128)(2,1)S(1)} %bitcast.111, bf16[1,8,2,2,272,128]{5,4,3,2,1,0:T(8,128)(2,1)S(1)} %maximum_bitcast_fusion, bf16[1,8,2,2,272,128]{5,4,3,2,1,0:T(8,128)(2,1)S(1)} %bitcast.112, bf16[1,8,2,2,272,128]{5,4,3,2,1,0:T(8,128)(2,1)S(1)} %bitcast.106), kind=kLoop, calls=%fused_computation.5 | loop fusion | flops 13369344 | bytes 17825792 | tf_op jit(solution)/shard_map/stack | solution.py:121
  171.1 0.8 collective-permute-start.4
  172.5 1.0 fusion.2
  175.8 1.0 slice_convert_fusion.1
  177.1 0.7 reshape.454.lids_ref
  177.8 17.1 %shard_map.58.refs_0_ = f32[2048,1024]{1,0:T(8,128)} custom-call(s32[128]{0:T(128)} %reshape.454.lids_ref, s32[128]{0:T(128)} %and_select_fusion.rids_ref, s32[3]{0:T(128)} %pad_add_fusion.rot_ref, bf16[4,8,2,2,272,128]{5,4,3,2,1,0:T(8,128)(2,1)} %pad_maximum_fusion.refs_0_, bf16[4,2,8,2,272,128]{5,4,3,2,1,0:T(8,128)(2,1)} %pad_maximum_fusion.1.refs_1_), custom_call_target="tpu_custom_call" | custom-call | flops 2147483648 | bytes 26214400 | tf_op jit(solution)/shard_map/pallas_call | solution.py:94
  194.9 1.0 fusion.3
  198.2 1.0 slice_convert_fusion.3
  199.5 0.7 reshape.452.lids_ref
  200.3 18.6 %shard_map.59 = f32[2048,1024]{1,0:T(8,128)} custom-call(s32[128]{0:T(128)} %reshape.452.lids_ref, s32[128]{0:T(128)} %and_select_fusion.1.rids_ref, s32[3]{0:T(128)} %pad_add_fusion.rot_ref, f32[2048,1024]{1,0:T(8,128)} %shard_map.58.refs_0_, bf16[4,8,2,2,272,128]{5,4,3,2,1,0:T(8,128)(2,1)} %collective-permute-done.4.refs_1_, ...), custom_call_target="tpu_custom_call", output_to_operand_aliasing={{}: (3, {})} | custom-call | flops 2147483648 | bytes 26214400 | tf_op jit(solution)/shard_map/pallas_call | solution.py:94
  (67 shorter events, 7.2 us)
Async XLA Ops:
  5.9 19.1 %collective-permute-start.5 = (bf16[2,272,128]{2,1,0:T(8,128)(2,1)}, bf16[2,272,128]{2,1,0:T(8,128)(2,1)}, u32[]{:S(2)}, u32[]{:S(2)}) collective-permute-start(bf16[2,272,128]{2,1,0:T(8,128)(2,1)} %get-tuple-element.31), channel_id=1, source_target_pairs={{0,2},{2,4},{4,6},{6,8},{8,10},{10,12},{12,14},{14,64},{64,66},{66... | collective-permute-start | bytes 417800 | tf_op jit(solution)/shard_map/ppermute | solution.py:140
  8.4 21.9 %collective-permute-start.6 = (bf16[2,272,128]{2,1,0:T(8,128)(2,1)}, bf16[2,272,128]{2,1,0:T(8,128)(2,1)}, u32[]{:S(2)}, u32[]{:S(2)}) collective-permute-start(bf16[2,272,128]{2,1,0:T(8,128)(2,1)} %get-tuple-element.30), channel_id=1, source_target_pairs={{0,4},{2,6},{4,8},{6,10},{8,12},{10,14},{12,64},{14,66},{64,68},{6... | collective-permute-start | bytes 417800 | tf_op jit(solution)/shard_map/ppermute | solution.py:140
  11.7 21.9 %collective-permute-start.7 = (bf16[2,272,128]{2,1,0:T(8,128)(2,1)}, bf16[2,272,128]{2,1,0:T(8,128)(2,1)}, u32[]{:S(2)}, u32[]{:S(2)}) collective-permute-start(bf16[2,272,128]{2,1,0:T(8,128)(2,1)} %get-tuple-element.29), channel_id=1, source_target_pairs={{0,6},{2,8},{4,10},{6,12},{8,14},{10,64},{12,66},{14,68},{64,70},{... | collective-permute-start | bytes 417800 | tf_op jit(solution)/shard_map/ppermute | solution.py:140
  14.9 20.3 %collective-permute-start.8 = (bf16[2,272,128]{2,1,0:T(8,128)(2,1)}, bf16[2,272,128]{2,1,0:T(8,128)(2,1)}, u32[]{:S(2)}, u32[]{:S(2)}) collective-permute-start(bf16[2,272,128]{2,1,0:T(8,128)(2,1)} %get-tuple-element.28), channel_id=1, source_target_pairs={{0,8},{2,10},{4,12},{6,14},{8,64},{10,66},{12,68},{14,70},{64,72},... | collective-permute-start | bytes 417800 | tf_op jit(solution)/shard_map/ppermute | solution.py:140
  15.2 23.1 %collective-permute-start.9 = (bf16[2,272,128]{2,1,0:T(8,128)(2,1)}, bf16[2,272,128]{2,1,0:T(8,128)(2,1)S(1)}, u32[]{:S(2)}, u32[]{:S(2)}) collective-permute-start(bf16[2,272,128]{2,1,0:T(8,128)(2,1)} %get-tuple-element.27), channel_id=1, source_target_pairs={{0,10},{2,12},{4,14},{6,64},{8,66},{10,68},{12,70},{14,72},{64,74}... | collective-permute-start | bytes 417800 | tf_op jit(solution)/shard_map/ppermute | solution.py:140
  19.1 65.2 %all-to-all-start = ((bf16[1,16,2,272,128]{4,3,2,0,1:T(8,128)(2,1)}), bf16[1,16,2,272,128]{4,3,2,0,1:T(8,128)(2,1)S(1)}, u32[]{:S(2)}, u32[]{:S(2)}) async-start(bf16[1,16,2,272,128]{4,3,2,0,1:T(8,128)(2,1)} %bitcast.110), calls=%async_computation | async-start | bytes 4456448 | tf_op jit(solution)/shard_map/all_to_all | solution.py:168
  24.3 35.2 %copy-start.3 = (bf16[2,272,128]{2,1,0:T(8,128)(2,1)S(1)}, bf16[2,272,128]{2,1,0:T(8,128)(2,1)}, u32[]{:S(2)}) copy-start(bf16[2,272,128]{2,1,0:T(8,128)(2,1)} %get-tuple-element.19) | copy-start | bytes 417796
  24.3 42.4 %copy-start.2 = (bf16[2,272,128]{2,1,0:T(8,128)(2,1)S(1)}, bf16[2,272,128]{2,1,0:T(8,128)(2,1)}, u32[]{:S(2)}) copy-start(bf16[2,272,128]{2,1,0:T(8,128)(2,1)} %get-tuple-element.18) | copy-start | bytes 417796
  24.3 45.2 %copy-start.1 = (bf16[2,272,128]{2,1,0:T(8,128)(2,1)S(1)}, bf16[2,272,128]{2,1,0:T(8,128)(2,1)}, u32[]{:S(2)}) copy-start(bf16[2,272,128]{2,1,0:T(8,128)(2,1)} %get-tuple-element.17) | copy-start | bytes 417796
  25.0 29.3 %collective-permute-start.10 = (bf16[2,272,128]{2,1,0:T(8,128)(2,1)}, bf16[2,272,128]{2,1,0:T(8,128)(2,1)S(1)}, u32[]{:S(2)}, u32[]{:S(2)}) collective-permute-start(bf16[2,272,128]{2,1,0:T(8,128)(2,1)} %get-tuple-element.26), channel_id=1, source_target_pairs={{0,12},{2,14},{4,64},{6,66},{8,68},{10,70},{12,72},{14,74},{64,76}... | collective-permute-start | bytes 417800 | tf_op jit(solution)/shard_map/ppermute | solution.py:140
  30.4 25.5 %collective-permute-start.11 = (bf16[2,272,128]{2,1,0:T(8,128)(2,1)}, bf16[2,272,128]{2,1,0:T(8,128)(2,1)S(1)}, u32[]{:S(2)}, u32[]{:S(2)}) collective-permute-start(bf16[2,272,128]{2,1,0:T(8,128)(2,1)} %get-tuple-element.25), channel_id=1, source_target_pairs={{0,14},{2,64},{4,66},{6,68},{8,70},{10,72},{12,74},{14,76},{64,78}... | collective-permute-start | bytes 417800 | tf_op jit(solution)/shard_map/ppermute | solution.py:140
  33.6 25.9 %collective-permute-start.12 = (bf16[2,272,128]{2,1,0:T(8,128)(2,1)}, bf16[2,272,128]{2,1,0:T(8,128)(2,1)S(1)}, u32[]{:S(2)}, u32[]{:S(2)}) collective-permute-start(bf16[2,272,128]{2,1,0:T(8,128)(2,1)} %get-tuple-element.24), channel_id=1, source_target_pairs={{0,64},{2,66},{4,68},{6,70},{8,72},{10,74},{12,76},{14,78},{64,0},... | collective-permute-start | bytes 417800 | tf_op jit(solution)/shard_map/ppermute | solution.py:140
  35.2 31.6 %collective-permute-start.13 = (bf16[2,272,128]{2,1,0:T(8,128)(2,1)}, bf16[2,272,128]{2,1,0:T(8,128)(2,1)S(1)}, u32[]{:S(2)}, u32[]{:S(2)}) collective-permute-start(bf16[2,272,128]{2,1,0:T(8,128)(2,1)} %get-tuple-element.23), channel_id=1, source_target_pairs={{0,66},{2,68},{4,70},{6,72},{8,74},{10,76},{12,78},{14,0},{64,2},{... | collective-permute-start | bytes 417800 | tf_op jit(solution)/shard_map/ppermute | solution.py:140
  38.2 31.3 %collective-permute-start.14 = (bf16[2,272,128]{2,1,0:T(8,128)(2,1)}, bf16[2,272,128]{2,1,0:T(8,128)(2,1)S(1)}, u32[]{:S(2)}, u32[]{:S(2)}) collective-permute-start(bf16[2,272,128]{2,1,0:T(8,128)(2,1)} %get-tuple-element.22), channel_id=1, source_target_pairs={{0,68},{2,70},{4,72},{6,74},{8,76},{10,78},{12,0},{14,2},{64,4},{6... | collective-permute-start | bytes 417800 | tf_op jit(solution)/shard_map/ppermute | solution.py:140
  54.3 15.9 %collective-permute-start.15 = (bf16[2,272,128]{2,1,0:T(8,128)(2,1)}, bf16[2,272,128]{2,1,0:T(8,128)(2,1)S(1)}, u32[]{:S(2)}, u32[]{:S(2)}) collective-permute-start(bf16[2,272,128]{2,1,0:T(8,128)(2,1)} %get-tuple-element.21), channel_id=1, source_target_pairs={{0,70},{2,72},{4,74},{6,76},{8,78},{10,0},{12,2},{14,4},{64,6},{66... | collective-permute-start | bytes 417800 | tf_op jit(solution)/shard_map/ppermute | solution.py:140
  55.8 15.1 %collective-permute-start.16 = (bf16[2,272,128]{2,1,0:T(8,128)(2,1)}, bf16[2,272,128]{2,1,0:T(8,128)(2,1)S(1)}, u32[]{:S(2)}, u32[]{:S(2)}) collective-permute-start(bf16[2,272,128]{2,1,0:T(8,128)(2,1)} %get-tuple-element.20), channel_id=1, source_target_pairs={{0,72},{2,74},{4,76},{6,78},{8,0},{10,2},{12,4},{14,6},{64,8},{66,... | collective-permute-start | bytes 417800 | tf_op jit(solution)/shard_map/ppermute | solution.py:140
  59.5 12.0 %collective-permute-start.17 = (bf16[2,272,128]{2,1,0:T(8,128)(2,1)S(1)}, bf16[2,272,128]{2,1,0:T(8,128)(2,1)S(1)}, u32[]{:S(2)}, u32[]{:S(2)}) collective-permute-start(bf16[2,272,128]{2,1,0:T(8,128)(2,1)S(1)} %copy-done.3), channel_id=1, source_target_pairs={{0,74},{2,76},{4,78},{6,0},{8,2},{10,4},{12,6},{14,8},{64,10},{66,... | collective-permute-start | bytes 417800 | tf_op jit(solution)/shard_map/ppermute | solution.py:140
  66.8 7.5 %collective-permute-start.18 = (bf16[2,272,128]{2,1,0:T(8,128)(2,1)S(1)}, bf16[2,272,128]{2,1,0:T(8,128)(2,1)S(1)}, u32[]{:S(2)}, u32[]{:S(2)}) collective-permute-start(bf16[2,272,128]{2,1,0:T(8,128)(2,1)S(1)} %copy-done.2), channel_id=1, source_target_pairs={{0,76},{2,78},{4,0},{6,2},{8,4},{10,6},{12,8},{14,10},{64,12},{66,... | collective-permute-start | bytes 417800 | tf_op jit(solution)/shard_map/ppermute | solution.py:140
  69.5 5.4 %collective-permute-start.19 = (bf16[2,272,128]{2,1,0:T(8,128)(2,1)S(1)}, bf16[2,272,128]{2,1,0:T(8,128)(2,1)S(1)}, u32[]{:S(2)}, u32[]{:S(2)}) collective-permute-start(bf16[2,272,128]{2,1,0:T(8,128)(2,1)S(1)} %copy-done.1), channel_id=1, source_target_pairs={{0,78},{2,0},{4,2},{6,4},{8,6},{10,8},{12,10},{14,12},{64,14},{66,... | collective-permute-start | bytes 417800 | tf_op jit(solution)/shard_map/ppermute | solution.py:140
  79.4 48.6 %collective-permute-start.21 = (bf16[2,8,2,272,128]{4,3,2,1,0:T(8,128)(2,1)}, bf16[2,8,2,272,128]{4,3,2,1,0:T(8,128)(2,1)}, u32[]{:S(2)}, u32[]{:S(2)}) collective-permute-start(bf16[2,8,2,272,128]{4,3,2,1,0:T(8,128)(2,1)} %bitcast.107), channel_id=1, source_target_pairs={{0,16},{16,32},{32,48},{48,0},{1,17},{17,33},{33,49},{49,1},{2,18}... | collective-permute-start | bytes 6684680 | tf_op jit(solution)/shard_map/ppermute | solution.py:111
  80.8 50.2 %collective-permute-start.20 = (bf16[2,8,2,272,128]{4,3,2,1,0:T(8,128)(2,1)}, bf16[2,8,2,272,128]{4,3,2,1,0:T(8,128)(2,1)}, u32[]{:S(2)}, u32[]{:S(2)}) collective-permute-start(bf16[2,8,2,272,128]{4,3,2,1,0:T(8,128)(2,1)} %bitcast.108), channel_id=1, source_target_pairs={{0,48},{16,0},{32,16},{48,32},{1,49},{17,1},{33,17},{49,33},{2,50}... | collective-permute-start | bytes 6684680 | tf_op jit(solution)/shard_map/ppermute | solution.py:111
  84.3 49.4 %collective-permute-start.1 = (bf16[8,2,2,272,128]{4,3,2,1,0:T(8,128)(2,1)S(1)}, bf16[8,2,2,272,128]{4,3,2,1,0:T(8,128)(2,1)S(1)}, u32[]{:S(2)}, u32[]{:S(2)}) collective-permute-start(bf16[8,2,2,272,128]{4,3,2,1,0:T(8,128)(2,1)S(1)} %bitcast.104), channel_id=1, source_target_pairs={{0,2},{2,4},{4,6},{6,0},{1,3},{3,5},{5,7},{7,1},{8,10},{10,12},{12... | collective-permute-start | bytes 6684680 | tf_op jit(solution)/shard_map/ppermute | solution.py:111
  86.5 50.3 %collective-permute-start = (bf16[8,2,2,272,128]{4,3,2,1,0:T(8,128)(2,1)S(1)}, bf16[8,2,2,272,128]{4,3,2,1,0:T(8,128)(2,1)S(1)}, u32[]{:S(2)}, u32[]{:S(2)}) collective-permute-start(bf16[8,2,2,272,128]{4,3,2,1,0:T(8,128)(2,1)S(1)} %bitcast.105), channel_id=1, source_target_pairs={{0,6},{2,0},{4,2},{6,4},{1,7},{3,1},{5,3},{7,5},{8,14},{10,8},{12,... | collective-permute-start | bytes 6684680 | tf_op jit(solution)/shard_map/ppermute | solution.py:111
  129.4 21.7 %collective-permute-start.22 = (bf16[1,8,2,272,128]{4,3,2,1,0:T(8,128)(2,1)S(1)}, bf16[1,8,2,272,128]{4,3,2,1,0:T(8,128)(2,1)S(1)}, u32[]{:S(2)}, u32[]{:S(2)}) collective-permute-start(bf16[1,8,2,272,128]{4,3,2,1,0:T(8,128)(2,1)S(1)} %slice.74), channel_id=1, source_target_pairs={{0,16},{16,32},{32,48},{48,0},{1,17},{17,33},{33,49},{49,1},{2,18}... | collective-permute-start | bytes 3342344 | tf_op jit(solution)/shard_map/ppermute | solution.py:111
  132.4 21.0 %collective-permute-start.23 = (bf16[1,8,2,272,128]{4,3,2,1,0:T(8,128)(2,1)S(1)}, bf16[1,8,2,272,128]{4,3,2,1,0:T(8,128)(2,1)S(1)}, u32[]{:S(2)}, u32[]{:S(2)}) collective-permute-start(bf16[1,8,2,272,128]{4,3,2,1,0:T(8,128)(2,1)S(1)} %slice.75), channel_id=1, source_target_pairs={{0,48},{16,0},{32,16},{48,32},{1,49},{17,1},{33,17},{49,33},{2,50}... | collective-permute-start | bytes 3342344 | tf_op jit(solution)/shard_map/ppermute | solution.py:111
  133.7 33.0 %collective-permute-start.2 = (bf16[4,2,2,272,128]{4,3,2,1,0:T(8,128)(2,1)S(1)}, bf16[4,2,2,272,128]{4,3,2,1,0:T(8,128)(2,1)S(1)}, u32[]{:S(2)}, u32[]{:S(2)}) collective-permute-start(bf16[4,2,2,272,128]{4,3,2,1,0:T(8,128)(2,1)S(1)} %slice.71), channel_id=1, source_target_pairs={{0,2},{2,4},{4,6},{6,0},{1,3},{3,5},{5,7},{7,1},{8,10},{10,12},{12... | collective-permute-start | bytes 3342344 | tf_op jit(solution)/shard_map/ppermute | solution.py:111
  136.9 16.7 %copy-start = (bf16[16,2,272,128]{3,2,1,0:T(8,128)(2,1)S(1)}, bf16[16,2,272,128]{3,2,1,0:T(8,128)(2,1)}, u32[]{:S(2)}) copy-start(bf16[16,2,272,128]{3,2,1,0:T(8,128)(2,1)} %gather_fusion) | copy-start | bytes 6684676
  136.9 29.9 %collective-permute-start.3 = (bf16[4,2,2,272,128]{4,3,2,1,0:T(8,128)(2,1)S(1)}, bf16[4,2,2,272,128]{4,3,2,1,0:T(8,128)(2,1)S(1)}, u32[]{:S(2)}, u32[]{:S(2)}) collective-permute-start(bf16[4,2,2,272,128]{4,3,2,1,0:T(8,128)(2,1)S(1)} %slice.72), channel_id=1, source_target_pairs={{0,6},{2,0},{4,2},{6,4},{1,7},{3,1},{5,3},{7,5},{8,14},{10,8},{12,... | collective-permute-start | bytes 3342344 | tf_op jit(solution)/shard_map/ppermute | solution.py:111
  159.9 35.0 %collective-permute-start.24 = (bf16[4,2,8,2,272,128]{5,4,3,2,1,0:T(8,128)(2,1)}, bf16[4,2,8,2,272,128]{5,4,3,2,1,0:T(8,128)(2,1)}, u32[]{:S(2)}, u32[]{:S(2)}) collective-permute-start(bf16[4,2,8,2,272,128]{5,4,3,2,1,0:T(8,128)(2,1)} %pad_maximum_fusion.1.refs_1_), channel_id=1, source_target_pairs={{0,1},{1,0},{2,3},{3,2},{4,5},{5,4},{6,7},{7,6},{8,9},{9,8},{10,11... | collective-permute-start | bytes 26738696 | tf_op jit(solution)/shard_map/ppermute | solution.py:111
  171.1 27.2 %collective-permute-start.4 = (bf16[4,8,2,2,272,128]{5,4,3,2,1,0:T(8,128)(2,1)}, bf16[4,8,2,2,272,128]{5,4,3,2,1,0:T(8,128)(2,1)}, u32[]{:S(2)}, u32[]{:S(2)}) collective-permute-start(bf16[4,8,2,2,272,128]{5,4,3,2,1,0:T(8,128)(2,1)} %pad_maximum_fusion.refs_0_), channel_id=1, source_target_pairs={{0,1},{1,0},{2,3},{3,2},{4,5},{5,4},{6,7},{7,6},{8,9},{9,8},{10,11... | collective-permute-start | bytes 26738696 | tf_op jit(solution)/shard_map/ppermute | solution.py:111
